TPU v7x, 32 devices: a whole 2x2x4 slice. The times are simulated.
32 devices in a mesh: shard: 16 (over z, x, core), replica: 2 (over y).
Axes of the slice: x: 2, y: 2, z: 4, core: 2. Of those that a mesh axis runs over, the one named last changes fastest.
Arguments:
- x_in: bfloat16 [2, 8192, 768], P('replica', 'shard'), may hold values from -6 to 6
- seq_units: int32 [2, 16], P('replica'), may hold values from 1 to 64, 512 in all within a row
- deal: int32 [2, 16], P('replica'), may hold values from 0 to 15, each once within a row
- gain_attn: float32 [768], replicated, may hold values from 0.1 to 1.9
- w_query: bfloat16 [768, 768], P('shard'), may hold values from -0.4375 to 0.4375
- w_key: bfloat16 [768, 768], P('shard'), may hold values from -0.21875 to 0.21875
- w_value: bfloat16 [768, 768], P('shard'), may hold values from -0.21875 to 0.21875
- w_out: bfloat16 [768, 768], P('shard'), may hold values from -0.875 to 0.875
- gain_ffn: float32 [768], replicated, may hold values from 0.1 to 1.9
- w_gate: bfloat16 [768, 2048], P('shard'), may hold values from -0.21875 to 0.21875
- w_up: bfloat16 [768, 2048], P('shard'), may hold values from -0.21875 to 0.21875
- w_down: bfloat16 [2048, 768], P('shard'), may hold values from -0.125 to 0.125
- d_out: bfloat16 [2, 16, 1024, 768], P('replica', 'shard'), may hold values from -6 to 6
Outputs:
- layer_out: bfloat16 [2, 16, 1024, 768], P('replica', 'shard')
- grad_x: bfloat16 [2, 8192, 768], P('replica', 'shard')
- grad_gain_attn: float32 [768], P('shard')
- grad_gain_ffn: float32 [768], P('shard')
- grad_w_query: float32 [768, 768], P('shard')
- grad_w_key: float32 [768, 768], P('shard')
- grad_w_value: float32 [768, 768], P('shard')
- grad_w_out: float32 [768, 768], P('shard')
- grad_w_gate: float32 [768, 2048], P('shard')
- grad_w_up: float32 [768, 2048], P('shard')
- grad_w_down: float32 [2048, 768], P('shard')
Inputs may be any that keep to these rules, and one draw needn't show every extreme that they name: `seq_units`: each group's 16 entries sum to 512. `deal`: each group's row names every sequence 0 to 15 once.
All inputs are finite; a program needn't handle non-finite values.
Results may differ from a plain program's by a relative error of at most 0.023.
Values may be sent and summed in bfloat16 or wider, within the bound.
No kernel may reach another device: no remote copies, remote signals or barrier semaphores. Data moves between devices by JAX's collectives and lax.ppermute only.
A program may use at most 320 MiB of HBM per device.

v0:
```python
import jax
import jax.numpy as jnp
from jax import lax
from jax.sharding import PartitionSpec as P

H = 12
HD = 64


norm_eps = 1e-06
neg_big = -1e30


def rms_scale(tok_rows, gain_vec):
    inverse = lax.rsqrt(jnp.mean(tok_rows * tok_rows, axis=-1, keepdims=True) + norm_eps)
    return tok_rows * inverse * gain_vec


def gelu_mix(gate_vals, up_vals):
    return jax.nn.gelu(gate_vals, approximate=True) * up_vals


def lookup(table, wanted):
    table_slots = jnp.arange(table.shape[0], dtype=jnp.int32)
    return jnp.sum(jnp.where(wanted[:, None] == table_slots[None, :], table[None, :], 0), axis=1)


def left_dot(lhs_mat, rhs_mat):
    return lax.dot_general(
        lhs_mat, rhs_mat, (((0,), (0,)), ((), ())), preferred_element_type=jnp.float32
    )


def right_dot(lhs_mat, rhs_mat):
    return lax.dot_general(
        lhs_mat, rhs_mat, (((1,), (1,)), ((), ())), preferred_element_type=jnp.float32
    )


def plain_dot(lhs_mat, rhs_mat):
    return jnp.dot(lhs_mat, rhs_mat, preferred_element_type=jnp.float32)


def attend_forward(queries, keys_all, values_all, live_keys):
    total_rows = queries.shape[0]
    row_block = min(512, total_rows)
    factor = HD ** (-0.5)
    key_heads = keys_all.reshape(total_rows, H, HD)
    value_heads = values_all.reshape(total_rows, H, HD)
    mixed_list = []
    stat_list = []
    for row_begin in range(0, total_rows, row_block):
        query_heads = queries[row_begin : row_begin + row_block].reshape(row_block, H, HD)
        scores = (
            jnp.einsum("qhd,khd->hqk", query_heads, key_heads, preferred_element_type=jnp.float32)
            * factor
        )
        scores = jnp.where(live_keys[None, None, :], scores, neg_big)
        row_max = jnp.max(scores, axis=-1, keepdims=True)
        exp_vals = jnp.exp(scores - row_max)
        row_total = jnp.sum(exp_vals, axis=-1, keepdims=True)
        prob_vals = (exp_vals / row_total).astype(jnp.bfloat16)
        mixed_rows = jnp.einsum(
            "hqk,khd->qhd", prob_vals, value_heads, preferred_element_type=jnp.float32
        )
        mixed_list.append(mixed_rows.reshape(row_block, H * HD))
        stat_list.append(row_max + jnp.log(row_total))
    return (jnp.concatenate(mixed_list, axis=0), jnp.concatenate(stat_list, axis=1))


def attend_backward(queries, keys_all, values_all, live_keys, log_totals, grad_mixed):
    total_rows = queries.shape[0]
    row_block = min(512, total_rows)
    factor = HD ** (-0.5)
    key_heads = keys_all.reshape(total_rows, H, HD)
    value_heads = values_all.reshape(total_rows, H, HD)
    grad_keys = jnp.zeros((total_rows, H, HD), jnp.float32)
    grad_values = jnp.zeros((total_rows, H, HD), jnp.float32)
    query_list = []
    for row_begin in range(0, total_rows, row_block):
        query_heads = queries[row_begin : row_begin + row_block].reshape(row_block, H, HD)
        grad_heads = grad_mixed[row_begin : row_begin + row_block].reshape(row_block, H, HD)
        scores = (
            jnp.einsum("qhd,khd->hqk", query_heads, key_heads, preferred_element_type=jnp.float32)
            * factor
        )
        scores = jnp.where(live_keys[None, None, :], scores, neg_big)
        prob_vals = jnp.exp(scores - log_totals[:, row_begin : row_begin + row_block])
        grad_probs = jnp.einsum(
            "qhd,khd->hqk", grad_heads, value_heads, preferred_element_type=jnp.float32
        )
        row_dot = jnp.sum(prob_vals * grad_probs, axis=-1, keepdims=True)
        grad_scores = (prob_vals * (grad_probs - row_dot)).astype(jnp.bfloat16)
        grad_query = (
            jnp.einsum("hqk,khd->qhd", grad_scores, key_heads, preferred_element_type=jnp.float32)
            * factor
        )
        query_list.append(grad_query.reshape(row_block, H * HD))
        grad_keys = (
            grad_keys
            + jnp.einsum(
                "hqk,qhd->khd", grad_scores, query_heads, preferred_element_type=jnp.float32
            )
            * factor
        )
        grad_values = grad_values + jnp.einsum(
            "hqk,qhd->khd",
            prob_vals.astype(jnp.bfloat16),
            grad_heads,
            preferred_element_type=jnp.float32,
        )
    return (
        jnp.concatenate(query_list, axis=0),
        grad_keys.reshape(total_rows, H * HD),
        grad_values.reshape(total_rows, H * HD),
    )


def shards(
    x_in,
    seq_units,
    deal,
    gain_attn,
    w_query,
    w_key,
    w_value,
    w_out,
    gain_ffn,
    w_gate,
    w_up,
    w_down,
    d_out,
):
    shard_count = lax.axis_size("shard")
    my_index = lax.axis_index("shard")
    width = x_in.shape[2]
    span = d_out.shape[2]
    unit_max = span // shard_count
    units_row = seq_units[0]
    order_row = deal[0]
    offsets = jnp.cumsum(units_row) - units_row
    inner_idx = jnp.arange(unit_max, dtype=jnp.int32)
    dest_idx = jnp.arange(shard_count, dtype=jnp.int32)
    counts = lookup(units_row, order_row)
    starts = lookup(offsets, order_row)
    row_index = starts[:, None] + jnp.minimum(inner_idx[None, :], counts[:, None] - 1)
    sent_live = inner_idx[None, :] < counts[:, None]
    local_rows = x_in[0]
    outgoing = jnp.where(
        sent_live[:, :, None], local_rows[row_index], jnp.zeros((), local_rows.dtype)
    )
    arrived = lax.all_to_all(outgoing, "shard", split_axis=0, concat_axis=0, tiled=True)
    own_count = jnp.sum(jnp.where(dest_idx == my_index, counts, 0))
    live_rows = jnp.broadcast_to(inner_idx[None, :] < own_count, (shard_count, unit_max)).reshape(
        span
    )
    wq_full, wk_full, wv_full, wo_full = (
        lax.all_gather(w_query, "shard", axis=0, tiled=True),
        lax.all_gather(w_key, "shard", axis=0, tiled=True),
        lax.all_gather(w_value, "shard", axis=0, tiled=True),
        lax.all_gather(w_out, "shard", axis=0, tiled=True),
    )
    tok_float = arrived.reshape(span, width).astype(jnp.float32)
    normed_one_f, norm_one_back = jax.vjp(rms_scale, tok_float, gain_attn)
    normed_one = normed_one_f.astype(jnp.bfloat16)
    queries = plain_dot(normed_one, wq_full).astype(jnp.bfloat16)
    keys_all = plain_dot(normed_one, wk_full).astype(jnp.bfloat16)
    values_all = plain_dot(normed_one, wv_full).astype(jnp.bfloat16)
    mixed_f, log_totals = attend_forward(queries, keys_all, values_all, live_rows)
    mixed_rows = mixed_f.astype(jnp.bfloat16)
    hidden_res = tok_float + plain_dot(mixed_rows, wo_full)
    wg_full, wu_full, wd_full = (
        lax.all_gather(w_gate, "shard", axis=0, tiled=True),
        lax.all_gather(w_up, "shard", axis=0, tiled=True),
        lax.all_gather(w_down, "shard", axis=0, tiled=True),
    )
    normed_two_f, norm_two_back = jax.vjp(rms_scale, hidden_res, gain_ffn)
    normed_two = normed_two_f.astype(jnp.bfloat16)
    gate_vals = plain_dot(normed_two, wg_full)
    up_vals = plain_dot(normed_two, wu_full)
    act_f, mix_back = jax.vjp(gelu_mix, gate_vals, up_vals)
    act_vals = act_f.astype(jnp.bfloat16)
    result = jnp.where(live_rows[:, None], hidden_res + plain_dot(act_vals, wd_full), 0.0)
    layer_out = result.astype(jnp.bfloat16).reshape(1, 1, span, width)
    wg_back, wu_back, wd_back = (
        lax.all_gather(w_gate, "shard", axis=0, tiled=True),
        lax.all_gather(w_up, "shard", axis=0, tiled=True),
        lax.all_gather(w_down, "shard", axis=0, tiled=True),
    )
    grad_y = jnp.where(live_rows[:, None], d_out[0, 0].astype(jnp.float32), 0.0)
    grad_ffn_b = grad_y.astype(jnp.bfloat16)
    grad_down = left_dot(act_vals, grad_ffn_b)
    grad_act = right_dot(grad_ffn_b, wd_back)
    grad_gate_f, grad_up_f = mix_back(grad_act)
    grad_gate_b = grad_gate_f.astype(jnp.bfloat16)
    grad_up_b = grad_up_f.astype(jnp.bfloat16)
    grad_wg = left_dot(normed_two, grad_gate_b)
    grad_wu = left_dot(normed_two, grad_up_b)
    grad_n2 = right_dot(grad_gate_b, wg_back) + right_dot(grad_up_b, wu_back)
    grad_h_norm, grad_gain_two = norm_two_back(grad_n2)
    ffn_share = (
        lax.psum_scatter(
            grad_wg.astype(jnp.bfloat16), "shard", scatter_dimension=0, tiled=True
        ).astype(jnp.float32),
        lax.psum_scatter(
            grad_wu.astype(jnp.bfloat16), "shard", scatter_dimension=0, tiled=True
        ).astype(jnp.float32),
        lax.psum_scatter(
            grad_down.astype(jnp.bfloat16), "shard", scatter_dimension=0, tiled=True
        ).astype(jnp.float32),
        lax.psum_scatter(
            grad_gain_two.astype(jnp.bfloat16), "shard", scatter_dimension=0, tiled=True
        ).astype(jnp.float32),
    )
    grad_hidden = grad_y + grad_h_norm
    wq_back, wk_back, wv_back, wo_back = (
        lax.all_gather(w_query, "shard", axis=0, tiled=True),
        lax.all_gather(w_key, "shard", axis=0, tiled=True),
        lax.all_gather(w_value, "shard", axis=0, tiled=True),
        lax.all_gather(w_out, "shard", axis=0, tiled=True),
    )
    grad_attn_b = grad_hidden.astype(jnp.bfloat16)
    grad_wo = left_dot(mixed_rows, grad_attn_b)
    grad_mixed = right_dot(grad_attn_b, wo_back).astype(jnp.bfloat16)
    grad_q_f, grad_k_f, grad_v_f = attend_backward(
        queries, keys_all, values_all, live_rows, log_totals, grad_mixed
    )
    grad_q_b = grad_q_f.astype(jnp.bfloat16)
    grad_k_b = grad_k_f.astype(jnp.bfloat16)
    grad_v_b = grad_v_f.astype(jnp.bfloat16)
    grad_wq = left_dot(normed_one, grad_q_b)
    grad_wk = left_dot(normed_one, grad_k_b)
    grad_wv = left_dot(normed_one, grad_v_b)
    grad_n1 = (
        right_dot(grad_q_b, wq_back) + right_dot(grad_k_b, wk_back) + right_dot(grad_v_b, wv_back)
    )
    grad_x_norm, grad_gain_one = norm_one_back(grad_n1)
    grad_tokens = (
        (grad_hidden + grad_x_norm).astype(jnp.bfloat16).reshape(shard_count, unit_max, width)
    )
    returned = lax.all_to_all(grad_tokens, "shard", split_axis=0, concat_axis=0, tiled=True)
    home_rows = (
        jnp.zeros(local_rows.shape, jnp.float32)
        .at[row_index]
        .add(jnp.where(sent_live[:, :, None], returned.astype(jnp.float32), 0.0))
    )
    grad_x = home_rows.astype(jnp.bfloat16)[None]
    attn_share = (
        lax.psum_scatter(
            grad_wq.astype(jnp.bfloat16), "shard", scatter_dimension=0, tiled=True
        ).astype(jnp.float32),
        lax.psum_scatter(
            grad_wk.astype(jnp.bfloat16), "shard", scatter_dimension=0, tiled=True
        ).astype(jnp.float32),
        lax.psum_scatter(
            grad_wv.astype(jnp.bfloat16), "shard", scatter_dimension=0, tiled=True
        ).astype(jnp.float32),
        lax.psum_scatter(
            grad_wo.astype(jnp.bfloat16), "shard", scatter_dimension=0, tiled=True
        ).astype(jnp.float32),
        lax.psum_scatter(
            grad_gain_one.astype(jnp.bfloat16), "shard", scatter_dimension=0, tiled=True
        ).astype(jnp.float32),
    )
    totals = (
        lax.psum(ffn_share[0].astype(jnp.bfloat16), "replica").astype(jnp.float32),
        lax.psum(ffn_share[1].astype(jnp.bfloat16), "replica").astype(jnp.float32),
        lax.psum(ffn_share[2].astype(jnp.bfloat16), "replica").astype(jnp.float32),
        lax.psum(ffn_share[3].astype(jnp.bfloat16), "replica").astype(jnp.float32),
        lax.psum(attn_share[0].astype(jnp.bfloat16), "replica").astype(jnp.float32),
        lax.psum(attn_share[1].astype(jnp.bfloat16), "replica").astype(jnp.float32),
        lax.psum(attn_share[2].astype(jnp.bfloat16), "replica").astype(jnp.float32),
        lax.psum(attn_share[3].astype(jnp.bfloat16), "replica").astype(jnp.float32),
        lax.psum(attn_share[4].astype(jnp.bfloat16), "replica").astype(jnp.float32),
    )
    return (
        layer_out,
        grad_x,
        totals[8],
        totals[3],
        totals[4],
        totals[5],
        totals[6],
        totals[7],
        totals[0],
        totals[1],
        totals[2],
    )


def solution(mesh):
    return jax.shard_map(
        shards,
        mesh=mesh,
        in_specs=(
            P("replica", "shard", None),
            P("replica", None),
            P("replica", None),
            P(),
            P("shard", None),
            P("shard", None),
            P("shard", None),
            P("shard", None),
            P(),
            P("shard", None),
            P("shard", None),
            P("shard", None),
            P("replica", "shard", None, None),
        ),
        out_specs=(
            P("replica", "shard", None, None),
            P("replica", "shard", None),
            P("shard"),
            P("shard"),
            P("shard", None),
            P("shard", None),
            P("shard", None),
            P("shard", None),
            P("shard", None),
            P("shard", None),
            P("shard", None),
        ),
        check_vma=False,
    )
```

profile of v0, /device:TPU:0, one launch (start us, length us, event | category | flops | bytes accessed | tf_op | source)
XLA Modules:
  0.0 894.5 jit_solution(441610172667195544)
XLA Ops:
  14.9 4.0 gather_fusion
  19.0 1.4 broadcast_select_fusion
  20.3 7.5 all-to-all-start
  29.4 35.4 %all-to-all-done = bf16[16,64,768]{2,1,0:T(8,128)(2,1)S(1)} async-done(((bf16[16,64,768]{2,1,0:T(8,128)(2,1)}), bf16[16,64,768]{2,1,0:T(8,128)(2,1)S(1)}, u32[]{:S(2)}, u32[]{:S(2)}) %all-to-all-start) | async-done | bytes 1572896 | tf_op jit(solution)/shard_map/all_to_all | solution.py:152
  65.2 1.6 fusion.27
  66.8 3.2 convolution_convert_fusion.5
  70.1 33.1 %all-gather.12.cloned.1.call-done = bf16[768,768]{1,0:T(8,128)(2,1)} async-done(((bf16[48,768]{1,0:T(8,128)(2,1)}), bf16[768,768]{1,0:T(8,128)(2,1)}) %all-gather.12.cloned.1.call-update) | async-done | bytes 1179664 | tf_op jit(solution)/shard_map/all_gather | solution.py:159
  103.3 3.2 convolution_convert_fusion.4
  106.5 10.5 %fusion.65 = f32[12,512,1024]{2,1,0:T(8,128)} fusion(bf16[512,12,64]{0,2,1:T(8,128)(2,1)S(1)} %bitcast.124, bf16[1024,12,64]{0,2,1:T(8,128)(2,1)S(1)} %bitcast.120), kind=kOutput, calls=%fused_computation.130 | convolution fusion | flops 805306368 | bytes 27525120 | tf_op jit(solution)/shard_map/qhd,khd->hqk/dot_general | solution.py:55
  117.0 16.7 %fusion.12 = (f32[12,512]{1,0:T(8,128)S(1)}, f32[12,512]{1,0:T(8,128)S(1)}, f32[12,512,1024]{2,1,0:T(8,128)}) fusion(pred[1024]{0:T(1024)(128)(4,1)S(1)} %broadcast_in_dim.135, f32[12,512,1024]{2,1,0:T(8,128)} %fusion.65, bf16[512,12,64]{0,2,1:T(8,128)(2,1)S(1)} %bitcast.130, bf16[1024,12,64]{0,2,1:T(8,128)(2,1)} %bitcast.121), kind=kOutput, calls=%fused_computation.26 | convolution fusion | flops 843042816 | bytes 52741120 | tf_op jit(solution)/shard_map/qhd,khd->hqk/dot_general | solution.py:55
  133.7 18.7 %fusion = (f32[12,512]{1,0:T(8,128)S(1)}, f32[12,512]{1,0:T(8,128)S(1)}) fusion(f32[12,512]{1,0:T(8,128)S(1)} %get-tuple-element.19, f32[12,512,1024]{2,1,0:T(8,128)} %get-tuple-element.47, pred[1024]{0:T(1024)(128)(4,1)S(1)} %broadcast_in_dim.135, f32[12,512]{1,0:T(8,128)S(1)} %get-tuple-element.20, f32[12,512,1024]{2,1,0:T(8,128)} %fusion.65), kind=kLoop, calls=%fused_computation.14 | loop fusion | flops 50319360 | bytes 50430976 | tf_op jit(solution)/shard_map/reduce_sum | solution.py:61
  152.4 3.2 convolution_convert_fusion.6
  155.6 11.7 %fusion.37 = bf16[12,64,512]{2,1,0:T(8,128)(2,1)S(1)} fusion(bf16[1024,12,64]{0,2,1:T(8,128)(2,1)S(1)} %bitcast.126, f32[12,512]{1,0:T(8,128)S(1)} %get-tuple-element.17, f32[12,512]{1,0:T(8,128)S(1)} %get-tuple-element.19, f32[12,512,1024]{2,1,0:T(8,128)} %get-tuple-element.47, pred[1024]{0:T(1024)(128)(4,1)S(1)} %broadcast_in_dim.135), kind=kOutput, calls=%fused_computation.87 | convolution fusion | flops 837156864 | bytes 27575296 | tf_op jit(solution)/shard_map/hqk,khd->qhd/dot_general | solution.py:63
  167.3 12.6 %fusion.36 = bf16[12,64,512]{2,1,0:T(8,128)(2,1)} fusion(bf16[1024,12,64]{0,2,1:T(8,128)(2,1)S(1)} %bitcast.127, f32[12,512]{1,0:T(8,128)S(1)} %get-tuple-element.18, f32[12,512]{1,0:T(8,128)S(1)} %get-tuple-element.20, f32[12,512,1024]{2,1,0:T(8,128)} %fusion.65, pred[1024]{0:T(1024)(128)(4,1)S(1)} %broadcast_in_dim.135), kind=kOutput, calls=%fused_computation.86 | convolution fusion | flops 837156864 | bytes 27575296 | tf_op jit(solution)/shard_map/hqk,khd->qhd/dot_general | solution.py:63
  179.9 2.2 all-gather.14.cloned.1.call-done
  182.1 3.2 multiply_reduce_fusion.4
  185.4 1.9 fusion.31
  187.8 40.9 %all-gather.18.cloned.1.call-done = bf16[768,2048]{1,0:T(8,128)(2,1)} async-done(((bf16[48,2048]{1,0:T(8,128)(2,1)}), bf16[768,2048]{1,0:T(8,128)(2,1)}) %all-gather.18.cloned.1.call-update) | async-done | bytes 3145744 | tf_op jit(solution)/shard_map/all_gather | solution.py:174
  228.7 7.5 fusion.67
  236.1 38.5 %all-gather.16.cloned.1.call-done = bf16[768,2048]{1,0:T(8,128)(2,1)} async-done(((bf16[48,2048]{1,0:T(8,128)(2,1)}), bf16[768,2048]{1,0:T(8,128)(2,1)}) %all-gather.16.cloned.1.call-update) | async-done | bytes 3145744 | tf_op jit(solution)/shard_map/all_gather | solution.py:173
  274.6 9.0 %fusion.66 = f32[1024,2048]{1,0:T(8,128)} fusion(bf16[1024,768]{1,0:T(8,128)(2,1)} %copy-done.22, bf16[768,2048]{1,0:T(8,128)(2,1)} %all-gather.16.cloned.1.call-done), kind=kOutput, calls=%fused_computation.131 | convolution fusion | flops 3221225472 | bytes 13107200 | tf_op jit(solution)/shard_map/dot_general | solution.py:41
  283.7 37.1 %all-gather.20.cloned.1.call-done = bf16[2048,768]{1,0:T(8,128)(2,1)} async-done(((bf16[128,768]{1,0:T(8,128)(2,1)}), bf16[2048,768]{1,0:T(8,128)(2,1)}) %all-gather.20.cloned.1.call-update) | async-done | bytes 3145744 | tf_op jit(solution)/shard_map/all_gather | solution.py:175
  320.8 15.1 %multiply_convert_fusion.2 = (bf16[1024,2048]{1,0:T(8,128)(2,1)S(1)}, bf16[1024,2048]{1,0:T(8,128)(2,1)}, bf16[1024,2048]{1,0:T(8,128)(2,1)}) fusion(f32[1024,2048]{1,0:T(8,128)} %fusion.66, f32[1024,2048]{1,0:T(8,128)} %fusion.67, bf16[2048,768]{1,0:T(8,128)(2,1)} %all-gather.20.cloned.1.call-done, bf16[1,1,1024,768]{3,2,1,0:T(8,128)(2,1)S(1)} %copy-done.16, ...), kind=kOutput, calls=%fused_computation.35 | convolution fusion | flops 3278110720 | bytes 34079744 | tf_op jit(solution)/shard_map/dot_general | solution.py:35
  335.9 7.2 fusion.68
  343.2 4.6 multiply_reduce_fusion.2
  349.0 1.7 copy-done.10
  350.8 2.5 convolution_convert_fusion.7
  353.3 3.3 convolution_convert_fusion.3
  358.1 10.6 %fusion.69 = f32[12,512,1024]{2,1,0:T(8,128)} fusion(bf16[512,12,64]{0,2,1:T(8,128)(2,1)S(1)} %bitcast.132, bf16[1024,12,64]{0,2,1:T(8,128)(2,1)S(1)} %bitcast.128), kind=kOutput, calls=%fused_computation.134 | convolution fusion | flops 805306368 | bytes 27525120 | tf_op jit(solution)/shard_map/qhd,khd->hqk/dot_general | solution.py:89
  368.7 12.6 %fusion.4 = f32[12,64,1024]{2,1,0:T(8,128)} fusion(bf16[512,12,64]{0,2,1:T(8,128)(2,1)S(1)} %bitcast.133, f32[12,512]{1,0:T(8,128)S(1)} %get-tuple-element.53, f32[12,512,1024]{2,1,0:T(8,128)} %fusion.65, pred[1024]{0:T(1024)(128)(4,1)S(1)} %broadcast_in_dim.135), kind=kOutput, calls=%fused_computation.18 | convolution fusion | flops 830472192 | bytes 29123584 | tf_op jit(solution)/shard_map/hqk,qhd->khd/dot_general | solution.py:106
  381.3 35.6 %multiply_reduce_fusion.1 = (f32[12,512]{1,0:T(8,128)S(1)}, f32[12,512]{1,0:T(8,128)S(1)}, f32[12,512,1024]{2,1,0:T(8,128)}) fusion(f32[12,512]{1,0:T(8,128)S(1)} %get-tuple-element.54, f32[12,512,1024]{2,1,0:T(8,128)} %get-tuple-element.47, pred[1024]{0:T(1024)(128)(4,1)S(1)} %broadcast_in_dim.135, f32[12,512,1024]{2,1,0:T(8,128)} %fusion.69, ...), kind=kOutput, calls=%fused_computation.6 | convolution fusion | flops 868208640 | bytes 103121920 | tf_op jit(solution)/shard_map/qhd,khd->hqk/dot_general | solution.py:89
  416.9 12.3 %add_convert_fusion = bf16[12,64,1024]{2,1,0:T(8,128)(2,1)S(1)} fusion(f32[12,64,1024]{2,1,0:T(8,128)} %fusion.4, bf16[512,12,64]{0,2,1:T(8,128)(2,1)S(1)} %bitcast.138, f32[12,512]{1,0:T(8,128)S(1)} %get-tuple-element.54, f32[12,512,1024]{2,1,0:T(8,128)} %get-tuple-element.47, pred[1024]{0:T(1024)(128)(4,1)S(1)} %broadcast_in_dim.135), kind=kOutput, calls=%fused_computation.64 | convolution fusion | flops 832045056 | bytes 30696448 | tf_op jit(solution)/shard_map/hqk,qhd->khd/dot_general | solution.py:106
  430.4 2.5 convolution_convert_fusion.8
  432.9 42.7 %multiply_convert_fusion.1 = (bf16[12,512,1024]{2,1,0:T(8,128)(2,1)}, bf16[12,512,1024]{2,1,0:T(8,128)(2,1)}) fusion(f32[12,512,1024]{2,1,0:T(8,128)} %get-tuple-element.51, f32[12,512]{1,0:T(8,128)S(1)} %get-tuple-element.15, f32[12,512]{1,0:T(8,128)S(1)} %get-tuple-element.54, f32[12,512,1024]{2,1,0:T(8,128)} %get-tuple-element.47, ...), kind=kLoop, calls=%fused_computation.5 | loop fusion | flops 75497472 | bytes 125928448 | tf_op jit(solution)/shard_map/convert_element_type | solution.py:93
  475.6 8.6 multiply_convert_fusion.7
  484.2 8.7 multiply_convert_fusion.6
  492.9 2.4 convolution_convert_fusion.10
  495.6 6.9 fusion.70
  502.6 7.2 multiply_convert_fusion.4
  509.8 2.5 convolution_convert_fusion.9
  512.4 7.9 convolution_convert_fusion
  520.4 7.9 convolution_convert_fusion.2
  528.5 7.8 convolution_convert_fusion.1
  537.5 2.8 fusion.38
  540.4 1.5 fusion.71
  542.5 2.5 fusion.28
  545.1 2.0 fusion.23
  547.1 3.8 all-to-all-start.1
  552.6 60.6 %reduce-scatter.10.cloned.1.call-done = bf16[48,768]{1,0:T(8,128)(2,1)} async-done(((bf16[768,768]{1,0:T(8,128)(2,1)}), bf16[48,768]{1,0:T(8,128)(2,1)}) %reduce-scatter.10.cloned.1.call-update) | async-done | bytes 73744 | tf_op jit(solution)/shard_map/reduce_scatter | solution.py:252
  613.1 69.2 %reduce-scatter.20.cloned.1.call-done = bf16[128,768]{1,0:T(8,128)(2,1)} async-done(((bf16[2048,768]{1,0:T(8,128)(2,1)}), bf16[128,768]{1,0:T(8,128)(2,1)}) %reduce-scatter.20.cloned.1.call-update) | async-done | bytes 196624 | tf_op jit(solution)/shard_map/reduce_scatter | solution.py:208
  682.3 69.0 %reduce-scatter.16.cloned.1.call-done = bf16[48,2048]{1,0:T(8,128)(2,1)} async-done(((bf16[768,2048]{1,0:T(8,128)(2,1)}), bf16[48,2048]{1,0:T(8,128)(2,1)}) %reduce-scatter.16.cloned.1.call-update) | async-done | bytes 196624 | tf_op jit(solution)/shard_map/reduce_scatter | solution.py:202
  751.3 69.0 %reduce-scatter.18.cloned.1.call-done = bf16[48,2048]{1,0:T(8,128)(2,1)} async-done(((bf16[768,2048]{1,0:T(8,128)(2,1)}), bf16[48,2048]{1,0:T(8,128)(2,1)}) %reduce-scatter.18.cloned.1.call-update) | async-done | bytes 196624 | tf_op jit(solution)/shard_map/reduce_scatter | solution.py:205
  820.3 8.6 fusion.35
  828.9 29.9 %all-reduce.2 = (bf16[768]{0:T(1024)(128)(2,1)S(1)}, bf16[768]{0:T(1024)(128)(2,1)S(1)}) all-reduce(bf16[768]{0:T(1024)(128)(2,1)S(1)} %get-tuple-element.13, bf16[768]{0:T(1024)(128)(2,1)S(1)} %copy-done.36), channel_id=2, replica_groups=mesh['shard'=16,'replica'=2] {'shard'}, use_global_device_ids=true, to_apply=%region_16.17.clone | all-reduce | flops 1536 | bytes 6144
  858.9 4.9 all-reduce.3
  864.9 2.0 convert_select_fusion.1
  866.9 8.6 scatter_custom_fusion
  876.4 1.6 convert_element_type.219
  878.0 1.6 convert_element_type.223
  879.5 1.6 convert_element_type.225
  881.1 1.6 convert_element_type.227
  882.6 1.7 convert_element_type.229
  884.3 1.7 convert_element_type.231
  886.0 1.7 convert_element_type.233
  (153 shorter events, 19.9 us)
Async XLA Ops:
  7.2 7.7 copy-start
  7.2 59.6 %all-gather.10.cloned.1.call-start = ((), (), s32[]{:S(2)}) async-start(), calls=%async_computation.10 | async-start | bytes 1253376 | tf_op jit(solution)/shard_map/all_gather | solution.py:158
  7.9 95.3 %all-gather.12.cloned.1.call-start = ((), (), s32[]{:S(2)}) async-start(), calls=%async_computation.11 | async-start | bytes 1253376 | tf_op jit(solution)/shard_map/all_gather | solution.py:159
  8.7 143.7 %all-gather.8.cloned.1.call-start = ((), (), s32[]{:S(2)}) async-start(), calls=%async_computation.9 | async-start | bytes 1253376 | tf_op jit(solution)/shard_map/all_gather | solution.py:160
  9.4 172.7 %all-gather.14.cloned.1.call-start = ((), (), s32[]{:S(2)}) async-start(), calls=%async_computation.12 | async-start | bytes 1253376 | tf_op jit(solution)/shard_map/all_gather | solution.py:161
  10.0 218.7 %all-gather.18.cloned.1.call-start = ((), (), s32[]{:S(2)}) async-start(), calls=%async_computation.14 | async-start | bytes 3342336 | tf_op jit(solution)/shard_map/all_gather | solution.py:174
  10.6 264.1 %all-gather.16.cloned.1.call-start = ((), (), s32[]{:S(2)}) async-start(), calls=%async_computation.13 | async-start | bytes 3342336 | tf_op jit(solution)/shard_map/all_gather | solution.py:173
  14.3 0.6 copy-start.35
  19.0 1.4 copy-start.32
  20.3 44.9 %copy-start.26 = (f32[768]{0:T(1024)S(1)}, f32[768]{0:T(1024)}, u32[]{:S(2)}) copy-start(f32[768]{0:T(1024)} %param.16) | copy-start | bytes 9220
  20.3 44.4 %all-to-all-start = ((bf16[16,64,768]{2,1,0:T(8,128)(2,1)}), bf16[16,64,768]{2,1,0:T(8,128)(2,1)S(1)}, u32[]{:S(2)}, u32[]{:S(2)}) async-start(bf16[16,64,768]{2,1,0:T(8,128)(2,1)} %broadcast_select_fusion), calls=%async_computation | async-start | bytes 3145728 | tf_op jit(solution)/shard_map/all_to_all | solution.py:152
  27.9 292.9 %all-gather.20.cloned.1.call-start = ((), (), s32[]{:S(2)}) async-start(), calls=%async_computation.15 | async-start | bytes 3342336 | tf_op jit(solution)/shard_map/all_gather | solution.py:175
  28.6 523.9 %reduce-scatter.14.cloned.1.call-start = ((), (), s32[]{:S(2)}) async-start(), calls=%async_computation.19 | async-start | bytes 1253376 | tf_op jit(solution)/shard_map/reduce_scatter | solution.py:258
  64.8 120.6 %copy-start.2 = (bf16[16,64,768]{2,1,0:T(8,128)(2,1)}, bf16[16,64,768]{2,1,0:T(8,128)(2,1)S(1)}, u32[]{:S(2)}) copy-start(bf16[16,64,768]{2,1,0:T(8,128)(2,1)S(1)} %all-to-all-done) | copy-start | bytes 4718596
  65.2 1.6 copy-start.30
  65.2 1.6 copy-start.28
  70.1 36.3 %copy-start.6 = (bf16[512,768]{0,1:T(8,128)(2,1)}, bf16[512,768]{0,1:T(8,128)(2,1)S(1)}, u32[]{:S(2)}) copy-start(bf16[512,768]{0,1:T(8,128)(2,1)S(1)} %get-tuple-element.39) | copy-start | bytes 2359300
  70.1 46.9 %copy-start.14 = (bf16[512,768]{0,1:T(8,128)(2,1)}, bf16[512,768]{0,1:T(8,128)(2,1)S(1)}, u32[]{:S(2)}) copy-start(bf16[512,768]{0,1:T(8,128)(2,1)S(1)} %get-tuple-element.40) | copy-start | bytes 2359300
  106.4 10.5 %copy-start.4 = (bf16[1024,768]{0,1:T(8,128)(2,1)}, bf16[1024,768]{0,1:T(8,128)(2,1)S(1)}, u32[]{:S(2)}) copy-start(bf16[1024,768]{0,1:T(8,128)(2,1)S(1)} %convolution_convert_fusion.4) | copy-start | bytes 4718596
  155.6 11.7 %copy-start.8 = (bf16[1024,768]{0,1:T(8,128)(2,1)}, bf16[1024,768]{0,1:T(8,128)(2,1)S(1)}, u32[]{:S(2)}) copy-start(bf16[1024,768]{0,1:T(8,128)(2,1)S(1)} %convolution_convert_fusion.6) | copy-start | bytes 4718596
  185.3 2.1 copy-start.12
  185.3 2.1 copy-start.34
  187.8 40.9 %copy-start.22 = (bf16[1024,768]{1,0:T(8,128)(2,1)}, bf16[1024,768]{1,0:T(8,128)(2,1)S(1)}, u32[]{:S(2)}) copy-start(bf16[1024,768]{1,0:T(8,128)(2,1)S(1)} %multiply_convert_fusion.5) | copy-start | bytes 4718596
  236.1 84.7 %copy-start.16 = (bf16[1,1,1024,768]{3,2,1,0:T(8,128)(2,1)S(1)}, bf16[1,1,1024,768]{3,2,1,0:T(8,128)(2,1)}, u32[]{:S(2)}) copy-start(bf16[1,1,1024,768]{3,2,1,0:T(8,128)(2,1)} %param.25) | copy-start | bytes 4718596
  320.8 15.1 %copy-start.38 = (bf16[768,2048]{1,0:T(8,128)(2,1)S(1)}, bf16[768,2048]{1,0:T(8,128)(2,1)}, u32[]{:S(2)}) copy-start(bf16[768,2048]{1,0:T(8,128)(2,1)} %all-gather.16.cloned.1.call-done) | copy-start | bytes 9437188
  335.9 7.2 copy-start.43
  335.9 7.2 copy-start.13
  335.9 7.2 copy-start.37
  347.7 3.0 copy-start.41
  349.0 1.8 copy-start.10
  350.8 2.6 copy-start.40
  353.3 199.2 %reduce-scatter.12.cloned.1.call-start = ((), (), s32[]{:S(2)}) async-start(), calls=%async_computation.18 | async-start | bytes 1253376 | tf_op jit(solution)/shard_map/reduce_scatter | solution.py:255
  356.6 1.4 copy-start.9
  416.9 13.5 %copy-start.20 = (bf16[16,64,768]{2,1,0:T(8,128)(2,1)S(1)}, bf16[16,64,768]{2,1,0:T(8,128)(2,1)}, u32[]{:S(2)}) copy-start(bf16[16,64,768]{2,1,0:T(8,128)(2,1)} %fusion.31) | copy-start | bytes 4718596
  429.2 1.2 copy-start.17
  432.9 119.7 %reduce-scatter.8.cloned.1.call-start = ((), (), s32[]{:S(2)}) async-start(), calls=%async_computation.16 | async-start | bytes 1253376 | tf_op jit(solution)/shard_map/reduce_scatter | solution.py:249
  432.9 42.7 %copy-start.5 = (bf16[1024,768]{0,1:T(8,128)(2,1)S(1)}, bf16[1024,768]{0,1:T(8,128)(2,1)}, u32[]{:S(2)}) copy-start(bf16[1024,768]{0,1:T(8,128)(2,1)} %copy-done.4) | copy-start | bytes 4718596
  484.2 8.7 copy-start.19
  492.9 2.5 copy-start.24
  492.9 2.7 copy-start.15
  495.4 7.2 copy-start.7
  495.4 117.7 %reduce-scatter.10.cloned.1.call-start = ((), (), s32[]{:S(2)}) async-start(), calls=%async_computation.17 | async-start | bytes 1253376 | tf_op jit(solution)/shard_map/reduce_scatter | solution.py:252
  502.6 7.3 copy-start.21
  512.3 169.9 %reduce-scatter.20.cloned.1.call-start = ((), (), s32[]{:S(2)}) async-start(), calls=%async_computation.22 | async-start | bytes 3342336 | tf_op jit(solution)/shard_map/reduce_scatter | solution.py:208
  520.3 230.9 %reduce-scatter.16.cloned.1.call-start = ((), (), s32[]{:S(2)}) async-start(), calls=%async_computation.20 | async-start | bytes 3342336 | tf_op jit(solution)/shard_map/reduce_scatter | solution.py:202
  528.3 292.0 %reduce-scatter.18.cloned.1.call-start = ((), (), s32[]{:S(2)}) async-start(), calls=%async_computation.21 | async-start | bytes 3342336 | tf_op jit(solution)/shard_map/reduce_scatter | solution.py:205
  536.4 1.1 copy-start.25
  537.5 2.8 copy-start.39
  540.3 1.5 copy-start.3
  540.3 1.9 copy-start.18
  540.3 2.2 copy-start.23
  540.3 2.2 copy-start.27
  540.4 2.2 copy-start.29
  542.5 2.5 copy-start.31
  542.5 2.6 copy-start.11
  547.1 4.2 copy-start.42
  547.1 317.8 %all-to-all-start.1 = ((bf16[16,64,768]{2,1,0:T(8,128)(2,1)}), bf16[16,64,768]{2,1,0:T(8,128)(2,1)S(1)}, u32[]{:S(2)}, u32[]{:S(2)}) async-start(bf16[16,64,768]{2,1,0:T(8,128)(2,1)} %bitcast.26), calls=%async_computation.1 | async-start | bytes 3145728 | tf_op jit(solution)/shard_map/all_to_all | solution.py:241
  550.9 325.5 %all-reduce.7.cloned.1.call-start = ((), (), s32[]{:S(2)}) async-start(), calls=%async_computation.23 | async-start | bytes 1769472 | tf_op jit(solution)/shard_map/psum | solution.py:270
  820.3 8.6 copy-start.36
  820.3 44.6 %copy-start.33 = (pred[16,64]{1,0:T(8,128)(4,1)S(1)}, pred[16,64]{1,0:T(8,128)(4,1)}, u32[]{:S(2)}) copy-start(pred[16,64]{1,0:T(8,128)(4,1)} %copy-done.32) | copy-start | bytes 3076
  866.9 20.9 %copy-start.1 = (bf16[1,512,768]{2,1,0:T(8,128)(2,1)S(1)}, bf16[1,512,768]{2,1,0:T(8,128)(2,1)}, u32[]{:S(2)}) copy-start(bf16[1,512,768]{2,1,0:T(8,128)(2,1)} %param.13) | copy-start | bytes 2359300
Sparse Core Ops, SparseCore 0:
  10.3 51.5 all-gather.9
  64.1 39.0 all-gather.11
  105.6 37.1 all-gather.7
  144.9 37.1 all-gather.13
  184.3 44.3 all-gather.17
  230.8 43.8 all-gather.15
  276.9 43.8 all-gather.19
  353.4 56.5 reduce-scatter.13
  433.0 56.6 reduce-scatter.11
  495.5 56.5 reduce-scatter.7
  555.7 57.3 reduce-scatter.9
  616.8 65.4 reduce-scatter.19
  686.1 65.1 reduce-scatter.15
  754.9 65.2 reduce-scatter.17
  822.8 35.5 all-reduce.6
where the time goes:
time: 900 us; the launch traced here: 895 us
  waiting for transfers between devices  459 us (51%)
  matrix products  262 us (29%)
  other arithmetic  97.9 us (11%)
  blocking collectives  34.8 us (4%)
  between operations  15.5 us (2%)
  starting transfers between devices  12.6 us (1%)
  local copies, waits for them, and re-layouts  12.1 us (1%)
    reduce_scatter x1, waiting for transfers between devices, shards(): lax.psum_scatter(grad_down.astype(jnp.bfloat16), 'shard', scatter_dimensi...  69.2 us
    reduce_scatter x1, waiting for transfers between devices, shards(): lax.psum_scatter(grad_wg.astype(jnp.bfloat16), 'shard', scatter_dimension...  69 us
    reduce_scatter x1, waiting for transfers between devices, shards(): lax.psum_scatter(grad_wu.astype(jnp.bfloat16), 'shard', scatter_dimension...  69 us
    reduce_scatter x1, waiting for transfers between devices, shards(): lax.psum_scatter(grad_wk.astype(jnp.bfloat16), 'shard', scatter_dimension...  60.6 us
    dot_general x2, matrix products, attend_backward(): jnp.einsum('qhd,khd->hqk', grad_heads, value_heads, preferred_element_typ...  46.2 us
    convert_element_type x1, other arithmetic, attend_backward(): grad_scores = (prob_vals * (grad_probs - row_dot)).astype(jnp.bfloat16)  42.7 us
    all_gather x1, waiting for transfers between devices, shards(): lax.all_gather(w_up, 'shard', axis=0, tiled=True)  40.9 us
    all_gather x1, waiting for transfers between devices, shards(): lax.all_gather(w_gate, 'shard', axis=0, tiled=True)  38.5 us
  transfers between devices with their start and end apart: 17, of which 10 were waited for; matrix products, arithmetic and copies ran while one was open for 36% of the time, Pallas kernels for 0%

commit v1 on v0

v1 whole, which is shorter than its diff:
```python
import functools

import jax
import jax.numpy as jnp
from jax import lax
from jax.experimental import pallas as pl
from jax.experimental.pallas import tpu as pltpu
from jax.sharding import PartitionSpec as P

H = 12
HD = 64
LANES = 256
GAIN_ROWS = 16

norm_eps = 1e-06
neg_big = -1e30
bf16 = jnp.bfloat16
f32 = jnp.float32


def rms_scale(tok_rows, gain_vec):
    inverse = lax.rsqrt(jnp.mean(tok_rows * tok_rows, axis=-1, keepdims=True) + norm_eps)
    return tok_rows * inverse * gain_vec


def gelu_mix(gate_vals, up_vals):
    return jax.nn.gelu(gate_vals, approximate=True) * up_vals


def left_dot(lhs_mat, rhs_mat):
    return lax.dot_general(
        lhs_mat, rhs_mat, (((0,), (0,)), ((), ())), preferred_element_type=jnp.float32
    )


def right_dot(lhs_mat, rhs_mat):
    return lax.dot_general(
        lhs_mat, rhs_mat, (((1,), (1,)), ((), ())), preferred_element_type=jnp.float32
    )


def plain_dot(lhs_mat, rhs_mat):
    return jnp.dot(lhs_mat, rhs_mat, preferred_element_type=jnp.float32)


def slot_start(units_ref, order_ref, slot, shard_count):
    wanted = order_ref[0, slot]
    start = jnp.int32(0)
    count = jnp.int32(0)
    for k in range(shard_count):
        units = units_ref[0, k]
        start = start + jnp.where(k < wanted, units, 0)
        count = count + jnp.where(k == wanted, units, 0)
    return start, count


def deal_kernel(units_ref, order_ref, rows_ref, out_ref):
    shard_count, unit_max, _ = out_ref.shape
    given = rows_ref.shape[0]
    row = lax.broadcasted_iota(jnp.int32, (unit_max, given), 0)
    col = lax.broadcasted_iota(jnp.int32, (unit_max, given), 1)

    def step(slot, carry):
        start, count = slot_start(units_ref, order_ref, slot, shard_count)
        pick = jnp.where((col - start == row) & (row < count), 1.0, 0.0).astype(bf16)
        out_ref[slot] = plain_dot(pick, rows_ref[...]).astype(bf16)
        return carry

    lax.fori_loop(0, shard_count, step, 0)


def undeal_kernel(units_ref, order_ref, back_ref, out_ref, pick_ref):
    shard_count, unit_max, width = back_ref.shape
    given = out_ref.shape[0]
    row = lax.broadcasted_iota(jnp.int32, (unit_max, given), 0)
    col = lax.broadcasted_iota(jnp.int32, (unit_max, given), 1)

    def step(slot, carry):
        start, count = slot_start(units_ref, order_ref, slot, shard_count)
        pick = jnp.where((col - start == row) & (row < count), 1.0, 0.0).astype(bf16)
        pick_ref[pl.ds(pl.multiple_of(slot * unit_max, unit_max), unit_max), :] = pick
        return carry

    lax.fori_loop(0, shard_count, step, 0)
    whole = back_ref[...].reshape(shard_count * unit_max, width)
    out_ref[...] = left_dot(pick_ref[...], whole).astype(bf16)


def smem():
    return pl.BlockSpec(memory_space=pltpu.SMEM)


def vmem():
    return pl.BlockSpec(memory_space=pltpu.VMEM)


def deal_rows(units, order, rows, shard_count, unit_max):
    return pl.pallas_call(
        deal_kernel,
        out_shape=jax.ShapeDtypeStruct((shard_count, unit_max, rows.shape[1]), bf16),
        in_specs=[smem(), smem(), vmem()],
        out_specs=vmem(),
        name="deal_rows",
    )(units, order, rows)


def undeal_rows(units, order, back, given):
    shard_count, unit_max, width = back.shape
    return pl.pallas_call(
        undeal_kernel,
        out_shape=jax.ShapeDtypeStruct((given, width), bf16),
        in_specs=[smem(), smem(), vmem()],
        out_specs=vmem(),
        scratch_shapes=[pltpu.VMEM((shard_count * unit_max, given), bf16)],
        name="undeal_rows",
    )(units, order, back)


def attend_forward(queries, keys_all, values_all, live_keys):
    total_rows = queries.shape[0]
    row_block = min(512, total_rows)
    factor = HD ** (-0.5)
    key_heads = keys_all.reshape(total_rows, H, HD)
    value_heads = values_all.reshape(total_rows, H, HD)
    mixed_list = []
    stat_list = []
    for row_begin in range(0, total_rows, row_block):
        query_heads = queries[row_begin : row_begin + row_block].reshape(row_block, H, HD)
        scores = (
            jnp.einsum("qhd,khd->hqk", query_heads, key_heads, preferred_element_type=jnp.float32)
            * factor
        )
        scores = jnp.where(live_keys[None, None, :], scores, neg_big)
        row_max = jnp.max(scores, axis=-1, keepdims=True)
        exp_vals = jnp.exp(scores - row_max)
        row_total = jnp.sum(exp_vals, axis=-1, keepdims=True)
        prob_vals = (exp_vals / row_total).astype(jnp.bfloat16)
        mixed_rows = jnp.einsum(
            "hqk,khd->qhd", prob_vals, value_heads, preferred_element_type=jnp.float32
        )
        mixed_list.append(mixed_rows.reshape(row_block, H * HD))
        stat_list.append(row_max + jnp.log(row_total))
    return (jnp.concatenate(mixed_list, axis=0), jnp.concatenate(stat_list, axis=1))


def attend_backward(queries, keys_all, values_all, live_keys, log_totals, grad_mixed):
    total_rows = queries.shape[0]
    row_block = min(512, total_rows)
    factor = HD ** (-0.5)
    key_heads = keys_all.reshape(total_rows, H, HD)
    value_heads = values_all.reshape(total_rows, H, HD)
    grad_keys = jnp.zeros((total_rows, H, HD), jnp.float32)
    grad_values = jnp.zeros((total_rows, H, HD), jnp.float32)
    query_list = []
    for row_begin in range(0, total_rows, row_block):
        query_heads = queries[row_begin : row_begin + row_block].reshape(row_block, H, HD)
        grad_heads = grad_mixed[row_begin : row_begin + row_block].reshape(row_block, H, HD)
        scores = (
            jnp.einsum("qhd,khd->hqk", query_heads, key_heads, preferred_element_type=jnp.float32)
            * factor
        )
        scores = jnp.where(live_keys[None, None, :], scores, neg_big)
        prob_vals = jnp.exp(scores - log_totals[:, row_begin : row_begin + row_block])
        grad_probs = jnp.einsum(
            "qhd,khd->hqk", grad_heads, value_heads, preferred_element_type=jnp.float32
        )
        row_dot = jnp.sum(prob_vals * grad_probs, axis=-1, keepdims=True)
        grad_scores = (prob_vals * (grad_probs - row_dot)).astype(jnp.bfloat16)
        grad_query = (
            jnp.einsum("hqk,khd->qhd", grad_scores, key_heads, preferred_element_type=jnp.float32)
            * factor
        )
        query_list.append(grad_query.reshape(row_block, H * HD))
        grad_keys = (
            grad_keys
            + jnp.einsum(
                "hqk,qhd->khd", grad_scores, query_heads, preferred_element_type=jnp.float32
            )
            * factor
        )
        grad_values = grad_values + jnp.einsum(
            "hqk,qhd->khd",
            prob_vals.astype(jnp.bfloat16),
            grad_heads,
            preferred_element_type=jnp.float32,
        )
    return (
        jnp.concatenate(query_list, axis=0),
        grad_keys.reshape(total_rows, H * HD),
        grad_values.reshape(total_rows, H * HD),
    )


def to_blocks(mat, parts):
    rows = mat.shape[0] // parts
    cols = mat.shape[1] // LANES
    split = mat.reshape(parts, rows, cols, LANES).transpose(0, 2, 1, 3)
    return split.reshape(parts, cols * rows, LANES)


def from_blocks(packed, rows):
    parts, total, _ = packed.shape
    cols = total // rows
    split = packed.reshape(parts, cols, rows, LANES).transpose(0, 2, 1, 3)
    return split.reshape(parts * rows, cols * LANES)


def gather_packed(mats):
    packed = jnp.concatenate([to_blocks(m, 1)[0] for m in mats], axis=0)
    count = lax.axis_size("shard")
    whole = lax.all_gather(packed, "shard", axis=0, tiled=True)
    whole = whole.reshape(count, packed.shape[0], LANES)
    out = []
    begin = 0
    for m in mats:
        size = m.shape[0] * (m.shape[1] // LANES)
        out.append(from_blocks(whole[:, begin : begin + size], m.shape[0]))
        begin += size
    return out


def replica_sum(part):
    count = lax.axis_size("replica")
    step = 1
    while step < count:
        other = lax.ppermute(part, "replica", [(i, i ^ step) for i in range(count)])
        part = (part.astype(f32) + other.astype(f32)).astype(bf16)
        step *= 2
    return part


def scatter_packed(mats, gain):
    count = lax.axis_size("shard")
    own = gain.shape[0] // count
    gain_rows = jnp.pad(
        gain.astype(bf16).reshape(count, 1, own), ((0, 0), (0, GAIN_ROWS - 1), (0, LANES - own))
    )
    packed = jnp.concatenate([to_blocks(m.astype(bf16), count) for m in mats] + [gain_rows], axis=1)
    flat = packed.reshape(-1, LANES)
    share = lax.psum_scatter(flat, "shard", scatter_dimension=0, tiled=True)
    total = replica_sum(share).astype(f32)
    out = []
    begin = 0
    for m in mats:
        rows = m.shape[0] // count
        size = rows * (m.shape[1] // LANES)
        out.append(from_blocks(total[None, begin : begin + size], rows))
        begin += size
    out.append(total[begin, :own])
    return out


def shards(
    x_in,
    seq_units,
    deal,
    gain_attn,
    w_query,
    w_key,
    w_value,
    w_out,
    gain_ffn,
    w_gate,
    w_up,
    w_down,
    d_out,
):
    shard_count = lax.axis_size("shard")
    my_index = lax.axis_index("shard")
    given, width = x_in.shape[1:]
    span = d_out.shape[2]
    unit_max = span // shard_count
    units_row = seq_units[0]
    order_row = deal[0]
    slot_ids = jnp.arange(shard_count, dtype=jnp.int32)
    inner_idx = jnp.arange(unit_max, dtype=jnp.int32)
    outgoing = deal_rows(seq_units, deal, x_in[0], shard_count, unit_max)
    arrived = lax.all_to_all(outgoing, "shard", split_axis=0, concat_axis=0, tiled=True)
    own_seq = jnp.sum(jnp.where(slot_ids == my_index, order_row, 0))
    own_count = jnp.sum(jnp.where(slot_ids == own_seq, units_row, 0))
    live_rows = jnp.broadcast_to(inner_idx[None, :] < own_count, (shard_count, unit_max)).reshape(
        span
    )
    wq_full, wk_full, wv_full, wo_full = gather_packed((w_query, w_key, w_value, w_out))
    wg_full, wu_full, wd_full = gather_packed((w_gate, w_up, w_down))
    tok_float = arrived.reshape(span, width).astype(jnp.float32)
    normed_one_f, norm_one_back = jax.vjp(rms_scale, tok_float, gain_attn)
    normed_one = normed_one_f.astype(jnp.bfloat16)
    queries = plain_dot(normed_one, wq_full).astype(jnp.bfloat16)
    keys_all = plain_dot(normed_one, wk_full).astype(jnp.bfloat16)
    values_all = plain_dot(normed_one, wv_full).astype(jnp.bfloat16)
    mixed_f, log_totals = attend_forward(queries, keys_all, values_all, live_rows)
    mixed_rows = mixed_f.astype(jnp.bfloat16)
    hidden_res = tok_float + plain_dot(mixed_rows, wo_full)
    normed_two_f, norm_two_back = jax.vjp(rms_scale, hidden_res, gain_ffn)
    normed_two = normed_two_f.astype(jnp.bfloat16)
    gate_vals = plain_dot(normed_two, wg_full)
    up_vals = plain_dot(normed_two, wu_full)
    act_f, mix_back = jax.vjp(gelu_mix, gate_vals, up_vals)
    act_vals = act_f.astype(jnp.bfloat16)
    result = jnp.where(live_rows[:, None], hidden_res + plain_dot(act_vals, wd_full), 0.0)
    layer_out = result.astype(jnp.bfloat16).reshape(1, 1, span, width)
    grad_y = jnp.where(live_rows[:, None], d_out[0, 0].astype(jnp.float32), 0.0)
    grad_ffn_b = grad_y.astype(jnp.bfloat16)
    grad_down = left_dot(act_vals, grad_ffn_b)
    grad_act = right_dot(grad_ffn_b, wd_full)
    grad_gate_f, grad_up_f = mix_back(grad_act)
    grad_gate_b = grad_gate_f.astype(jnp.bfloat16)
    grad_up_b = grad_up_f.astype(jnp.bfloat16)
    grad_wg = left_dot(normed_two, grad_gate_b)
    grad_wu = left_dot(normed_two, grad_up_b)
    grad_n2 = right_dot(grad_gate_b, wg_full) + right_dot(grad_up_b, wu_full)
    grad_h_norm, grad_gain_two = norm_two_back(grad_n2)
    out_wg, out_wu, out_wd, out_gain_two = scatter_packed((grad_wg, grad_wu, grad_down), grad_gain_two)
    grad_hidden = grad_y + grad_h_norm
    grad_attn_b = grad_hidden.astype(jnp.bfloat16)
    grad_wo = left_dot(mixed_rows, grad_attn_b)
    grad_mixed = right_dot(grad_attn_b, wo_full).astype(jnp.bfloat16)
    grad_q_f, grad_k_f, grad_v_f = attend_backward(
        queries, keys_all, values_all, live_rows, log_totals, grad_mixed
    )
    grad_q_b = grad_q_f.astype(jnp.bfloat16)
    grad_k_b = grad_k_f.astype(jnp.bfloat16)
    grad_v_b = grad_v_f.astype(jnp.bfloat16)
    grad_wq = left_dot(normed_one, grad_q_b)
    grad_wk = left_dot(normed_one, grad_k_b)
    grad_wv = left_dot(normed_one, grad_v_b)
    grad_n1 = (
        right_dot(grad_q_b, wq_full) + right_dot(grad_k_b, wk_full) + right_dot(grad_v_b, wv_full)
    )
    grad_x_norm, grad_gain_one = norm_one_back(grad_n1)
    grad_tokens = (
        (grad_hidden + grad_x_norm).astype(jnp.bfloat16).reshape(shard_count, unit_max, width)
    )
    returned = lax.all_to_all(grad_tokens, "shard", split_axis=0, concat_axis=0, tiled=True)
    grad_x = undeal_rows(seq_units, deal, returned, given)[None]
    out_wq, out_wk, out_wv, out_wo, out_gain_one = scatter_packed(
        (grad_wq, grad_wk, grad_wv, grad_wo), grad_gain_one
    )
    return (
        layer_out,
        grad_x,
        out_gain_one,
        out_gain_two,
        out_wq,
        out_wk,
        out_wv,
        out_wo,
        out_wg,
        out_wu,
        out_wd,
    )


def solution(mesh):
    return jax.shard_map(
        shards,
        mesh=mesh,
        in_specs=(
            P("replica", "shard", None),
            P("replica", None),
            P("replica", None),
            P(),
            P("shard", None),
            P("shard", None),
            P("shard", None),
            P("shard", None),
            P(),
            P("shard", None),
            P("shard", None),
            P("shard", None),
            P("replica", "shard", None, None),
        ),
        out_specs=(
            P("replica", "shard", None, None),
            P("replica", "shard", None),
            P("shard"),
            P("shard"),
            P("shard", None),
            P("shard", None),
            P("shard", None),
            P("shard", None),
            P("shard", None),
            P("shard", None),
            P("shard", None),
        ),
        check_vma=False,
    )
```

time: 900 us -> 667 us (0.74)
  waiting for transfers between devices: 459 us -> 217 us
  local copies, waits for them, and re-layouts: 12.1 us -> 82.9 us
  blocking collectives: 34.8 us -> 0 us
  matrix products: 262 us -> 237 us
  other arithmetic: 97.9 us -> 77.7 us
  Pallas kernels: 0 us -> 10.9 us
    all_gather x7 -> x2, waiting for transfers between devices: 152 us -> 9.79 us  [gather_packed(): whole = lax.all_gather(packed, 'shard', axis=0, tiled=True)]
    reduce_scatter x7 -> x2, waiting for transfers between devices: 268 us -> 152 us  [scatter_packed(): share = lax.psum_scatter(flat, 'shard', scatter_dimension=0, tiled=True)]
    unnamed x1 -> x0, blocking collectives: 29.9 us -> none
    transpose x0 -> x26, local copies, waits for them, and re-layouts: none -> 21.9 us  [the longest x12 13.3 us: from_blocks(): split = packed.reshape(parts, cols, rows, LANES).transpose(0, 2, 1, 3)]
    unnamed x91 -> x151, local copies, waits for them, and re-layouts: 7.63 us -> 27.4 us
    reshape x0 -> x10, local copies, waits for them, and re-layouts: none -> 16.6 us  [to_blocks(): split = mat.reshape(parts, rows, cols, LANES).transpose(0, 2, 1, 3)]
    convert_element_type x10 -> x2, other arithmetic: 14.3 us -> 1.18 us  [scatter_packed(): total = replica_sum(share).astype(f32)]
    dot_general x7, matrix products: 37.8 us -> 26.3 us  [plain_dot(): return jnp.dot(lhs_mat, rhs_mat, preferred_element_type=jnp.float32)]
  transfers between devices with their start and end apart: 17 -> 8, of which waited for: 10 -> 5; matrix products, arithmetic and copies ran while one was open for 36% -> 22% of each run, Pallas kernels for 0% -> 2%
where the time goes in v1:
time: 667 us; the launch traced here: 658 us
  matrix products  237 us (36%)
  waiting for transfers between devices  217 us (33%)
  local copies, waits for them, and re-layouts  82.9 us (12%)
  other arithmetic  77.7 us (12%)
  starting transfers between devices  17.2 us (3%)
  between operations  15.2 us (2%)
  Pallas kernels  10.9 us (2%)
    reduce_scatter x2, waiting for transfers between devices, scatter_packed(): share = lax.psum_scatter(flat, 'shard', scatter_dimension=0, tiled=True)  152 us
    all_to_all x1, waiting for transfers between devices, shards(): lax.all_to_all(outgoing, 'shard', split_axis=0, concat_axis=0, tiled=True)  46.5 us
    dot_general x2, matrix products, attend_backward(): jnp.einsum('qhd,khd->hqk', grad_heads, value_heads, preferred_element_typ...  45.7 us
    convert_element_type x1, other arithmetic, attend_backward(): grad_scores = (prob_vals * (grad_probs - row_dot)).astype(jnp.bfloat16)  42 us
    dot_general x7, matrix products, right_dot(): lax.dot_general(lhs_mat, rhs_mat, (((1,), (1,)), ((), ())), preferred_ele...  35.6 us
    dot_general x2, matrix products, attend_forward(): jnp.einsum('qhd,khd->hqk', query_heads, key_heads, preferred_element_type...  27.6 us
    unnamed x151, local copies, waits for them, and re-layouts  27.4 us
    dot_general x7, matrix products, plain_dot(): return jnp.dot(lhs_mat, rhs_mat, preferred_element_type=jnp.float32)  26.3 us
  transfers between devices with their start and end apart: 8, of which 5 were waited for; matrix products, arithmetic and copies ran while one was open for 22% of the time, Pallas kernels for 2%

profile of v1, /device:TPU:0, one launch (start us, length us, event | category | flops | bytes accessed | tf_op | source)
XLA Modules:
  0.0 658.1 jit_solution(14381144748814090960)
XLA Ops:
  11.8 6.6 %deal_rows.1 = bf16[16,64,768]{2,1,0:T(8,128)(2,1)} custom-call(s32[1,16]{1,0:T(1,128)} %units_ref.3, s32[1,16]{1,0:T(1,128)} %order_ref.3, bf16[512,768]{1,0:T(8,128)(2,1)} %bitcast.366), custom_call_target="tpu_custom_call" | custom-call | tf_op jit(solution)/shard_map/deal_rows/pallas_call | solution.py:98
  18.4 7.5 %all-to-all-start = ((bf16[16,64,768]{2,1,0:T(8,128)(2,1)}), bf16[16,64,768]{2,1,0:T(8,128)(2,1)S(1)}, u32[]{:S(2)}, u32[]{:S(2)}) async-start(bf16[16,64,768]{2,1,0:T(8,128)(2,1)} %deal_rows.1), calls=%async_computation | async-start | bytes 3145728 | tf_op jit(solution)/shard_map/all_to_all | solution.py:278
  30.2 46.5 %all-to-all-done = bf16[16,64,768]{2,1,0:T(8,128)(2,1)S(1)} async-done(((bf16[16,64,768]{2,1,0:T(8,128)(2,1)}), bf16[16,64,768]{2,1,0:T(8,128)(2,1)S(1)}, u32[]{:S(2)}, u32[]{:S(2)}) %all-to-all-start) | async-done | bytes 1572896 | tf_op jit(solution)/shard_map/all_to_all | solution.py:278
  78.3 9.8 %all-gather.3.cloned.1.call-done = bf16[9216,256]{1,0:T(8,128)(2,1)} async-done(((bf16[576,256]{1,0:T(8,128)(2,1)}), bf16[9216,256]{1,0:T(8,128)(2,1)}) %all-gather.3.cloned.1.call-update) | async-done | bytes 4718608 | tf_op jit(solution)/shard_map/all_gather | solution.py:211
  88.1 2.6 fusion.81
  91.6 1.3 copy.86
  96.2 1.4 convolution_convert_fusion.5
  99.5 1.4 convolution_convert_fusion.4
  101.0 2.6 convolution_convert_fusion.6
  103.5 10.4 %fusion.86 = f32[12,512,1024]{2,1,0:T(8,128)} fusion(bf16[512,12,64]{0,2,1:T(8,128)(2,1)S(1)} %bitcast.284, bf16[1024,12,64]{0,2,1:T(8,128)(2,1)S(1)} %bitcast.280), kind=kOutput, calls=%fused_computation.152 | convolution fusion | flops 805306368 | bytes 27525120 | tf_op jit(solution)/shard_map/qhd,khd->hqk/dot_general | solution.py:130
  114.0 17.2 %fusion.13 = (f32[12,512]{1,0:T(8,128)S(1)}, f32[12,512]{1,0:T(8,128)S(1)}, f32[12,512,1024]{2,1,0:T(8,128)}) fusion(pred[1024]{0:T(1024)(128)(4,1)S(1)} %broadcast_in_dim.78, f32[12,512,1024]{2,1,0:T(8,128)} %fusion.86, bf16[512,12,64]{0,2,1:T(8,128)(2,1)} %bitcast.303, bf16[1024,12,64]{0,2,1:T(8,128)(2,1)S(1)} %bitcast.281), kind=kOutput, calls=%fused_computation.26 | convolution fusion | flops 843042816 | bytes 52741120 | tf_op jit(solution)/shard_map/qhd,khd->hqk/dot_general | solution.py:130
  131.2 18.9 %fusion = (f32[12,512]{1,0:T(8,128)S(1)}, f32[12,512]{1,0:T(8,128)S(1)}) fusion(f32[12,512]{1,0:T(8,128)S(1)} %get-tuple-element.41, f32[12,512,1024]{2,1,0:T(8,128)} %get-tuple-element.70, pred[1024]{0:T(1024)(128)(4,1)S(1)} %broadcast_in_dim.78, f32[12,512]{1,0:T(8,128)S(1)} %get-tuple-element.42, f32[12,512,1024]{2,1,0:T(8,128)} %fusion.86), kind=kLoop, calls=%fused_computation.12 | loop fusion | flops 50319360 | bytes 50430976 | tf_op jit(solution)/shard_map/reduce_sum | solution.py:136
  150.0 11.2 %fusion.54 = bf16[12,64,512]{2,1,0:T(8,128)(2,1)S(1)} fusion(bf16[1024,12,64]{0,2,1:T(8,128)(2,1)S(1)} %bitcast.286, f32[12,512]{1,0:T(8,128)S(1)} %get-tuple-element.39, f32[12,512]{1,0:T(8,128)S(1)} %get-tuple-element.41, f32[12,512,1024]{2,1,0:T(8,128)} %get-tuple-element.70, pred[1024]{0:T(1024)(128)(4,1)S(1)} %broadcast_in_dim.78), kind=kOutput, calls=%fused_computation.100 | convolution fusion | flops 837156864 | bytes 27575296 | tf_op jit(solution)/shard_map/hqk,khd->qhd/dot_general | solution.py:138
  161.3 12.2 %fusion.53 = bf16[12,64,512]{2,1,0:T(8,128)(2,1)S(1)} fusion(bf16[1024,12,64]{0,2,1:T(8,128)(2,1)S(1)} %bitcast.287, f32[12,512]{1,0:T(8,128)S(1)} %get-tuple-element.40, f32[12,512]{1,0:T(8,128)S(1)} %get-tuple-element.42, f32[12,512,1024]{2,1,0:T(8,128)} %fusion.86, pred[1024]{0:T(1024)(128)(4,1)S(1)} %broadcast_in_dim.78), kind=kOutput, calls=%fused_computation.99 | convolution fusion | flops 837156864 | bytes 27575296 | tf_op jit(solution)/shard_map/hqk,khd->qhd/dot_general | solution.py:138
  173.5 1.7 multiply_reduce_fusion.4
  175.2 1.6 copy-done.7
  177.2 7.3 %fusion.80 = (bf16[16,384,256]{2,1,0:T(8,128)(2,1)}, bf16[16,384,256]{2,1,0:T(8,128)(2,1)}, bf16[16,384,256]{2,1,0:T(8,128)(2,1)}) fusion(bf16[16,1152,256]{2,1,0:T(8,128)(2,1)} %bitcast.302), kind=kLoop, calls=%fused_computation.146 | loop fusion | bytes 18874368 | tf_op jit(solution)/shard_map/slice | solution.py:217
  184.5 4.9 copy.64
  189.4 3.2 copy.63
  194.5 1.3 copy.62
  196.9 5.7 fusion.88
  202.6 5.7 fusion.87
  208.4 15.7 %multiply_convert_fusion.2 = (bf16[1024,2048]{1,0:T(8,128)(2,1)}, bf16[1024,2048]{1,0:T(8,128)(2,1)}, bf16[1024,2048]{1,0:T(8,128)(2,1)}) fusion(f32[1024,2048]{1,0:T(8,128)} %fusion.87, f32[1024,2048]{1,0:T(8,128)} %fusion.88, bf16[96,8,16,128]{3,2,1,0:T(8,128)(2,1)S(1)} %bitcast.332, bf16[1,1,1024,768]{3,2,1,0:T(8,128)(2,1)S(1)} %copy-done.21, ...), kind=kOutput, calls=%fused_computation.36 | convolution fusion | flops 3278110720 | bytes 34079744 | tf_op jit(solution)/shard_map/dot_general | solution.py:37
  224.1 5.4 fusion.89
  229.5 4.5 multiply_reduce_fusion.2
  235.4 2.4 convolution_convert_fusion.7
  237.8 1.4 convolution_convert_fusion.3
  239.4 10.4 %fusion.90 = f32[12,512,1024]{2,1,0:T(8,128)} fusion(bf16[512,12,64]{0,2,1:T(8,128)(2,1)S(1)} %bitcast.305, bf16[1024,12,64]{0,2,1:T(8,128)(2,1)S(1)} %bitcast.288), kind=kOutput, calls=%fused_computation.156 | convolution fusion | flops 805306368 | bytes 27525120 | tf_op jit(solution)/shard_map/qhd,khd->hqk/dot_general | solution.py:164
  249.8 12.6 %fusion.5 = f32[12,64,1024]{2,1,0:T(8,128)} fusion(bf16[512,12,64]{0,2,1:T(8,128)(2,1)S(1)} %bitcast.306, f32[12,512]{1,0:T(8,128)S(1)} %get-tuple-element.76, f32[12,512,1024]{2,1,0:T(8,128)} %fusion.86, pred[1024]{0:T(1024)(128)(4,1)S(1)} %broadcast_in_dim.78), kind=kOutput, calls=%fused_computation.18 | convolution fusion | flops 830472192 | bytes 29123584 | tf_op jit(solution)/shard_map/hqk,qhd->khd/dot_general | solution.py:181
  262.3 35.3 %multiply_reduce_fusion.1 = (f32[12,512]{1,0:T(8,128)S(1)}, f32[12,512]{1,0:T(8,128)S(1)}, f32[12,512,1024]{2,1,0:T(8,128)}) fusion(f32[12,512]{1,0:T(8,128)S(1)} %get-tuple-element.77, f32[12,512,1024]{2,1,0:T(8,128)} %get-tuple-element.70, pred[1024]{0:T(1024)(128)(4,1)S(1)} %broadcast_in_dim.78, f32[12,512,1024]{2,1,0:T(8,128)} %fusion.90, ...), kind=kOutput, calls=%fused_computation.4 | convolution fusion | flops 868208640 | bytes 103121920 | tf_op jit(solution)/shard_map/qhd,khd->hqk/dot_general | solution.py:164
  297.7 42.0 %multiply_convert_fusion.1 = (bf16[12,512,1024]{2,1,0:T(8,128)(2,1)}, bf16[12,512,1024]{2,1,0:T(8,128)(2,1)}) fusion(f32[12,512,1024]{2,1,0:T(8,128)} %get-tuple-element.74, f32[12,512]{1,0:T(8,128)S(1)} %get-tuple-element.37, f32[12,512]{1,0:T(8,128)S(1)} %get-tuple-element.77, f32[12,512,1024]{2,1,0:T(8,128)} %get-tuple-element.70, ...), kind=kLoop, calls=%fused_computation.3 | loop fusion | flops 75497472 | bytes 125928448 | tf_op jit(solution)/shard_map/convert_element_type | solution.py:168
  339.7 9.6 %multiply_convert_fusion.7 = bf16[12,64,512]{2,1,0:T(8,128)(2,1)} fusion(bf16[1024,12,64]{0,2,1:T(8,128)(2,1)S(1)} %bitcast.283, bf16[12,512,1024]{2,1,0:T(8,128)(2,1)} %get-tuple-element.68), kind=kOutput, calls=%fused_computation.90 | convolution fusion | flops 806092800 | bytes 14942208 | tf_op jit(solution)/shard_map/hqk,khd->qhd/dot_general | solution.py:170
  349.3 8.9 %fusion.91 = f32[12,64,1024]{2,1,0:T(8,128)} fusion(bf16[512,12,64]{0,2,1:T(8,128)(2,1)} %bitcast.304, bf16[12,512,1024]{2,1,0:T(8,128)(2,1)} %get-tuple-element.68), kind=kOutput, calls=%fused_computation.157 | convolution fusion | flops 805306368 | bytes 16515072 | tf_op jit(solution)/shard_map/hqk,qhd->khd/dot_general | solution.py:176
  358.1 6.2 multiply_convert_fusion.6
  364.4 4.5 multiply_convert_fusion.4
  368.9 2.5 convolution_convert_fusion.9
  371.4 3.3 fusion.92
  375.8 12.3 %add_convert_fusion = bf16[12,64,1024]{2,1,0:T(8,128)(2,1)S(1)} fusion(f32[12,64,1024]{2,1,0:T(8,128)} %fusion.5, bf16[512,12,64]{0,2,1:T(8,128)(2,1)S(1)} %bitcast.330, f32[12,512]{1,0:T(8,128)} %copy-done.41, f32[12,512,1024]{2,1,0:T(8,128)} %get-tuple-element.70, pred[1024]{0:T(1024)(128)(4,1)S(1)} %broadcast_in_dim.78), kind=kOutput, calls=%fused_computation.71 | convolution fusion | flops 832045056 | bytes 30696448 | tf_op jit(solution)/shard_map/hqk,qhd->khd/dot_general | solution.py:181
  389.3 2.4 convolution_convert_fusion.8
  391.8 2.3 reshape.414
  395.3 2.4 reshape.412
  399.0 3.1 fusion.57
  402.8 2.2 fusion.36
  405.0 2.2 fusion.35
  407.2 2.4 convolution_convert_fusion.10
  409.8 2.6 reshape.410
  417.9 5.9 convolution_convert_fusion.2
  424.9 2.5 copy.70
  428.4 3.7 convolution_convert_fusion.1
  433.2 2.5 copy.71
  435.7 1.6 copy-done.60
  437.3 5.1 convolution_convert_fusion
  442.3 3.2 copy.72
  445.5 2.6 copy.94
  448.2 5.5 copy.73
  453.8 6.8 %fusion.15 = bf16[16,1168,256]{2,1,0:T(8,128)(2,1)} fusion(bf16[16,1,48]{2,1,0:T(2,128)(2,1)S(1)} %convert_element_type.247, bf16[16,384,256]{2,1,0:T(8,128)(2,1)} %bitcast.301, bf16[16,384,256]{2,1,0:T(8,128)(2,1)} %bitcast.300, bf16[16,384,256]{2,1,0:T(8,128)(2,1)S(1)} %bitcast.299), kind=kLoop, calls=%fused_computation.28 | loop fusion | flops 47841280 | bytes 19006976 | tf_op jit(solution)/shard_map/concatenate | solution.py:238
  460.7 6.5 all-to-all-start.1
  467.2 48.7 %reduce-scatter.3.cloned.1.call-done = bf16[592,256]{1,0:T(8,128)(2,1)} async-done(((bf16[9472,256]{1,0:T(8,128)(2,1)}), bf16[592,256]{1,0:T(8,128)(2,1)}) %reduce-scatter.3.cloned.1.call-update) | async-done | bytes 303120 | tf_op jit(solution)/shard_map/reduce_scatter | solution.py:240
  515.9 1.5 collective-permute-start
  517.4 7.8 %fusion.45 = bf16[1,1,1024,768]{3,2,1,0:T(8,128)(2,1)} fusion(f32[1024,768]{1,0:T(8,128)S(1)} %copy-done.9, pred[1024]{0:T(1024)(128)(4,1)S(1)} %broadcast_in_dim.78, bf16[1024,2048]{1,0:T(8,128)(2,1)} %get-tuple-element.45, bf16[96,8,16,128]{3,2,1,0:T(8,128)(2,1)} %bitcast.331), kind=kOutput, calls=%fused_computation.85 | convolution fusion | flops 3223584768 | bytes 12059648 | tf_op jit(solution)/shard_map/dot_general | solution.py:43
  525.2 4.3 undeal_rows.1
  529.4 103.1 %reduce-scatter.5.cloned.1.call-done = bf16[1168,256]{1,0:T(8,128)(2,1)} async-done(((bf16[18688,256]{1,0:T(8,128)(2,1)}), bf16[1168,256]{1,0:T(8,128)(2,1)}) %reduce-scatter.5.cloned.1.call-update) | async-done | bytes 598032 | tf_op jit(solution)/shard_map/reduce_scatter | solution.py:240
  632.6 1.5 collective-permute-start.1
  638.8 8.9 %collective-permute-done.1 = bf16[1168,256]{1,0:T(8,128)(2,1)S(1)} collective-permute-done((bf16[1168,256]{1,0:T(8,128)(2,1)}, bf16[1168,256]{1,0:T(8,128)(2,1)S(1)}, u32[]{:S(2)}, u32[]{:S(2)}) %collective-permute-start.1) | collective-permute-done | bytes 598048 | tf_op jit(solution)/shard_map/ppermute | solution.py:226
  (215 shorter events, 43.4 us)
Async XLA Ops:
  7.2 80.9 %all-gather.3.cloned.1.call-start = ((), (), s32[]{:S(2)}) async-start(), calls=%async_computation.4 | async-start | bytes 5013504 | tf_op jit(solution)/shard_map/all_gather | solution.py:211
  11.0 15.0 %copy-start.42 = (bf16[48,2048]{1,0:T(8,128)(2,1)S(1)}, bf16[48,2048]{1,0:T(8,128)(2,1)}, u32[]{:S(2)}) copy-start(bf16[48,2048]{1,0:T(8,128)(2,1)} %param.22) | copy-start | bytes 589828
  11.8 14.4 %copy-start.43 = (bf16[48,2048]{1,0:T(8,128)(2,1)S(1)}, bf16[48,2048]{1,0:T(8,128)(2,1)}, u32[]{:S(2)}) copy-start(bf16[48,2048]{1,0:T(8,128)(2,1)} %param.23) | copy-start | bytes 589828
  18.4 7.9 %copy-start.44 = (bf16[128,768]{1,0:T(8,128)(2,1)S(1)}, bf16[128,768]{1,0:T(8,128)(2,1)}, u32[]{:S(2)}) copy-start(bf16[128,768]{1,0:T(8,128)(2,1)} %param.24) | copy-start | bytes 589828
  18.4 58.4 %all-to-all-start = ((bf16[16,64,768]{2,1,0:T(8,128)(2,1)}), bf16[16,64,768]{2,1,0:T(8,128)(2,1)S(1)}, u32[]{:S(2)}, u32[]{:S(2)}) async-start(bf16[16,64,768]{2,1,0:T(8,128)(2,1)} %deal_rows.1), calls=%async_computation | async-start | bytes 3145728 | tf_op jit(solution)/shard_map/all_to_all | solution.py:278
  26.0 2.3 copy-start.52
  26.0 151.2 %all-gather.5.cloned.1.call-start = ((), (), s32[]{:S(2)}) async-start(), calls=%async_computation.5 | async-start | bytes 10027008 | tf_op jit(solution)/shard_map/all_gather | solution.py:211
  26.1 51.8 %copy-start.45 = (f32[768]{0:T(1024)S(1)}, f32[768]{0:T(1024)}, u32[]{:S(2)}) copy-start(f32[768]{0:T(1024)} %param.16) | copy-start | bytes 9220
  27.5 488.4 %reduce-scatter.3.cloned.1.call-start = ((), (), s32[]{:S(2)}) async-start(), calls=%async_computation.6 | async-start | bytes 5152768 | tf_op jit(solution)/shard_map/reduce_scatter | solution.py:240
  76.8 96.7 %copy-start = (bf16[16,64,768]{2,1,0:T(8,128)(2,1)}, bf16[16,64,768]{2,1,0:T(8,128)(2,1)S(1)}, u32[]{:S(2)}) copy-start(bf16[16,64,768]{2,1,0:T(8,128)(2,1)S(1)} %all-to-all-done) | copy-start | bytes 4718596
  78.3 17.9 %copy-start.25 = (bf16[16,64,768]{2,1,0:T(8,128)(2,1)}, bf16[16,64,768]{2,1,0:T(8,128)(2,1)S(1)}, u32[]{:S(2)}) copy-start(bf16[16,64,768]{2,1,0:T(8,128)(2,1)S(1)} %fusion.39) | copy-start | bytes 4718596
  94.0 4.7 copy-start.32
  96.2 4.8 copy-start.13
  97.7 1.8 copy-start.26
  98.7 4.9 copy-start.4
  100.9 13.0 %copy-start.2 = (bf16[1024,768]{0,1:T(8,128)(2,1)}, bf16[1024,768]{0,1:T(8,128)(2,1)S(1)}, u32[]{:S(2)}) copy-start(bf16[1024,768]{0,1:T(8,128)(2,1)S(1)} %convolution_convert_fusion.4) | copy-start | bytes 4718596
  131.2 18.9 %copy-start.5 = (bf16[1024,768]{0,1:T(8,128)(2,1)S(1)}, bf16[1024,768]{0,1:T(8,128)(2,1)}, u32[]{:S(2)}) copy-start(bf16[1024,768]{0,1:T(8,128)(2,1)} %convolution_convert_fusion.6) | copy-start | bytes 4718596
  161.3 12.2 %copy-start.54 = (bf16[12,64,512]{2,1,0:T(8,128)(2,1)}, bf16[12,64,512]{2,1,0:T(8,128)(2,1)S(1)}, u32[]{:S(2)}) copy-start(bf16[12,64,512]{2,1,0:T(8,128)(2,1)S(1)} %fusion.54) | copy-start | bytes 2359300
  161.3 12.2 %copy-start.34 = (bf16[96,8,3,256]{3,1,2,0:T(8,128)(2,1)S(1)}, bf16[96,8,3,256]{3,1,2,0:T(8,128)(2,1)}, u32[]{:S(2)}) copy-start(bf16[96,8,3,256]{3,1,2,0:T(8,128)(2,1)} %copy.86) | copy-start | bytes 3538948
  173.5 1.7 copy-start.56
  173.5 3.3 copy-start.50
  175.2 1.6 copy-start.7
  175.2 122.4 %copy-start.41 = (f32[12,512]{1,0:T(8,128)}, f32[12,512]{1,0:T(8,128)S(1)}, u32[]{:S(2)}) copy-start(f32[12,512]{1,0:T(8,128)S(1)} %get-tuple-element.77) | copy-start | bytes 73732
  177.1 25.5 %copy-start.29 = (bf16[1024,768]{1,0:T(8,128)(2,1)}, bf16[1024,768]{1,0:T(8,128)(2,1)S(1)}, u32[]{:S(2)}) copy-start(bf16[1024,768]{1,0:T(8,128)(2,1)S(1)} %multiply_convert_fusion.5) | copy-start | bytes 4718596
  192.6 1.9 copy-start.6
  202.6 5.8 copy-start.19
  202.6 5.8 copy-start.21
  224.1 5.4 copy-start.8
  224.1 5.5 copy-start.58
  235.4 2.4 copy-start.10
  235.4 2.4 copy-start.35
  239.4 23.0 %copy-start.17 = (bf16[512,768]{0,1:T(8,128)(2,1)}, bf16[512,768]{0,1:T(8,128)(2,1)S(1)}, u32[]{:S(2)}) copy-start(bf16[512,768]{0,1:T(8,128)(2,1)S(1)} %get-tuple-element.55) | copy-start | bytes 2359300
  297.7 42.0 %copy-start.3 = (bf16[1024,768]{0,1:T(8,128)(2,1)S(1)}, bf16[1024,768]{0,1:T(8,128)(2,1)}, u32[]{:S(2)}) copy-start(bf16[1024,768]{0,1:T(8,128)(2,1)} %copy-done.2) | copy-start | bytes 4718596
  339.7 18.5 %slice-start = ((s8[12582912]{0:T(1024)(128)(4,1)}), s8[4194304]{0:T(1024)(128)(4,1)S(1)}, s32[]{:S(2)}) async-start(s8[12582912]{0:T(1024)(128)(4,1)} %bitcast.277), calls=%async_computation.8 | async-start | bytes 8388608
  339.7 18.5 %slice-start.1 = ((s8[12582912]{0:T(1024)(128)(4,1)}), s8[4194304]{0:T(1024)(128)(4,1)S(1)}, s32[]{:S(2)}) async-start(s8[12582912]{0:T(1024)(128)(4,1)} %bitcast.277), calls=%async_computation.9 | async-start | bytes 8388608
  349.3 8.9 %slice-start.2 = ((s8[12582912]{0:T(1024)(128)(4,1)}), s8[4194304]{0:T(1024)(128)(4,1)S(1)}, s32[]{:S(2)}) async-start(s8[12582912]{0:T(1024)(128)(4,1)} %bitcast.277), calls=%async_computation.10 | async-start | bytes 8388608
  364.4 4.6 copy-start.27
  368.9 2.5 copy-start.33
  371.4 3.3 copy-start.36
  375.8 13.5 %copy-start.28 = (bf16[16,64,768]{2,1,0:T(8,128)(2,1)S(1)}, bf16[16,64,768]{2,1,0:T(8,128)(2,1)}, u32[]{:S(2)}) copy-start(bf16[16,64,768]{2,1,0:T(8,128)(2,1)} %copy-done.25) | copy-start | bytes 4718596
  395.3 3.7 copy-start.37
  399.0 3.2 copy-start.1
  399.0 3.2 copy-start.14
  399.0 3.3 copy-start.20
  399.0 3.7 copy-start.24
  399.0 3.7 copy-start.46
  399.0 3.7 copy-start.47
  402.8 2.2 copy-start.49
  402.8 2.3 copy-start.11
  405.0 2.2 copy-start.38
  412.3 2.5 copy-start.15
  416.0 1.9 copy-start.30
  417.8 214.7 %reduce-scatter.5.cloned.1.call-start = ((), (), s32[]{:S(2)}) async-start(), calls=%async_computation.7 | async-start | bytes 10166272 | tf_op jit(solution)/shard_map/reduce_scatter | solution.py:240
  424.9 3.5 copy-start.59
  433.1 2.5 copy-start.22
  433.2 4.1 copy-start.60
  448.2 5.5 copy-start.51
  448.2 5.6 copy-start.12
  460.7 56.7 %copy-start.9 = (f32[1024,768]{1,0:T(8,128)S(1)}, f32[1024,768]{1,0:T(8,128)}, u32[]{:S(2)}) copy-start(f32[1024,768]{1,0:T(8,128)} %copy-done.7) | copy-start | bytes 9437188
  460.7 64.5 %all-to-all-start.1 = ((bf16[16,64,768]{2,1,0:T(8,128)(2,1)}), bf16[16,64,768]{2,1,0:T(8,128)(2,1)}, u32[]{:S(2)}, u32[]{:S(2)}) async-start(bf16[16,64,768]{2,1,0:T(8,128)(2,1)} %bitcast.315), calls=%async_computation.1 | async-start | bytes 3145728 | tf_op jit(solution)/shard_map/all_to_all | solution.py:335
  515.9 118.2 %copy-start.40 = (bf16[592,256]{1,0:T(8,128)(2,1)S(1)}, bf16[592,256]{1,0:T(8,128)(2,1)}, u32[]{:S(2)}) copy-start(bf16[592,256]{1,0:T(8,128)(2,1)} %reduce-scatter.3.cloned.1.call-done) | copy-start | bytes 909316
  515.9 118.2 %collective-permute-start = (bf16[592,256]{1,0:T(8,128)(2,1)}, bf16[592,256]{1,0:T(8,128)(2,1)}, u32[]{:S(2)}, u32[]{:S(2)}) collective-permute-start(bf16[592,256]{1,0:T(8,128)(2,1)} %reduce-scatter.3.cloned.1.call-done), channel_id=1, source_target_pairs={{0,1},{1,0},{2,3},{3,2},{4,5},{5,4},{6,7},{7,6},{8,9},{9,8},{10,11... | collective-permute-start | bytes 909320 | tf_op jit(solution)/shard_map/ppermute | solution.py:226
  632.6 15.2 %copy-start.39 = (bf16[1168,256]{1,0:T(8,128)(2,1)S(1)}, bf16[1168,256]{1,0:T(8,128)(2,1)}, u32[]{:S(2)}) copy-start(bf16[1168,256]{1,0:T(8,128)(2,1)} %reduce-scatter.5.cloned.1.call-done) | copy-start | bytes 1794052
  632.6 15.2 %collective-permute-start.1 = (bf16[1168,256]{1,0:T(8,128)(2,1)}, bf16[1168,256]{1,0:T(8,128)(2,1)S(1)}, u32[]{:S(2)}, u32[]{:S(2)}) collective-permute-start(bf16[1168,256]{1,0:T(8,128)(2,1)} %reduce-scatter.5.cloned.1.call-done), channel_id=1, source_target_pairs={{0,1},{1,0},{2,3},{3,2},{4,5},{5,4},{6,7},{7,6},{8,9},{9,8},{10,11... | collective-permute-start | bytes 1794056 | tf_op jit(solution)/shard_map/ppermute | solution.py:226
  (8 other events, 9.8 us)
Sparse Core Ops, SparseCore 0:
  11.9 76.1 all-gather.2
  90.4 81.3 all-gather.4
  418.0 97.8 reduce-scatter.2
  519.9 112.6 reduce-scatter.4

commit v2 on v1

v2 whole, which is shorter than its diff:
```python
import functools

import jax
import jax.numpy as jnp
from jax import lax
from jax.experimental import pallas as pl
from jax.experimental.pallas import tpu as pltpu
from jax.sharding import PartitionSpec as P

H = 12
HD = 64
LANES = 256
GAIN_ROWS = 16

norm_eps = 1e-06
neg_big = -1e30
bf16 = jnp.bfloat16
f32 = jnp.float32


def left_dot(lhs_mat, rhs_mat):
    return lax.dot_general(
        lhs_mat, rhs_mat, (((0,), (0,)), ((), ())), preferred_element_type=jnp.float32
    )


def right_dot(lhs_mat, rhs_mat):
    return lax.dot_general(
        lhs_mat, rhs_mat, (((1,), (1,)), ((), ())), preferred_element_type=jnp.float32
    )


def plain_dot(lhs_mat, rhs_mat):
    return jnp.dot(lhs_mat, rhs_mat, preferred_element_type=jnp.float32)


def slot_start(units_ref, order_ref, slot, shard_count):
    wanted = order_ref[0, slot]
    start = jnp.int32(0)
    count = jnp.int32(0)
    for k in range(shard_count):
        units = units_ref[0, k]
        start = start + jnp.where(k < wanted, units, 0)
        count = count + jnp.where(k == wanted, units, 0)
    return start, count


def deal_kernel(units_ref, order_ref, rows_ref, out_ref):
    shard_count, unit_max, _ = out_ref.shape
    given = rows_ref.shape[0]
    row = lax.broadcasted_iota(jnp.int32, (unit_max, given), 0)
    col = lax.broadcasted_iota(jnp.int32, (unit_max, given), 1)

    def step(slot, carry):
        start, count = slot_start(units_ref, order_ref, slot, shard_count)
        pick = jnp.where((col - start == row) & (row < count), 1.0, 0.0).astype(bf16)
        out_ref[slot] = plain_dot(pick, rows_ref[...]).astype(bf16)
        return carry

    lax.fori_loop(0, shard_count, step, 0)


def undeal_kernel(units_ref, order_ref, back_ref, out_ref, pick_ref):
    shard_count, unit_max, width = back_ref.shape
    given = out_ref.shape[0]
    row = lax.broadcasted_iota(jnp.int32, (unit_max, given), 0)
    col = lax.broadcasted_iota(jnp.int32, (unit_max, given), 1)

    def step(slot, carry):
        start, count = slot_start(units_ref, order_ref, slot, shard_count)
        pick = jnp.where((col - start == row) & (row < count), 1.0, 0.0).astype(bf16)
        pick_ref[pl.ds(pl.multiple_of(slot * unit_max, unit_max), unit_max), :] = pick
        return carry

    lax.fori_loop(0, shard_count, step, 0)
    whole = back_ref[...].reshape(shard_count * unit_max, width)
    out_ref[...] = left_dot(pick_ref[...], whole).astype(bf16)


def smem():
    return pl.BlockSpec(memory_space=pltpu.SMEM)


def vmem():
    return pl.BlockSpec(memory_space=pltpu.VMEM)


def deal_rows(units, order, rows, shard_count, unit_max):
    return pl.pallas_call(
        deal_kernel,
        out_shape=jax.ShapeDtypeStruct((shard_count, unit_max, rows.shape[1]), bf16),
        in_specs=[smem(), smem(), vmem()],
        out_specs=vmem(),
        name="deal_rows",
    )(units, order, rows)


def undeal_rows(units, order, back, given):
    shard_count, unit_max, width = back.shape
    return pl.pallas_call(
        undeal_kernel,
        out_shape=jax.ShapeDtypeStruct((given, width), bf16),
        in_specs=[smem(), smem(), vmem()],
        out_specs=vmem(),
        scratch_shapes=[pltpu.VMEM((shard_count * unit_max, given), bf16)],
        name="undeal_rows",
    )(units, order, back)


def const_block(shape):
    zeros = (0,) * len(shape)
    return pl.BlockSpec(shape, lambda *_: zeros)


def params():
    return pltpu.CompilerParams(vmem_limit_bytes=60 << 20)


def cost(flops, moved, trans=0):
    return pl.CostEstimate(flops=flops, bytes_accessed=moved, transcendentals=trans)


def inverse_rms(rows):
    return lax.rsqrt(jnp.mean(rows * rows, axis=-1, keepdims=True) + norm_eps)


def whole_block(ref):
    parts, rows, lanes = ref.shape
    return ref[...].reshape(parts * rows, lanes)


def qkv_kernel(x_ref, gain_ref, w_ref, n1_ref, qkv_ref):
    block = pl.program_id(0)

    @pl.when(block == 0)
    def _():
        rows = x_ref[...].astype(f32)
        n1_ref[...] = (rows * inverse_rms(rows) * gain_ref[...]).astype(bf16)

    factor = jnp.where(block < n1_ref.shape[1] // LANES, HD ** (-0.5), 1.0)
    made = plain_dot(n1_ref[...], whole_block(w_ref)).astype(bf16).astype(f32)
    qkv_ref[...] = (made * factor).astype(bf16)


def make_qkv(tokens, gain, packed, rows):
    span, width = tokens.shape
    parts = packed.shape[0]
    blocks = 3 * width // LANES
    return pl.pallas_call(
        qkv_kernel,
        grid=(blocks,),
        out_shape=(
            jax.ShapeDtypeStruct((span, width), bf16),
            jax.ShapeDtypeStruct((span, 3 * width), bf16),
        ),
        in_specs=[
            const_block((span, width)),
            const_block((1, width)),
            pl.BlockSpec((parts, rows, LANES), lambda j: (0, j, 0)),
        ],
        out_specs=(
            const_block((span, width)),
            pl.BlockSpec((span, LANES), lambda j: (0, j)),
        ),
        compiler_params=params(),
        cost_estimate=cost(6 * span * width * width, 14 << 20),
        name="make_qkv",
    )(tokens, gain, packed)


def live_bias(count, span, unit_max):
    row = lax.broadcasted_iota(jnp.int32, (span, 2 * HD), 0)
    return jnp.where(lax.rem(row, unit_max) < count, 0.0, neg_big).astype(bf16)


def head_keys(keys, bias, lane, head):
    inside = (lane // HD) == head
    return jnp.where(inside, keys, jnp.where(lane == (1 - head) * HD, bias, jnp.zeros_like(keys)))


def head_queries(queries, lane, head):
    inside = (lane // HD) == head
    one = jnp.where(lane == (1 - head) * HD, 1.0, 0.0).astype(bf16)
    return jnp.where(inside, queries, one)


def attend_kernel(unit_max, chunk, count_ref, q_ref, k_ref, v_ref, o_ref, lse_ref, kb_ref, vt_ref):
    span = q_ref.shape[0]
    pair = 2 * HD
    lane = lax.broadcasted_iota(jnp.int32, (span, pair), 1)
    bias = live_bias(count_ref[0], span, unit_max)
    keys = k_ref[...]
    values_t = v_ref[...].T
    for head in range(2):
        kb_ref[head] = head_keys(keys, bias, lane, head)
        vt_ref[head, :HD] = values_t[head * HD : (head + 1) * HD]
        vt_ref[head, HD:] = jnp.ones((vt_ref.shape[1] - HD, span), bf16)
    lane_c = lane[:chunk]
    for begin in range(0, span, chunk):
        queries = q_ref[begin : begin + chunk, :]
        mixed = []
        for head in range(2):
            scores = right_dot(kb_ref[head], head_queries(queries, lane_c, head))
            top = jnp.max(scores, axis=0, keepdims=True)
            probs = jnp.exp(scores - top).astype(bf16)
            both = plain_dot(vt_ref[head], probs)
            total = both[HD : HD + 1]
            mixed.append(both[:HD] * (1.0 / total))
            lse_ref[0, head : head + 1, begin : begin + chunk] = top + jnp.log(total)
        o_ref[begin : begin + chunk, :] = jnp.concatenate(mixed, axis=0).T.astype(bf16)


def attend_forward(count, qkv, unit_max):
    span = qkv.shape[0]
    width = qkv.shape[1] // 3
    pair = 2 * HD
    pairs = width // pair

    def block(first):
        return pl.BlockSpec((span, pair), lambda p: (0, first + p))

    return pl.pallas_call(
        functools.partial(attend_kernel, unit_max, 512),
        grid=(pairs,),
        out_shape=(
            jax.ShapeDtypeStruct((span, width), bf16),
            jax.ShapeDtypeStruct((pairs, 8, span), f32),
        ),
        in_specs=[smem(), block(0), block(pairs), block(2 * pairs)],
        out_specs=(block(0), pl.BlockSpec((1, 8, span), lambda p: (p, 0, 0))),
        scratch_shapes=[
            pltpu.VMEM((2, span, pair), bf16),
            pltpu.VMEM((2, HD + 16, span), bf16),
        ],
        compiler_params=params(),
        cost_estimate=cost(4 * span * span * width, 8 << 20, span * span * H),
        name="attend_forward",
    )(count, qkv, qkv, qkv)


def out_kernel(x_ref, o_ref, w_ref, gain_ref, h_ref, n2_ref):
    parts, total, lanes = w_ref.shape
    width = h_ref.shape[1]
    rows = width // parts
    for c in range(width // lanes):
        weight = w_ref[:, c * rows : (c + 1) * rows, :].reshape(width, lanes)
        cols = slice(c * lanes, (c + 1) * lanes)
        h_ref[:, cols] = x_ref[:, cols].astype(f32) + plain_dot(o_ref[...], weight)
    hidden = h_ref[...]
    n2_ref[...] = (hidden * inverse_rms(hidden) * gain_ref[...]).astype(bf16)


def out_project(tokens, mixed, packed, gain, rows):
    span, width = tokens.shape
    parts = packed.shape[0]
    blocks = width // LANES
    return pl.pallas_call(
        out_kernel,
        grid=(1,),
        out_shape=(
            jax.ShapeDtypeStruct((span, width), f32),
            jax.ShapeDtypeStruct((span, width), bf16),
        ),
        in_specs=[
            const_block((span, width)),
            const_block((span, width)),
            pl.BlockSpec((parts, blocks * rows, LANES), lambda i: (0, 3, 0)),
            const_block((1, width)),
        ],
        out_specs=(const_block((span, width)), const_block((span, width))),
        compiler_params=params(),
        cost_estimate=cost(2 * span * width * width, 9 << 20),
        name="out_project",
    )(tokens, mixed, packed, gain)


def spread_gain(total, parts):
    width = total.shape[1]
    own = width // parts
    shape = (parts, GAIN_ROWS, LANES)
    part = lax.broadcasted_iota(jnp.int32, shape, 0)
    row = lax.broadcasted_iota(jnp.int32, shape, 1)
    place = row * LANES + lax.broadcasted_iota(jnp.int32, shape, 2)
    mine = (place >= part * own) & (place < (part + 1) * own)
    out = jnp.zeros(shape, f32)
    for c in range(width // LANES):
        piece = jnp.broadcast_to(total[:, c * LANES : (c + 1) * LANES][None], shape)
        out = jnp.where((row == c) & mine, piece, out)
    return out.astype(bf16)


def ffn_kernel(
    unit_max,
    count_ref,
    h_ref,
    n2_ref,
    d_ref,
    gain_ref,
    wg_ref,
    wu_ref,
    wd_ref,
    out_ref,
    gh_ref,
    ghb_ref,
    pack_ref,
    gb_ref,
    y_ref,
    gn_ref,
    stage_gate,
    stage_up,
    stage_down,
    stage_gain,
    sems,
):
    step = pl.program_id(0)
    steps = pl.num_programs(0)
    slot = lax.rem(step, 2)
    span, width = h_ref.shape
    parts, rows, _ = wg_ref.shape
    few, down_all, _ = wd_ref.shape
    cols = width // LANES
    down = down_all // cols
    ff_blocks = steps

    def copies(which, at):
        return (
            pltpu.make_async_copy(
                stage_gate.at[at],
                pack_ref.at[:, pl.ds(pl.multiple_of(which * rows, 8), rows), :],
                sems.at[0, at],
            ),
            pltpu.make_async_copy(
                stage_up.at[at],
                pack_ref.at[:, pl.ds(pl.multiple_of((ff_blocks + which) * rows, 8), rows), :],
                sems.at[1, at],
            ),
            pltpu.make_async_copy(
                stage_down.at[at],
                pack_ref.at[pl.ds(which * few, few), pl.ds(2 * ff_blocks * rows, down_all), :],
                sems.at[2, at],
            ),
        )

    row = lax.broadcasted_iota(jnp.int32, (span, 1), 0)
    live = lax.rem(row, unit_max) < count_ref[0]

    @pl.when(step == 0)
    def _():
        gb_ref[...] = jnp.where(live, d_ref[...].astype(f32), 0.0).astype(bf16)

    @pl.when(step >= 2)
    def _():
        for copy in copies(step - 2, slot):
            copy.wait()

    n2 = n2_ref[...]
    gb = gb_ref[...]
    w_gate = whole_block(wg_ref)
    w_up = whole_block(wu_ref)
    gate = plain_dot(n2, w_gate)
    up = plain_dot(n2, w_up)
    downs = [
        wd_ref[:, c * down : (c + 1) * down, :].reshape(few * down, LANES) for c in range(cols)
    ]
    g_act = right_dot(gb[:, :LANES], downs[0])
    for c in range(1, cols):
        g_act += right_dot(gb[:, c * LANES : (c + 1) * LANES], downs[c])
    c0 = 0.7978845608028654
    c1 = 0.044715
    square = gate * gate
    tang = jnp.tanh(c0 * gate * (1.0 + c1 * square))
    half = 0.5 * (1.0 + tang)
    gelu = gate * half
    slope = half + (0.5 * c0) * gate * (1.0 - tang * tang) * (1.0 + (3.0 * c1) * square)
    act = (gelu * up).astype(bf16)
    g_gate = (g_act * up * slope).astype(bf16)
    g_up = (g_act * gelu).astype(bf16)
    for c in range(cols):
        place = slice(c * LANES, (c + 1) * LANES)
        add = plain_dot(act, downs[c])
        grad = right_dot(g_gate, w_gate[place]) + right_dot(g_up, w_up[place])
        wide = left_dot(act, gb[:, place]).astype(bf16).reshape(few, down, LANES)
        stage_down[slot, :, c * down : (c + 1) * down, :] = wide

        @pl.when(step == 0)
        def _():
            y_ref[:, place] = add
            gn_ref[:, place] = grad

        @pl.when(step > 0)
        def _():
            y_ref[:, place] += add
            gn_ref[:, place] += grad

    stage_gate[slot] = left_dot(n2, g_gate).astype(bf16).reshape(parts, rows, LANES)
    stage_up[slot] = left_dot(n2, g_up).astype(bf16).reshape(parts, rows, LANES)
    for copy in copies(step, slot):
        copy.start()

    @pl.when(step == steps - 1)
    def _():
        hidden = h_ref[...]
        out_ref[...] = jnp.where(live, hidden + y_ref[...], 0.0).astype(bf16)
        inv = inverse_rms(hidden)
        grad = gn_ref[...]
        scaled = hidden * inv
        total = jnp.sum(grad * scaled, axis=0, keepdims=True)
        stage_gain[...] = spread_gain(total, parts)
        last = pltpu.make_async_copy(
            stage_gain,
            pack_ref.at[:, pl.ds(2 * ff_blocks * rows + down_all, GAIN_ROWS), :],
            sems.at[3, 0],
        )
        last.start()
        weighted = grad * gain_ref[...]
        mean = jnp.mean(scaled * weighted, axis=-1, keepdims=True)
        g_h = gb_ref[...].astype(f32) + inv * (weighted - scaled * mean)
        gh_ref[...] = g_h
        ghb_ref[...] = g_h.astype(bf16)
        for copy in copies(step - 1, 1 - slot) + copies(step, slot):
            copy.wait()
        last.wait()


def ffn_both(count, hidden, normed, d_rows, gain, packed, unit_max, rows, down):
    span, width = hidden.shape
    parts = packed.shape[0]
    ff = parts * down
    blocks = ff // LANES
    cols = width // LANES
    few = LANES // down
    moved = 2 * blocks * rows + cols * down
    full = const_block((span, width))
    return pl.pallas_call(
        functools.partial(ffn_kernel, unit_max),
        grid=(blocks,),
        out_shape=(
            jax.ShapeDtypeStruct((span, width), bf16),
            jax.ShapeDtypeStruct((span, width), f32),
            jax.ShapeDtypeStruct((span, width), bf16),
            jax.ShapeDtypeStruct((parts, moved + GAIN_ROWS, LANES), bf16),
        ),
        in_specs=[
            smem(),
            full,
            full,
            full,
            const_block((1, width)),
            pl.BlockSpec((parts, rows, LANES), lambda j: (0, j, 0)),
            pl.BlockSpec((parts, rows, LANES), lambda j: (0, blocks + j, 0)),
            pl.BlockSpec((few, cols * down, LANES), lambda j: (j, 2 * blocks * rows // (cols * down), 0)),
        ],
        out_specs=(full, full, full, pl.BlockSpec(memory_space=pl.ANY)),
        scratch_shapes=[
            pltpu.VMEM((span, width), bf16),
            pltpu.VMEM((span, width), f32),
            pltpu.VMEM((span, width), f32),
            pltpu.VMEM((2, parts, rows, LANES), bf16),
            pltpu.VMEM((2, parts, rows, LANES), bf16),
            pltpu.VMEM((2, few, cols * down, LANES), bf16),
            pltpu.VMEM((parts, GAIN_ROWS, LANES), bf16),
            pltpu.SemaphoreType.DMA((4, 2)),
        ],
        compiler_params=params(),
        cost_estimate=cost(18 * span * width * ff, 36 << 20, span * ff),
        name="ffn_both",
    )(count, hidden, normed, d_rows, gain, packed, packed, packed)


def attend_back_kernel(
    unit_max,
    chunk,
    count_ref,
    q_ref,
    k_ref,
    v_ref,
    o_ref,
    lse_ref,
    n1_ref,
    x_ref,
    gh_ref,
    ghb_ref,
    gain_ref,
    wq_ref,
    wk_ref,
    wv_ref,
    wo_ref,
    gx_ref,
    pack_ref,
    wo_s,
    do_s,
    delta_s,
    kt_s,
    dqt_s,
    dk_s,
    dv_s,
    gn_s,
    stage,
    stage_gain,
    sems,
    gain_sem,
):
    step = pl.program_id(0)
    steps = pl.num_programs(0)
    span, width = x_ref.shape
    parts, rows, _ = wq_ref.shape
    cols = width // LANES
    pair = 2 * HD
    heads = LANES // HD
    lane = lax.broadcasted_iota(jnp.int32, (span, pair), 1)
    lane_c = lane[:chunk]
    mine = pl.ds(pl.multiple_of(step * LANES, LANES), LANES)

    def copies(which):
        return [
            pltpu.make_async_copy(
                stage.at[m],
                pack_ref.at[:, pl.ds(pl.multiple_of((m * cols + which) * rows, 8), rows), :],
                sems.at[m],
            )
            for m in range(4)
        ]

    @pl.when(step == 0)
    def _():
        for c in range(cols):
            wo_s[c] = wo_ref[:, c * rows : (c + 1) * rows, :].reshape(width, LANES)

    g_o = right_dot(ghb_ref[:, :LANES], wo_s[0, mine, :])
    for c in range(1, cols):
        g_o += right_dot(ghb_ref[:, c * LANES : (c + 1) * LANES], wo_s[c, mine, :])
    g_o = g_o.astype(bf16)
    do_s[...] = g_o
    prod = g_o.astype(f32) * o_ref[:, mine].astype(f32)
    high = prod.astype(bf16)
    low = (prod - high.astype(f32)).astype(bf16)
    picker = jnp.where(
        lax.broadcasted_iota(jnp.int32, (8, LANES), 1) // HD
        == lax.broadcasted_iota(jnp.int32, (8, LANES), 0),
        1.0,
        0.0,
    ).astype(bf16)
    delta_s[...] = right_dot(picker, high) + right_dot(picker, low)
    kt_s[...] = k_ref[...].T
    dk_s[...] = jnp.zeros_like(dk_s)
    dv_s[...] = jnp.zeros_like(dv_s)
    bias = live_bias(count_ref[0], span, unit_max)

    def one_head(head, carry):
        half = head // 2
        sub = lax.rem(head, 2)
        side = pl.ds(pl.multiple_of(half * pair, pair), pair)
        inside = (lane // HD) == sub
        inside_c = (lane_c // HD) == sub
        zero = jnp.zeros((), bf16)
        keys = head_keys(k_ref[:, side], bias, lane, sub)
        values = jnp.where(inside, v_ref[:, side], zero)
        keys_t = kt_s[pl.ds(pl.multiple_of(head * HD, HD), HD), :]
        d_k = None
        d_v = None
        for begin in range(0, span, chunk):
            part = slice(begin, begin + chunk)
            queries = q_ref[part, side]
            grads = do_s[part, side]
            scores = right_dot(keys, head_queries(queries, lane_c, sub))
            probs = jnp.exp(scores - lse_ref[half, pl.ds(sub, 1), part])
            d_probs = right_dot(values, grads)
            d_scores = (probs * (d_probs - delta_s[pl.ds(head, 1), part])).astype(bf16)
            add_v = plain_dot(probs.astype(bf16), jnp.where(inside_c, grads, zero))
            add_k = plain_dot(d_scores, jnp.where(inside_c, queries, zero))
            d_v = add_v if d_v is None else d_v + add_v
            d_k = add_k if d_k is None else d_k + add_k
            dqt_s[pl.ds(pl.multiple_of(head * HD, HD), HD), part] = plain_dot(keys_t, d_scores)
        dk_s[:, side] += d_k
        dv_s[:, side] += d_v
        return carry

    lax.fori_loop(0, heads, one_head, 0)
    d_q = (dqt_s[...].T * (HD ** (-0.5))).astype(bf16)
    d_k = dk_s[...].astype(bf16)
    d_v = dv_s[...].astype(bf16)

    add = (
        right_dot(d_q, whole_block(wq_ref))
        + right_dot(d_k, whole_block(wk_ref))
        + right_dot(d_v, whole_block(wv_ref))
    )

    @pl.when(step == 0)
    def _():
        gn_s[...] = add

    @pl.when(step > 0)
    def _():
        gn_s[...] += add
        for copy in copies(step - 1):
            copy.wait()

    n1 = n1_ref[...]
    for m, grad in enumerate((d_q, d_k, d_v)):
        stage[m] = left_dot(n1, grad).astype(bf16).reshape(parts, rows, LANES)
    stage[3] = left_dot(o_ref[...], ghb_ref[:, mine]).astype(bf16).reshape(parts, rows, LANES)
    for copy in copies(step):
        copy.start()

    @pl.when(step == steps - 1)
    def _():
        tokens = x_ref[...].astype(f32)
        inv = inverse_rms(tokens)
        grad = gn_s[...]
        scaled = tokens * inv
        total = jnp.sum(grad * scaled, axis=0, keepdims=True)
        stage_gain[...] = spread_gain(total, parts)
        last = pltpu.make_async_copy(
            stage_gain, pack_ref.at[:, pl.ds(4 * cols * rows, GAIN_ROWS), :], gain_sem.at[0]
        )
        last.start()
        weighted = grad * gain_ref[...]
        mean = jnp.mean(scaled * weighted, axis=-1, keepdims=True)
        gx_ref[...] = (gh_ref[...] + inv * (weighted - scaled * mean)).astype(bf16)
        for copy in copies(step):
            copy.wait()
        last.wait()


def attend_back(count, qkv, mixed, lse, n1, tokens, g_h, g_hb, gain, packed, unit_max, rows):
    span, width = tokens.shape
    parts = packed.shape[0]
    cols = width // LANES
    full = const_block((span, width))

    def block(first):
        return pl.BlockSpec((span, LANES), lambda p: (0, first + p))

    def weight(first):
        return pl.BlockSpec((parts, rows, LANES), lambda p: (0, first + p, 0))

    return pl.pallas_call(
        functools.partial(attend_back_kernel, unit_max, 512),
        grid=(cols,),
        out_shape=(
            jax.ShapeDtypeStruct((span, width), bf16),
            jax.ShapeDtypeStruct((parts, 4 * cols * rows + GAIN_ROWS, LANES), bf16),
        ),
        in_specs=[
            smem(),
            block(0),
            block(cols),
            block(2 * cols),
            full,
            pl.BlockSpec((2, 8, span), lambda p: (p, 0, 0)),
            full,
            full,
            full,
            full,
            const_block((1, width)),
            weight(0),
            weight(cols),
            weight(2 * cols),
            pl.BlockSpec((parts, cols * rows, LANES), lambda p: (0, 3, 0)),
        ],
        out_specs=(full, pl.BlockSpec(memory_space=pl.ANY)),
        scratch_shapes=[
            pltpu.VMEM((cols, width, LANES), bf16),
            pltpu.VMEM((span, LANES), bf16),
            pltpu.VMEM((8, span), f32),
            pltpu.VMEM((LANES, span), bf16),
            pltpu.VMEM((LANES, span), f32),
            pltpu.VMEM((span, LANES), f32),
            pltpu.VMEM((span, LANES), f32),
            pltpu.VMEM((span, width), f32),
            pltpu.VMEM((4, parts, rows, LANES), bf16),
            pltpu.VMEM((parts, GAIN_ROWS, LANES), bf16),
            pltpu.SemaphoreType.DMA((4,)),
            pltpu.SemaphoreType.DMA((1,)),
        ],
        compiler_params=params(),
        cost_estimate=cost(10 * span * span * width + 16 * span * width * width, 24 << 20, span * span * H),
        name="attend_back",
    )(count, qkv, qkv, qkv, mixed, lse, n1, tokens, g_h, g_hb, gain, packed, packed, packed, packed)


def finish_kernel(layout, own, gain_cols, me_ref, mine_ref, other_ref, *outs):
    begin = 0
    for (rows, blocks), out_ref in zip(layout, outs[:-1]):
        for c in range(blocks):
            at = slice(begin, begin + rows)
            out_ref[:, c * LANES : (c + 1) * LANES] = mine_ref[at].astype(f32) + other_ref[at].astype(f32)
            begin += rows
    at = slice(begin, begin + GAIN_ROWS)
    row = lax.broadcasted_iota(jnp.int32, (GAIN_ROWS, own), 0)
    from_lane = lax.broadcasted_iota(jnp.int32, (LANES, own), 0)
    to_lane = lax.broadcasted_iota(jnp.int32, (LANES, own), 1)
    total = jnp.zeros((GAIN_ROWS, own), f32)
    for c in range(gain_cols):
        pick = jnp.where(from_lane + c * LANES == to_lane + me_ref[0] * own, 1.0, 0.0).astype(bf16)
        found = plain_dot(mine_ref[at], pick) + plain_dot(other_ref[at], pick)
        total += jnp.where(row == c, found, 0.0)
    outs[-1][...] = jnp.sum(total, axis=0, keepdims=True)


def finish(packed, layout, own):
    parts = packed.shape[0]
    flat = packed.reshape(-1, LANES)
    share = lax.psum_scatter(flat, "shard", scatter_dimension=0, tiled=True)
    count = lax.axis_size("replica")
    step = 1
    other = jnp.zeros_like(share)
    while step < count:
        if step > 1:
            share = (share.astype(f32) + other.astype(f32)).astype(bf16)
        other = lax.ppermute(share, "replica", [(i, i ^ step) for i in range(count)])
        step *= 2
    me = lax.axis_index("shard").reshape(1)
    outs = pl.pallas_call(
        functools.partial(finish_kernel, layout, own, parts * own // LANES),
        out_shape=tuple(jax.ShapeDtypeStruct((r, b * LANES), f32) for r, b in layout)
        + (jax.ShapeDtypeStruct((1, own), f32),),
        in_specs=[smem(), vmem(), vmem()],
        out_specs=(vmem(),) * (len(layout) + 1),
        compiler_params=params(),
        cost_estimate=cost(0, 4 << 20),
        name="finish",
    )(me, share, other)
    return outs[:-1] + (outs[-1][0],)


def to_blocks(mat, parts):
    rows = mat.shape[0] // parts
    cols = mat.shape[1] // LANES
    split = mat.reshape(parts, rows, cols, LANES).transpose(0, 2, 1, 3)
    return split.reshape(parts, cols * rows, LANES)


def gather_packed(mats):
    packed = jnp.concatenate([to_blocks(m, 1)[0] for m in mats], axis=0)
    whole = lax.all_gather(packed, "shard", axis=0, tiled=True)
    return whole.reshape(-1, packed.shape[0], LANES)


def shards(
    x_in,
    seq_units,
    deal,
    gain_attn,
    w_query,
    w_key,
    w_value,
    w_out,
    gain_ffn,
    w_gate,
    w_up,
    w_down,
    d_out,
):
    shard_count = lax.axis_size("shard")
    my_index = lax.axis_index("shard")
    given, width = x_in.shape[1:]
    span = d_out.shape[2]
    unit_max = span // shard_count
    rows = w_query.shape[0]
    down = w_down.shape[0]
    slot_ids = jnp.arange(shard_count, dtype=jnp.int32)
    outgoing = deal_rows(seq_units, deal, x_in[0], shard_count, unit_max)
    arrived = lax.all_to_all(outgoing, "shard", split_axis=0, concat_axis=0, tiled=True)
    own_seq = jnp.sum(jnp.where(slot_ids == my_index, deal[0], 0))
    count = jnp.sum(jnp.where(slot_ids == own_seq, seq_units[0], 0)).reshape(1)
    attn_pack = gather_packed((w_query, w_key, w_value, w_out))
    ffn_pack = gather_packed((w_gate, w_up, w_down))
    tokens = arrived.reshape(span, width)
    gain_one = gain_attn.reshape(1, width)
    gain_two = gain_ffn.reshape(1, width)
    n1, qkv = make_qkv(tokens, gain_one, attn_pack, rows)
    mixed, lse = attend_forward(count, qkv, unit_max)
    hidden, n2 = out_project(tokens, mixed, attn_pack, gain_two, rows)
    layer_out, g_h, g_hb, ffn_grads = ffn_both(
        count, hidden, n2, d_out[0, 0], gain_two, ffn_pack, unit_max, rows, down
    )
    own = width // shard_count
    cols = width // LANES
    wide = w_gate.shape[1] // LANES
    out_wg, out_wu, out_wd, out_gain_two = finish(
        ffn_grads, ((rows, wide), (rows, wide), (down, cols)), own
    )
    g_x, attn_grads = attend_back(
        count, qkv, mixed, lse, n1, tokens, g_h, g_hb, gain_one, attn_pack, unit_max, rows
    )
    returned = lax.all_to_all(
        g_x.reshape(shard_count, unit_max, width), "shard", split_axis=0, concat_axis=0, tiled=True
    )
    grad_x = undeal_rows(seq_units, deal, returned, given)[None]
    out_wq, out_wk, out_wv, out_wo, out_gain_one = finish(attn_grads, ((rows, cols),) * 4, own)
    return (
        layer_out.reshape(1, 1, span, width),
        grad_x,
        out_gain_one,
        out_gain_two,
        out_wq,
        out_wk,
        out_wv,
        out_wo,
        out_wg,
        out_wu,
        out_wd,
    )


def solution(mesh):
    return jax.shard_map(
        shards,
        mesh=mesh,
        in_specs=(
            P("replica", "shard", None),
            P("replica", None),
            P("replica", None),
            P(),
            P("shard", None),
            P("shard", None),
            P("shard", None),
            P("shard", None),
            P(),
            P("shard", None),
            P("shard", None),
            P("shard", None),
            P("replica", "shard", None, None),
        ),
        out_specs=(
            P("replica", "shard", None, None),
            P("replica", "shard", None),
            P("shard"),
            P("shard"),
            P("shard", None),
            P("shard", None),
            P("shard", None),
            P("shard", None),
            P("shard", None),
            P("shard", None),
            P("shard", None),
        ),
        check_vma=False,
    )
```

time: 667 us -> 453 us (0.68); the launches traced: 658 us -> 452 us
  matrix products: 237 us -> 0 us
  Pallas kernels: 10.9 us -> 169 us
  local copies, waits for them, and re-layouts: 82.9 us -> 8.21 us
  other arithmetic: 77.7 us -> 3.5 us
  waiting for transfers between devices: 217 us -> 244 us
    dot_general x33 -> x0, matrix products: 237 us -> none  [the longest x2 45.7 us: attend_backward(): jnp.einsum('qhd,khd->hqk', grad_heads, value_heads, preferred_element_typ...]
    pallas_call x0 -> x7, Pallas kernels: none -> 158 us  [the longest x1 57.8 us: attend_back(): pl.pallas_call(functools.partial(attend_back_kernel, unit_max, 512), grid...]
    convert_element_type x6 -> x0, other arithmetic: 46.1 us -> none  [the longest x1 42 us: attend_backward(): grad_scores = (prob_vals * (grad_probs - row_dot)).astype(jnp.bfloat16)]
    all_gather x2, waiting for transfers between devices: 9.79 us -> 51.9 us  [gather_packed(): whole = lax.all_gather(packed, 'shard', axis=0, tiled=True)]
    unnamed x151 -> x25, local copies, waits for them, and re-layouts: 27.4 us -> 2.97 us
    reduce_sum x4 -> x2, other arithmetic: 21.1 us -> 1.91 us  [the longest x1 1.28 us: shards(): count = jnp.sum(jnp.where(slot_ids == own_seq, seq_units[0], 0)).reshape(1)]
    transpose x12 -> x0, local copies, waits for them, and re-layouts: 13.3 us -> none  [from_blocks(): split = packed.reshape(parts, cols, rows, LANES).transpose(0, 2, 1, 3)]
    reshape x10 -> x6, local copies, waits for them, and re-layouts: 16.6 us -> 3.89 us  [to_blocks(): split = mat.reshape(parts, rows, cols, LANES).transpose(0, 2, 1, 3)]
  transfers between devices with their start and end apart: 8 -> 8, of which waited for: 5 -> 6; matrix products, arithmetic and copies ran while one was open for 22% -> 1% of each run, Pallas kernels for 2% -> 25%
where the time goes in v2:
time: 453 us; the launch traced here: 452 us
  waiting for transfers between devices  244 us (54%)
  Pallas kernels  169 us (37%)
  starting transfers between devices  14.4 us (3%)
  between operations  14 us (3%)
  local copies, waits for them, and re-layouts  8.21 us (2%)
    reduce_scatter x2, waiting for transfers between devices, finish(): share = lax.psum_scatter(flat, 'shard', scatter_dimension=0, tiled=True)  143 us
    pallas_call x1, Pallas kernels, attend_back(): pl.pallas_call(functools.partial(attend_back_kernel, unit_max, 512), grid...  57.8 us
    pallas_call x1, Pallas kernels, ffn_both(): pl.pallas_call(functools.partial(ffn_kernel, unit_max), grid=(blocks,), o...  52.9 us
    all_gather x2, waiting for transfers between devices, gather_packed(): whole = lax.all_gather(packed, 'shard', axis=0, tiled=True)  51.9 us
    all_to_all x1, waiting for transfers between devices, shards(): lax.all_to_all(outgoing, 'shard', split_axis=0, concat_axis=0, tiled=True)  47.3 us
    pallas_call x1, Pallas kernels, attend_forward(): pl.pallas_call(functools.partial(attend_kernel, unit_max, 512), grid=(pai...  26.2 us
    pallas_call x1, Pallas kernels, make_qkv(): pl.pallas_call(qkv_kernel, grid=(blocks,), out_shape=(jax.ShapeDtypeStruc...  10.8 us
  transfers between devices with their start and end apart: 8, of which 6 were waited for; matrix products, arithmetic and copies ran while one was open for 1% of the time, Pallas kernels for 25%

profile of v2, /device:TPU:0, one launch (start us, length us, event | category | flops | bytes accessed | tf_op | source)
XLA Modules:
  0.0 452.5 jit_solution(15810911348290770556)
XLA Ops:
  7.2 0.0 copy-start.4
  7.2 0.0 copy-start.5
  7.2 0.0 all-gather.3.cloned.1.call-start
  7.2 1.0 reshape.80
  8.3 0.9 reshape.81
  9.2 0.0 copy-start.6
  9.2 1.0 reshape.82
  10.2 0.9 reshape.83
  11.1 0.7 pad_maximum_fusion.1
  11.9 0.0 all-gather.3.cloned.1.call-update
  11.9 0.0 all-gather.5.cloned.1.call-start
  12.0 0.0 copy-done.4
  12.1 0.0 copy-done.5
  12.2 0.0 copy-done.6
  12.2 0.2 copy.40
  12.3 0.2 copy.41
  12.5 0.9 pad_maximum_fusion
  13.3 0.0 all-gather.5.cloned.1.call-update
  13.4 6.6 %deal_rows.1 = bf16[16,64,768]{2,1,0:T(8,128)(2,1)} custom-call(s32[1,16]{1,0:T(1,128)} %units_ref.3, s32[1,16]{1,0:T(1,128)} %order_ref.3, bf16[512,768]{1,0:T(8,128)(2,1)} %bitcast.59), custom_call_target="tpu_custom_call" | custom-call | tf_op jit(solution)/shard_map/deal_rows/pallas_call | solution.py:89
  20.0 0.0 copy-start.7
  20.0 0.0 copy-start.8
  20.0 0.0 copy-start.10
  20.0 0.0 copy-start.9
  20.0 7.5 %all-to-all-start = ((bf16[16,64,768]{2,1,0:T(8,128)(2,1)}), bf16[16,64,768]{2,1,0:T(8,128)(2,1)S(1)}, u32[]{:S(2)}, u32[]{:S(2)}) async-start(bf16[16,64,768]{2,1,0:T(8,128)(2,1)} %deal_rows.1), calls=%async_computation | async-start | bytes 3145728 | tf_op jit(solution)/shard_map/all_to_all | solution.py:765
  27.5 0.0 reduce-scatter.5.cloned.1.call-start
  27.6 0.0 copy-done.7
  27.6 0.6 reshape.79.gain_ref
  28.2 0.0 copy-done.8
  28.2 0.6 reshape.85.gain_ref
  28.8 0.0 copy-done.10
  28.8 0.6 fusion
  29.4 0.0 copy-done.9
  29.4 1.3 fusion.1
  30.7 47.3 %all-to-all-done = bf16[16,64,768]{2,1,0:T(8,128)(2,1)S(1)} async-done(((bf16[16,64,768]{2,1,0:T(8,128)(2,1)}), bf16[16,64,768]{2,1,0:T(8,128)(2,1)S(1)}, u32[]{:S(2)}, u32[]{:S(2)}) %all-to-all-start) | async-done | bytes 1572896 | tf_op jit(solution)/shard_map/all_to_all | solution.py:765
  78.0 0.0 copy-start.1
  78.0 10.6 %all-gather.3.cloned.1.call-done = bf16[9216,256]{1,0:T(8,128)(2,1)} async-done(((bf16[576,256]{1,0:T(8,128)(2,1)}), bf16[9216,256]{1,0:T(8,128)(2,1)}) %all-gather.3.cloned.1.call-update) | async-done | bytes 4718608 | tf_op jit(solution)/shard_map/all_gather | solution.py:737
  88.6 0.0 copy-done.1
  88.6 10.8 %make_qkv.1 = (bf16[1024,768]{1,0:T(8,128)(2,1)}, bf16[1024,2304]{1,0:T(8,128)(2,1)}) custom-call(bf16[1024,768]{1,0:T(8,128)(2,1)} %bitcast.43, f32[1,768]{1,0:T(1,128)} %reshape.79.gain_ref, bf16[16,576,256]{2,1,0:T(8,128)(2,1)} %bitcast.47), custom_call_target="tpu_custom_call" | custom-call | flops 3623878656 | bytes 14680064 | tf_op jit(solution)/shard_map/make_qkv/pallas_call | solution.py:149
  99.4 26.2 %attend_forward.1 = (bf16[1024,768]{1,0:T(8,128)(2,1)}, f32[6,8,1024]{2,1,0:T(8,128)}) custom-call(s32[1]{0:T(128)} %bitcast.2.count_ref, bf16[1024,2304]{1,0:T(8,128)(2,1)} %get-tuple-element.32.q_ref.k_ref.v_ref, bf16[1024,2304]{1,0:T(8,128)(2,1)} %get-tuple-element.32.q_ref.k_ref.v_ref, bf16[1024,2304]{1,0:T(8,128)(2,1)} %get-tuple-element.32.q_ref.k_ref.v_ref), custom_call_target="tpu_custom_call" | custom-call | flops 3221225472 | bytes 8388608 | tf_op jit(solution)/shard_map/attend_forward/pallas_call | solution.py:222
  125.6 6.0 %out_project.1 = (f32[1024,768]{1,0:T(8,128)}, bf16[1024,768]{1,0:T(8,128)(2,1)}) custom-call(bf16[1024,768]{1,0:T(8,128)(2,1)} %bitcast.44, bf16[1024,768]{1,0:T(8,128)(2,1)} %get-tuple-element.33.o_ref, bf16[16,576,256]{2,1,0:T(8,128)(2,1)} %bitcast.48, f32[1,768]{1,0:T(1,128)} %reshape.85.gain_ref), custom_call_target="tpu_custom_call" | custom-call | flops 1207959552 | bytes 9437184 | tf_op jit(solution)/shard_map/out_project/pallas_call | solution.py:257
  131.6 41.3 %all-gather.5.cloned.1.call-done = bf16[18432,256]{1,0:T(8,128)(2,1)} async-done(((bf16[1152,256]{1,0:T(8,128)(2,1)}), bf16[18432,256]{1,0:T(8,128)(2,1)}) %all-gather.5.cloned.1.call-update) | async-done | bytes 9437200 | tf_op jit(solution)/shard_map/all_gather | solution.py:737
  172.9 52.9 %ffn_both.1 = (bf16[1024,768]{1,0:T(8,128)(2,1)}, f32[1024,768]{1,0:T(8,128)}, bf16[1024,768]{1,0:T(8,128)(2,1)}, bf16[16,1168,256]{2,1,0:T(8,128)(2,1)}) custom-call(s32[1]{0:T(128)} %bitcast.2.count_ref, f32[1024,768]{1,0:T(8,128)} %get-tuple-element.34.h_ref, bf16[1024,768]{1,0:T(8,128)(2,1)} %get-tuple-element.35.n2_ref, bf16[1024,768]{1,0:T(8,128)(2,1)} %bitcast.74, ...), custom_call_target="tpu_custom_call" | custom-call | flops 28991029248 | bytes 37748736 | tf_op jit(solution)/shard_map/ffn_both/pallas_call | solution.py:434
  225.8 0.0 reduce-scatter.5.cloned.1.call-update
  225.8 0.0 reduce-scatter.3.cloned.1.call-start
  225.9 57.8 %attend_back.1 = (bf16[1024,768]{1,0:T(8,128)(2,1)}, bf16[16,592,256]{2,1,0:T(8,128)(2,1)}) custom-call(s32[1]{0:T(128)} %bitcast.2.count_ref, bf16[1024,2304]{1,0:T(8,128)(2,1)} %get-tuple-element.32.q_ref.k_ref.v_ref, bf16[1024,2304]{1,0:T(8,128)(2,1)} %get-tuple-element.32.q_ref.k_ref.v_ref, bf16[1024,2304]{1,0:T(8,128)(2,1)} %get-tuple-element.32.q_ref.k_ref.v_ref, ...), custom_call_target="tpu_custom_call" | custom-call | flops 17716740096 | bytes 25165824 | tf_op jit(solution)/shard_map/attend_back/pallas_call | solution.py:638
  283.7 0.0 reduce-scatter.3.cloned.1.call-update
  283.7 3.7 all-to-all-start.1
  287.4 65.1 %reduce-scatter.5.cloned.1.call-done.mine_ref = bf16[1168,256]{1,0:T(8,128)(2,1)} async-done(((bf16[18688,256]{1,0:T(8,128)(2,1)}), bf16[1168,256]{1,0:T(8,128)(2,1)}) %reduce-scatter.5.cloned.1.call-update) | async-done | bytes 598032 | tf_op jit(solution)/shard_map/reduce_scatter | solution.py:705
  352.5 1.5 collective-permute-start.1
  354.0 78.2 %reduce-scatter.3.cloned.1.call-done.mine_ref = bf16[592,256]{1,0:T(8,128)(2,1)} async-done(((bf16[9472,256]{1,0:T(8,128)(2,1)}), bf16[592,256]{1,0:T(8,128)(2,1)}) %reduce-scatter.3.cloned.1.call-update) | async-done | bytes 303120 | tf_op jit(solution)/shard_map/reduce_scatter | solution.py:705
  432.2 1.5 collective-permute-start
  433.6 0.0 all-to-all-done.1.back_ref
  433.6 0.0 copy-start
  433.6 1.2 copy-done
  434.8 4.1 undeal_rows.1
  439.0 1.1 collective-permute-done.other_ref
  440.1 0.0 copy-start.3
  440.1 0.7 copy-done.3
  440.8 1.9 finish.2
  442.7 0.0 collective-permute-done.1.other_ref
  442.7 0.0 copy-start.2
  442.7 0.8 copy-done.2
  443.5 2.4 finish.3
  (8 shorter events, 0.2 us)
Async XLA Ops:
  7.2 4.8 %copy-start.4 = (bf16[48,2048]{1,0:T(8,128)(2,1)S(1)}, bf16[48,2048]{1,0:T(8,128)(2,1)}, u32[]{:S(2)}) copy-start(bf16[48,2048]{1,0:T(8,128)(2,1)} %param.22) | copy-start | bytes 589828
  7.2 4.9 %copy-start.5 = (bf16[48,2048]{1,0:T(8,128)(2,1)S(1)}, bf16[48,2048]{1,0:T(8,128)(2,1)}, u32[]{:S(2)}) copy-start(bf16[48,2048]{1,0:T(8,128)(2,1)} %param.23) | copy-start | bytes 589828
  7.2 81.4 %all-gather.3.cloned.1.call-start = ((), (), s32[]{:S(2)}) async-start(), calls=%async_computation.4 | async-start | bytes 5013504 | tf_op jit(solution)/shard_map/all_gather | solution.py:737
  9.2 2.9 copy-start.6
  11.9 161.0 %all-gather.5.cloned.1.call-start = ((), (), s32[]{:S(2)}) async-start(), calls=%async_computation.5 | async-start | bytes 10027008 | tf_op jit(solution)/shard_map/all_gather | solution.py:737
  20.0 7.6 %copy-start.7 = (f32[768]{0:T(1024)S(1)}, f32[768]{0:T(1024)}, u32[]{:S(2)}) copy-start(f32[768]{0:T(1024)} %param.16) | copy-start | bytes 9220
  20.0 8.2 %copy-start.8 = (f32[768]{0:T(1024)S(1)}, f32[768]{0:T(1024)}, u32[]{:S(2)}) copy-start(f32[768]{0:T(1024)} %param.21) | copy-start | bytes 9220
  20.0 8.8 %copy-start.10 = (s32[1,16]{1,0:T(1,128)S(1)}, s32[1,16]{1,0:T(1,128)}, u32[]{:S(2)}) copy-start(s32[1,16]{1,0:T(1,128)} %order_ref.3) | copy-start | bytes 196
  20.0 9.4 %copy-start.9 = (s32[1,16]{1,0:T(1,128)S(1)}, s32[1,16]{1,0:T(1,128)}, u32[]{:S(2)}) copy-start(s32[1,16]{1,0:T(1,128)} %units_ref.3) | copy-start | bytes 196
  20.0 58.0 %all-to-all-start = ((bf16[16,64,768]{2,1,0:T(8,128)(2,1)}), bf16[16,64,768]{2,1,0:T(8,128)(2,1)S(1)}, u32[]{:S(2)}, u32[]{:S(2)}) async-start(bf16[16,64,768]{2,1,0:T(8,128)(2,1)} %deal_rows.1), calls=%async_computation | async-start | bytes 3145728 | tf_op jit(solution)/shard_map/all_to_all | solution.py:765
  27.5 325.0 %reduce-scatter.5.cloned.1.call-start = ((), (), s32[]{:S(2)}) async-start(), calls=%async_computation.7 | async-start | bytes 10166272 | tf_op jit(solution)/shard_map/reduce_scatter | solution.py:705
  78.0 10.6 %copy-start.1 = (bf16[16,64,768]{2,1,0:T(8,128)(2,1)}, bf16[16,64,768]{2,1,0:T(8,128)(2,1)S(1)}, u32[]{:S(2)}) copy-start(bf16[16,64,768]{2,1,0:T(8,128)(2,1)S(1)} %all-to-all-done) | copy-start | bytes 4718596
  225.8 206.3 %reduce-scatter.3.cloned.1.call-start = ((), (), s32[]{:S(2)}) async-start(), calls=%async_computation.6 | async-start | bytes 5152768 | tf_op jit(solution)/shard_map/reduce_scatter | solution.py:705
  283.7 149.9 %all-to-all-start.1 = ((bf16[16,64,768]{2,1,0:T(8,128)(2,1)}), bf16[16,64,768]{2,1,0:T(8,128)(2,1)S(1)}, u32[]{:S(2)}, u32[]{:S(2)}) async-start(bf16[16,64,768]{2,1,0:T(8,128)(2,1)} %bitcast.24), calls=%async_computation.1 | async-start | bytes 3145728 | tf_op jit(solution)/shard_map/all_to_all | solution.py:788
  352.5 90.2 %collective-permute-start.1 = (bf16[1168,256]{1,0:T(8,128)(2,1)}, bf16[1168,256]{1,0:T(8,128)(2,1)S(1)}, u32[]{:S(2)}, u32[]{:S(2)}) collective-permute-start(bf16[1168,256]{1,0:T(8,128)(2,1)} %reduce-scatter.5.cloned.1.call-done.mine_ref), channel_id=1, source_target_pairs={{0,1},{1,0},{2,3},{3,2},{4,5},{5,4},{6,7},{7,6},{8,9},{9,8},{10,11... | collective-permute-start | bytes 1794056 | tf_op jit(solution)/shard_map/ppermute | solution.py:712
  432.2 7.9 %collective-permute-start = (bf16[592,256]{1,0:T(8,128)(2,1)}, bf16[592,256]{1,0:T(8,128)(2,1)S(1)}, u32[]{:S(2)}, u32[]{:S(2)}) collective-permute-start(bf16[592,256]{1,0:T(8,128)(2,1)} %reduce-scatter.3.cloned.1.call-done.mine_ref), channel_id=1, source_target_pairs={{0,1},{1,0},{2,3},{3,2},{4,5},{5,4},{6,7},{7,6},{8,9},{9,8},{10,11... | collective-permute-start | bytes 909320 | tf_op jit(solution)/shard_map/ppermute | solution.py:712
  433.6 1.2 copy-start
  440.1 0.7 copy-start.3
  442.7 0.8 copy-start.2
Sparse Core Ops, SparseCore 0:
  12.0 76.5 all-gather.2
  91.4 81.4 all-gather.4
  225.9 126.5 reduce-scatter.4
  356.2 75.8 reduce-scatter.2

commit v3 on v2

--- a/solution.py
+++ b/solution.py
@@ -471,6 +471,7 @@
     unit_max,
     chunk,
     count_ref,
+    place_ref,
     q_ref,
     k_ref,
     v_ref,
@@ -486,7 +487,8 @@
     wv_ref,
     wo_ref,
     gx_ref,
-    pack_ref,
+    keep_ref,
+    send_ref,
     wo_s,
     do_s,
     delta_s,
@@ -511,15 +513,22 @@
     lane_c = lane[:chunk]
     mine = pl.ds(pl.multiple_of(step * LANES, LANES), LANES)
 
+    half_parts = parts // 2
+
     def copies(which):
         return [
             pltpu.make_async_copy(
-                stage.at[m],
-                pack_ref.at[:, pl.ds(pl.multiple_of((m * cols + which) * rows, 8), rows), :],
-                sems.at[m],
+                stage.at[m, pl.ds(side * half_parts, half_parts)],
+                to_ref.at[:, pl.ds(pl.multiple_of((m * cols + which) * rows, 8), rows), :],
+                sems.at[m, side],
             )
             for m in range(4)
+            for side, to_ref in enumerate((keep_ref, send_ref))
         ]
+
+    def put(m, grad):
+        for part in range(parts):
+            stage[m, place_ref[part]] = grad[part * rows : (part + 1) * rows].astype(bf16)
 
     @pl.when(step == 0)
     def _():
@@ -598,8 +607,8 @@
 
     n1 = n1_ref[...]
     for m, grad in enumerate((d_q, d_k, d_v)):
-        stage[m] = left_dot(n1, grad).astype(bf16).reshape(parts, rows, LANES)
-    stage[3] = left_dot(o_ref[...], ghb_ref[:, mine]).astype(bf16).reshape(parts, rows, LANES)
+        put(m, left_dot(n1, grad))
+    put(3, left_dot(o_ref[...], ghb_ref[:, mine]))
     for copy in copies(step):
         copy.start()
 
@@ -610,20 +619,27 @@
         grad = gn_s[...]
         scaled = tokens * inv
         total = jnp.sum(grad * scaled, axis=0, keepdims=True)
-        stage_gain[...] = spread_gain(total, parts)
-        last = pltpu.make_async_copy(
-            stage_gain, pack_ref.at[:, pl.ds(4 * cols * rows, GAIN_ROWS), :], gain_sem.at[0]
-        )
-        last.start()
+        spread = spread_gain(total, parts)
+        for part in range(parts):
+            stage_gain[place_ref[part]] = spread[part]
+        last = [
+            pltpu.make_async_copy(
+                stage_gain.at[pl.ds(side * half_parts, half_parts)],
+                to_ref.at[:, pl.ds(4 * cols * rows, GAIN_ROWS), :],
+                gain_sem.at[side],
+            )
+            for side, to_ref in enumerate((keep_ref, send_ref))
+        ]
+        for copy in last:
+            copy.start()
         weighted = grad * gain_ref[...]
         mean = jnp.mean(scaled * weighted, axis=-1, keepdims=True)
         gx_ref[...] = (gh_ref[...] + inv * (weighted - scaled * mean)).astype(bf16)
-        for copy in copies(step):
+        for copy in copies(step) + last:
             copy.wait()
-        last.wait()
-
-
-def attend_back(count, qkv, mixed, lse, n1, tokens, g_h, g_hb, gain, packed, unit_max, rows):
+
+
+def attend_back(count, place, qkv, mixed, lse, n1, tokens, g_h, g_hb, gain, packed, unit_max, rows):
     span, width = tokens.shape
     parts = packed.shape[0]
     cols = width // LANES
@@ -640,9 +656,11 @@
         grid=(cols,),
         out_shape=(
             jax.ShapeDtypeStruct((span, width), bf16),
-            jax.ShapeDtypeStruct((parts, 4 * cols * rows + GAIN_ROWS, LANES), bf16),
+            jax.ShapeDtypeStruct((parts // 2, 4 * cols * rows + GAIN_ROWS, LANES), bf16),
+            jax.ShapeDtypeStruct((parts // 2, 4 * cols * rows + GAIN_ROWS, LANES), bf16),
         ),
         in_specs=[
+            smem(),
             smem(),
             block(0),
             block(cols),
@@ -659,7 +677,7 @@
             weight(2 * cols),
             pl.BlockSpec((parts, cols * rows, LANES), lambda p: (0, 3, 0)),
         ],
-        out_specs=(full, pl.BlockSpec(memory_space=pl.ANY)),
+        out_specs=(full, pl.BlockSpec(memory_space=pl.ANY), pl.BlockSpec(memory_space=pl.ANY)),
         scratch_shapes=[
             pltpu.VMEM((cols, width, LANES), bf16),
             pltpu.VMEM((span, LANES), bf16),
@@ -671,13 +689,13 @@
             pltpu.VMEM((span, width), f32),
             pltpu.VMEM((4, parts, rows, LANES), bf16),
             pltpu.VMEM((parts, GAIN_ROWS, LANES), bf16),
-            pltpu.SemaphoreType.DMA((4,)),
-            pltpu.SemaphoreType.DMA((1,)),
+            pltpu.SemaphoreType.DMA((4, 2)),
+            pltpu.SemaphoreType.DMA((2,)),
         ],
         compiler_params=params(),
         cost_estimate=cost(10 * span * span * width + 16 * span * width * width, 24 << 20, span * span * H),
         name="attend_back",
-    )(count, qkv, qkv, qkv, mixed, lse, n1, tokens, g_h, g_hb, gain, packed, packed, packed, packed)
+    )(count, place, qkv, qkv, qkv, mixed, lse, n1, tokens, g_h, g_hb, gain, packed, packed, packed, packed)
 
 
 def finish_kernel(layout, own, gain_cols, me_ref, mine_ref, other_ref, *outs):
@@ -699,10 +717,49 @@
     outs[-1][...] = jnp.sum(total, axis=0, keepdims=True)
 
 
-def finish(packed, layout, own):
-    parts = packed.shape[0]
-    flat = packed.reshape(-1, LANES)
-    share = lax.psum_scatter(flat, "shard", scatter_dimension=0, tiled=True)
+def relative_places(shard_count):
+    along = shard_count // 4
+    mine = lax.axis_index("shard")
+    part = jnp.arange(shard_count, dtype=jnp.int32)
+    core = lax.rem(part, 2) ^ lax.rem(mine, 2)
+    side = lax.rem(part // 2, 2) ^ lax.rem(mine // 2, 2)
+    steps = lax.rem(part // 4 - mine // 4 + along, along)
+    return (core * 2 + side) * along + steps
+
+
+def to_core(value):
+    count = lax.axis_size("shard")
+    return lax.ppermute(value, "shard", [(i, i ^ 1) for i in range(count)])
+
+
+def to_side(value):
+    count = lax.axis_size("shard")
+    return lax.ppermute(value, "shard", [(i, i ^ 2) for i in range(count)])
+
+
+def along_z(value, step):
+    count = lax.axis_size("shard")
+    return lax.ppermute(value, "shard", [(i, (i + 4 * step) % count) for i in range(count)])
+
+
+def scatter_queue(packed):
+    return lax.psum_scatter(packed.reshape(-1, LANES), "shard", scatter_dimension=0, tiled=True)
+
+
+def scatter_permute(keep, send):
+    along = keep.shape[0] // 2
+    came = to_core(send)
+    pass_on = (keep[along:].astype(f32) + came[along:].astype(f32)).astype(bf16)
+    crossed = to_side(pass_on)
+    column = (keep[:along].astype(f32) + came[:along].astype(f32) + crossed.astype(f32)).astype(bf16)
+    found = [along_z(column[k], k) for k in range(1, along)]
+    total = column[0].astype(f32)
+    for piece in found:
+        total = total + piece.astype(f32)
+    return total.astype(bf16)
+
+
+def finish(share, layout, own, parts):
     count = lax.axis_size("replica")
     step = 1
     other = jnp.zeros_like(share)
@@ -779,17 +836,22 @@
     own = width // shard_count
     cols = width // LANES
     wide = w_gate.shape[1] // LANES
-    out_wg, out_wu, out_wd, out_gain_two = finish(
-        ffn_grads, ((rows, wide), (rows, wide), (down, cols)), own
-    )
-    g_x, attn_grads = attend_back(
-        count, qkv, mixed, lse, n1, tokens, g_h, g_hb, gain_one, attn_pack, unit_max, rows
+    ffn_share = scatter_queue(ffn_grads)
+    place = relative_places(shard_count)
+    g_x, keep, send = attend_back(
+        count, place, qkv, mixed, lse, n1, tokens, g_h, g_hb, gain_one, attn_pack, unit_max, rows
     )
     returned = lax.all_to_all(
         g_x.reshape(shard_count, unit_max, width), "shard", split_axis=0, concat_axis=0, tiled=True
     )
     grad_x = undeal_rows(seq_units, deal, returned, given)[None]
-    out_wq, out_wk, out_wv, out_wo, out_gain_one = finish(attn_grads, ((rows, cols),) * 4, own)
+    attn_share = scatter_permute(keep, send)
+    out_wq, out_wk, out_wv, out_wo, out_gain_one = finish(
+        attn_share, ((rows, cols),) * 4, own, shard_count
+    )
+    out_wg, out_wu, out_wd, out_gain_two = finish(
+        ffn_share, ((rows, wide), (rows, wide), (down, cols)), own, shard_count
+    )
     return (
         layer_out.reshape(1, 1, span, width),
         grad_x,

time: 453 us -> 414 us (0.914)
  waiting for transfers between devices: 244 us -> 194 us
  other arithmetic: 3.5 us -> 9.26 us
    reduce_scatter x2 -> x1, waiting for transfers between devices: 143 us -> 11.5 us  [scatter_queue(): lax.psum_scatter(packed.reshape(-1, LANES), 'shard', scatter_dimension=0,...]
    ppermute x0 -> x5, waiting for transfers between devices: none -> 80.7 us  [the longest x1 59.5 us: to_side(): return lax.ppermute(value, 'shard', [(i, i ^ 2) for i in range(count)])]
    convert_element_type x0 -> x3, other arithmetic: none -> 5.24 us  [the longest x1 2.23 us: scatter_permute(): pass_on = (keep[along:].astype(f32) + came[along:].astype(f32)).astype(bf16)]
  transfers between devices with their start and end apart: 8 -> 12, of which waited for: 6 -> 8; matrix products, arithmetic and copies ran while one was open for 1% -> 3% of each run, Pallas kernels for 25% -> 28%
where the time goes in v3:
time: 414 us; the launch traced here: 413 us
  waiting for transfers between devices  194 us (47%)
  Pallas kernels  169 us (41%)
  starting transfers between devices  18.6 us (4%)
  between operations  14 us (3%)
  other arithmetic  9.26 us (2%)
  local copies, waits for them, and re-layouts  8.21 us (2%)
    ppermute x1, waiting for transfers between devices, to_side(): return lax.ppermute(value, 'shard', [(i, i ^ 2) for i in range(count)])  59.5 us
    pallas_call x1, Pallas kernels, attend_back(): pl.pallas_call(functools.partial(attend_back_kernel, unit_max, 512), grid...  58.2 us
    pallas_call x1, Pallas kernels, ffn_both(): pl.pallas_call(functools.partial(ffn_kernel, unit_max), grid=(blocks,), o...  52.8 us
    all_gather x2, waiting for transfers between devices, gather_packed(): whole = lax.all_gather(packed, 'shard', axis=0, tiled=True)  52 us
    all_to_all x1, waiting for transfers between devices, shards(): lax.all_to_all(outgoing, 'shard', split_axis=0, concat_axis=0, tiled=True)  47.3 us
    pallas_call x1, Pallas kernels, attend_forward(): pl.pallas_call(functools.partial(attend_kernel, unit_max, 512), grid=(pai...  26.2 us
    ppermute x3, waiting for transfers between devices, along_z(): lax.ppermute(value, 'shard', [(i, (i + 4 * step) % count) for i in range(...  20.2 us
    reduce_scatter x1, waiting for transfers between devices, scatter_queue(): lax.psum_scatter(packed.reshape(-1, LANES), 'shard', scatter_dimension=0,...  11.5 us
  transfers between devices with their start and end apart: 12, of which 8 were waited for; matrix products, arithmetic and copies ran while one was open for 3% of the time, Pallas kernels for 28%

profile of v3, /device:TPU:0, one launch (start us, length us, event | category | flops | bytes accessed | tf_op | source)
XLA Modules:
  0.0 412.7 jit_solution(6845366285604522298)
XLA Ops:
  7.2 0.0 copy-start.5
  7.2 0.0 copy-start.6
  7.2 0.0 all-gather.3.cloned.1.call-start
  7.2 1.0 reshape.82
  8.3 0.9 reshape.81
  9.2 0.0 copy-start.7
  9.2 1.0 reshape.80
  10.2 0.9 reshape.79
  11.1 0.7 pad_maximum_fusion.1
  11.9 0.0 all-gather.3.cloned.1.call-update
  11.9 0.0 all-gather.5.cloned.1.call-start
  12.0 0.0 copy-done.5
  12.0 0.2 copy.40
  12.1 0.2 copy.41
  12.3 0.0 copy-done.6
  12.5 0.9 pad_maximum_fusion
  13.3 0.0 all-gather.5.cloned.1.call-update
  13.4 6.6 %deal_rows.1 = bf16[16,64,768]{2,1,0:T(8,128)(2,1)} custom-call(s32[1,16]{1,0:T(1,128)} %units_ref.3, s32[1,16]{1,0:T(1,128)} %order_ref.3, bf16[512,768]{1,0:T(8,128)(2,1)} %bitcast.69), custom_call_target="tpu_custom_call" | custom-call | tf_op jit(solution)/shard_map/deal_rows/pallas_call | solution.py:89
  20.0 7.5 %all-to-all-start = ((bf16[16,64,768]{2,1,0:T(8,128)(2,1)}), bf16[16,64,768]{2,1,0:T(8,128)(2,1)S(1)}, u32[]{:S(2)}, u32[]{:S(2)}) async-start(bf16[16,64,768]{2,1,0:T(8,128)(2,1)} %deal_rows.1), calls=%async_computation | async-start | bytes 3145728 | tf_op jit(solution)/shard_map/all_to_all | solution.py:822
  27.5 0.0 reduce-scatter.2.cloned.1.call-start
  27.6 0.0 copy-done.8
  27.6 0.6 reshape.78.gain_ref
  28.2 0.0 copy-done.9
  28.2 0.6 reshape.84.gain_ref
  28.8 0.6 fusion.5
  29.4 1.3 fusion.6
  30.7 47.3 %all-to-all-done = bf16[16,64,768]{2,1,0:T(8,128)(2,1)S(1)} async-done(((bf16[16,64,768]{2,1,0:T(8,128)(2,1)}), bf16[16,64,768]{2,1,0:T(8,128)(2,1)S(1)}, u32[]{:S(2)}, u32[]{:S(2)}) %all-to-all-start) | async-done | bytes 1572896 | tf_op jit(solution)/shard_map/all_to_all | solution.py:822
  78.0 10.6 %all-gather.3.cloned.1.call-done = bf16[9216,256]{1,0:T(8,128)(2,1)} async-done(((bf16[576,256]{1,0:T(8,128)(2,1)}), bf16[9216,256]{1,0:T(8,128)(2,1)}) %all-gather.3.cloned.1.call-update) | async-done | bytes 4718608 | tf_op jit(solution)/shard_map/all_gather | solution.py:794
  88.6 10.8 %make_qkv.1 = (bf16[1024,768]{1,0:T(8,128)(2,1)}, bf16[1024,2304]{1,0:T(8,128)(2,1)}) custom-call(bf16[1024,768]{1,0:T(8,128)(2,1)} %bitcast.53, f32[1,768]{1,0:T(1,128)} %reshape.78.gain_ref, bf16[16,576,256]{2,1,0:T(8,128)(2,1)} %bitcast.56), custom_call_target="tpu_custom_call" | custom-call | flops 3623878656 | bytes 14680064 | tf_op jit(solution)/shard_map/make_qkv/pallas_call | solution.py:149
  99.4 26.2 %attend_forward.1 = (bf16[1024,768]{1,0:T(8,128)(2,1)}, f32[6,8,1024]{2,1,0:T(8,128)}) custom-call(s32[1]{0:T(128)} %bitcast.2.count_ref, bf16[1024,2304]{1,0:T(8,128)(2,1)} %get-tuple-element.33.q_ref.k_ref.v_ref, bf16[1024,2304]{1,0:T(8,128)(2,1)} %get-tuple-element.33.q_ref.k_ref.v_ref, bf16[1024,2304]{1,0:T(8,128)(2,1)} %get-tuple-element.33.q_ref.k_ref.v_ref), custom_call_target="tpu_custom_call" | custom-call | flops 3221225472 | bytes 8388608 | tf_op jit(solution)/shard_map/attend_forward/pallas_call | solution.py:222
  125.6 6.0 %out_project.1 = (f32[1024,768]{1,0:T(8,128)}, bf16[1024,768]{1,0:T(8,128)(2,1)}) custom-call(bf16[1024,768]{1,0:T(8,128)(2,1)} %bitcast.54, bf16[1024,768]{1,0:T(8,128)(2,1)} %get-tuple-element.34.o_ref, bf16[16,576,256]{2,1,0:T(8,128)(2,1)} %bitcast.57, f32[1,768]{1,0:T(1,128)} %reshape.84.gain_ref), custom_call_target="tpu_custom_call" | custom-call | flops 1207959552 | bytes 9437184 | tf_op jit(solution)/shard_map/out_project/pallas_call | solution.py:257
  131.6 41.4 %all-gather.5.cloned.1.call-done = bf16[18432,256]{1,0:T(8,128)(2,1)} async-done(((bf16[1152,256]{1,0:T(8,128)(2,1)}), bf16[18432,256]{1,0:T(8,128)(2,1)}) %all-gather.5.cloned.1.call-update) | async-done | bytes 9437200 | tf_op jit(solution)/shard_map/all_gather | solution.py:794
  172.9 52.8 %ffn_both.1 = (bf16[1024,768]{1,0:T(8,128)(2,1)}, f32[1024,768]{1,0:T(8,128)}, bf16[1024,768]{1,0:T(8,128)(2,1)}, bf16[16,1168,256]{2,1,0:T(8,128)(2,1)}) custom-call(s32[1]{0:T(128)} %bitcast.2.count_ref, f32[1024,768]{1,0:T(8,128)} %get-tuple-element.35.h_ref, bf16[1024,768]{1,0:T(8,128)(2,1)} %get-tuple-element.36.n2_ref, bf16[1024,768]{1,0:T(8,128)(2,1)} %bitcast.84, ...), custom_call_target="tpu_custom_call" | custom-call | flops 28991029248 | bytes 37748736 | tf_op jit(solution)/shard_map/ffn_both/pallas_call | solution.py:434
  225.8 0.0 reduce-scatter.2.cloned.1.call-update
  225.8 0.5 fusion.11.place_ref
  226.3 58.2 %attend_back.1 = (bf16[1024,768]{1,0:T(8,128)(2,1)}, bf16[8,592,256]{2,1,0:T(8,128)(2,1)}, bf16[8,592,256]{2,1,0:T(8,128)(2,1)}) custom-call(s32[1]{0:T(128)} %bitcast.2.count_ref, s32[16]{0:T(128)} %fusion.11.place_ref, bf16[1024,2304]{1,0:T(8,128)(2,1)} %get-tuple-element.33.q_ref.k_ref.v_ref, bf16[1024,2304]{1,0:T(8,128)(2,1)} %get-tuple-element.33.q_ref.k_ref.v_ref, ...), custom_call_target="tpu_custom_call" | custom-call | flops 17716740096 | bytes 25165824 | tf_op jit(solution)/shard_map/attend_back/pallas_call | solution.py:654
  284.5 0.3 collective-permute-start
  284.8 3.7 all-to-all-start.1
  288.6 1.0 collective-permute-done
  289.6 2.2 add_convert_fusion.1
  291.8 0.8 collective-permute-start.1
  292.6 59.5 %collective-permute-done.1 = bf16[4,592,256]{2,1,0:T(8,128)(2,1)S(1)} collective-permute-done((bf16[4,592,256]{2,1,0:T(8,128)(2,1)S(1)}, bf16[4,592,256]{2,1,0:T(8,128)(2,1)S(1)}, u32[]{:S(2)}, u32[]{:S(2)}) %collective-permute-start.1) | collective-permute-done | bytes 1212448 | tf_op jit(solution)/shard_map/ppermute | solution.py:737
  352.1 0.0 copy-done.2
  352.1 1.7 add_convert_fusion
  353.8 0.8 slice_bitcast_fusion.2
  354.6 2.7 collective-permute-start.4
  357.3 0.0 collective-permute-start.3
  357.3 0.6 collective-permute-start.2
  357.8 11.5 %reduce-scatter.2.cloned.1.call-done.mine_ref = bf16[1168,256]{1,0:T(8,128)(2,1)} async-done(((bf16[18688,256]{1,0:T(8,128)(2,1)}), bf16[1168,256]{1,0:T(8,128)(2,1)}) %reduce-scatter.2.cloned.1.call-update) | async-done | bytes 598032 | tf_op jit(solution)/shard_map/reduce_scatter | solution.py:746
  369.3 1.4 collective-permute-start.6
  370.8 0.0 collective-permute-done.4
  370.8 20.2 %collective-permute-done.3 = bf16[592,256]{1,0:T(8,128)(2,1)} collective-permute-done((bf16[592,256]{1,0:T(8,128)(2,1)S(1)}, bf16[592,256]{1,0:T(8,128)(2,1)}, u32[]{:S(2)}, u32[]{:S(2)}) %collective-permute-start.3) | collective-permute-done | bytes 303136 | tf_op jit(solution)/shard_map/ppermute | solution.py:742
  390.9 0.0 collective-permute-done.2
  390.9 1.3 fusion.2.mine_ref
  392.2 0.0 copy-start.3
  392.3 1.5 collective-permute-start.5
  393.7 0.0 all-to-all-done.1.back_ref
  393.7 1.2 copy-done
  394.9 4.1 %undeal_rows.1 = bf16[512,768]{1,0:T(8,128)(2,1)} custom-call(s32[1,16]{1,0:T(1,128)} %units_ref.3, s32[1,16]{1,0:T(1,128)} %order_ref.3, bf16[16,64,768]{2,1,0:T(8,128)(2,1)} %copy-done), custom_call_target="tpu_custom_call" | custom-call | tf_op jit(solution)/shard_map/undeal_rows/pallas_call | solution.py:100
  399.1 2.1 collective-permute-done.5.other_ref
  401.2 0.7 copy-done.4
  401.9 1.9 finish.2
  403.8 0.0 collective-permute-done.6.other_ref
  403.8 2.4 finish.3
  (21 shorter events, 0.2 us)
Async XLA Ops:
  7.2 4.8 %copy-start.5 = (bf16[128,768]{1,0:T(8,128)(2,1)S(1)}, bf16[128,768]{1,0:T(8,128)(2,1)}, u32[]{:S(2)}) copy-start(bf16[128,768]{1,0:T(8,128)(2,1)} %param.24) | copy-start | bytes 589828
  7.2 5.1 %copy-start.6 = (bf16[48,2048]{1,0:T(8,128)(2,1)S(1)}, bf16[48,2048]{1,0:T(8,128)(2,1)}, u32[]{:S(2)}) copy-start(bf16[48,2048]{1,0:T(8,128)(2,1)} %param.23) | copy-start | bytes 589828
  7.2 81.4 %all-gather.3.cloned.1.call-start = ((), (), s32[]{:S(2)}) async-start(), calls=%async_computation.3 | async-start | bytes 5013504 | tf_op jit(solution)/shard_map/all_gather | solution.py:794
  9.2 3.2 copy-start.7
  11.9 161.0 %all-gather.5.cloned.1.call-start = ((), (), s32[]{:S(2)}) async-start(), calls=%async_computation.4 | async-start | bytes 10027008 | tf_op jit(solution)/shard_map/all_gather | solution.py:794
  20.0 7.6 %copy-start.8 = (f32[768]{0:T(1024)S(1)}, f32[768]{0:T(1024)}, u32[]{:S(2)}) copy-start(f32[768]{0:T(1024)} %param.16) | copy-start | bytes 9220
  20.0 8.2 %copy-start.9 = (f32[768]{0:T(1024)S(1)}, f32[768]{0:T(1024)}, u32[]{:S(2)}) copy-start(f32[768]{0:T(1024)} %param.21) | copy-start | bytes 9220
  20.0 8.8 %copy-start.11 = (s32[1,16]{1,0:T(1,128)S(1)}, s32[1,16]{1,0:T(1,128)}, u32[]{:S(2)}) copy-start(s32[1,16]{1,0:T(1,128)} %order_ref.3) | copy-start | bytes 196
  20.0 9.4 %copy-start.10 = (s32[1,16]{1,0:T(1,128)S(1)}, s32[1,16]{1,0:T(1,128)}, u32[]{:S(2)}) copy-start(s32[1,16]{1,0:T(1,128)} %units_ref.3) | copy-start | bytes 196
  20.0 58.0 %all-to-all-start = ((bf16[16,64,768]{2,1,0:T(8,128)(2,1)}), bf16[16,64,768]{2,1,0:T(8,128)(2,1)S(1)}, u32[]{:S(2)}, u32[]{:S(2)}) async-start(bf16[16,64,768]{2,1,0:T(8,128)(2,1)} %deal_rows.1), calls=%async_computation | async-start | bytes 3145728 | tf_op jit(solution)/shard_map/all_to_all | solution.py:822
  27.5 341.8 %reduce-scatter.2.cloned.1.call-start = ((), (), s32[]{:S(2)}) async-start(), calls=%async_computation.5 | async-start | bytes 10166272 | tf_op jit(solution)/shard_map/reduce_scatter | solution.py:746
  78.0 10.6 %copy-start.1 = (bf16[16,64,768]{2,1,0:T(8,128)(2,1)}, bf16[16,64,768]{2,1,0:T(8,128)(2,1)S(1)}, u32[]{:S(2)}) copy-start(bf16[16,64,768]{2,1,0:T(8,128)(2,1)S(1)} %all-to-all-done) | copy-start | bytes 4718596
  284.5 5.0 %collective-permute-start = (bf16[8,592,256]{2,1,0:T(8,128)(2,1)}, bf16[8,592,256]{2,1,0:T(8,128)(2,1)}, u32[]{:S(2)}, u32[]{:S(2)}) collective-permute-start(bf16[8,592,256]{2,1,0:T(8,128)(2,1)} %get-tuple-element.44), channel_id=1, source_target_pairs={{0,2},{2,0},{4,6},{6,4},{8,10},{10,8},{12,14},{14,12},{16,18},{18,... | collective-permute-start | bytes 7274504 | tf_op jit(solution)/shard_map/ppermute | solution.py:732
  284.8 108.9 %all-to-all-start.1 = ((bf16[16,64,768]{2,1,0:T(8,128)(2,1)}), bf16[16,64,768]{2,1,0:T(8,128)(2,1)S(1)}, u32[]{:S(2)}, u32[]{:S(2)}) async-start(bf16[16,64,768]{2,1,0:T(8,128)(2,1)} %bitcast.62), calls=%async_computation.1 | async-start | bytes 3145728 | tf_op jit(solution)/shard_map/all_to_all | solution.py:844
  289.6 62.5 %copy-start.2 = (bf16[8,592,256]{2,1,0:T(8,128)(2,1)S(1)}, bf16[8,592,256]{2,1,0:T(8,128)(2,1)}, u32[]{:S(2)}) copy-start(bf16[8,592,256]{2,1,0:T(8,128)(2,1)} %get-tuple-element.43) | copy-start | bytes 7274500
  291.8 60.3 %collective-permute-start.1 = (bf16[4,592,256]{2,1,0:T(8,128)(2,1)S(1)}, bf16[4,592,256]{2,1,0:T(8,128)(2,1)S(1)}, u32[]{:S(2)}, u32[]{:S(2)}) collective-permute-start(bf16[4,592,256]{2,1,0:T(8,128)(2,1)S(1)} %add_convert_fusion.1), channel_id=1, source_target_pairs={{0,4},{2,6},{4,0},{6,2},{8,12},{10,14},{12,8},{14,10},{16,20},{18,... | collective-permute-start | bytes 3637256 | tf_op jit(solution)/shard_map/ppermute | solution.py:737
  354.6 16.2 %collective-permute-start.4 = (bf16[592,256]{1,0:T(8,128)(2,1)}, bf16[592,256]{1,0:T(8,128)(2,1)}, u32[]{:S(2)}, u32[]{:S(2)}) collective-permute-start(bf16[592,256]{1,0:T(8,128)(2,1)} %get-tuple-element.56), channel_id=1, source_target_pairs={{0,24},{2,26},{4,28},{6,30},{8,0},{10,2},{12,4},{14,6},{16,8},{18,... | collective-permute-start | bytes 909320 | tf_op jit(solution)/shard_map/ppermute | solution.py:742
  357.3 33.7 %collective-permute-start.3 = (bf16[592,256]{1,0:T(8,128)(2,1)S(1)}, bf16[592,256]{1,0:T(8,128)(2,1)}, u32[]{:S(2)}, u32[]{:S(2)}) collective-permute-start(bf16[592,256]{1,0:T(8,128)(2,1)S(1)} %get-tuple-element.57), channel_id=1, source_target_pairs={{0,16},{2,18},{4,20},{6,22},{8,24},{10,26},{12,28},{14,30},{16,0},... | collective-permute-start | bytes 909320 | tf_op jit(solution)/shard_map/ppermute | solution.py:742
  357.3 33.7 %collective-permute-start.2 = (bf16[592,256]{1,0:T(8,128)(2,1)S(1)}, bf16[592,256]{1,0:T(8,128)(2,1)}, u32[]{:S(2)}, u32[]{:S(2)}) collective-permute-start(bf16[592,256]{1,0:T(8,128)(2,1)S(1)} %get-tuple-element.55), channel_id=1, source_target_pairs={{0,8},{2,10},{4,12},{6,14},{8,16},{10,18},{12,20},{14,22},{16,24},... | collective-permute-start | bytes 909320 | tf_op jit(solution)/shard_map/ppermute | solution.py:742
  369.3 34.5 %collective-permute-start.6 = (bf16[1168,256]{1,0:T(8,128)(2,1)}, bf16[1168,256]{1,0:T(8,128)(2,1)}, u32[]{:S(2)}, u32[]{:S(2)}) collective-permute-start(bf16[1168,256]{1,0:T(8,128)(2,1)} %reduce-scatter.2.cloned.1.call-done.mine_ref), channel_id=1, source_target_pairs={{0,1},{1,0},{2,3},{3,2},{4,5},{5,4},{6,7},{7,6},{8,9},{9,8},{10,11... | collective-permute-start | bytes 1794056 | tf_op jit(solution)/shard_map/ppermute | solution.py:769
  392.2 8.9 %copy-start.3 = (bf16[592,256]{1,0:T(8,128)(2,1)}, bf16[592,256]{1,0:T(8,128)(2,1)S(1)}, u32[]{:S(2)}) copy-start(bf16[592,256]{1,0:T(8,128)(2,1)S(1)} %fusion.2.mine_ref) | copy-start | bytes 909316
  392.3 8.9 %collective-permute-start.5 = (bf16[592,256]{1,0:T(8,128)(2,1)S(1)}, bf16[592,256]{1,0:T(8,128)(2,1)S(1)}, u32[]{:S(2)}, u32[]{:S(2)}) collective-permute-start(bf16[592,256]{1,0:T(8,128)(2,1)S(1)} %fusion.2.mine_ref), channel_id=1, source_target_pairs={{0,1},{1,0},{2,3},{3,2},{4,5},{5,4},{6,7},{7,6},{8,9},{9,8},{10,11... | collective-permute-start | bytes 909320 | tf_op jit(solution)/shard_map/ppermute | solution.py:769
  393.7 1.2 copy-start
  401.2 0.7 copy-start.4
Sparse Core Ops, SparseCore 0:
  12.0 76.5 all-gather.2
  91.4 81.4 all-gather.4
  225.9 143.3 reduce-scatter.1

commit v4 on v3

--- a/solution.py
+++ b/solution.py
@@ -45,34 +45,30 @@
     return start, count
 
 
-def deal_kernel(units_ref, order_ref, rows_ref, out_ref):
-    shard_count, unit_max, _ = out_ref.shape
-    given = rows_ref.shape[0]
+def pick_rows(units_ref, order_ref, pick_ref, shard_count, unit_max):
+    given = pick_ref.shape[1]
     row = lax.broadcasted_iota(jnp.int32, (unit_max, given), 0)
-    col = lax.broadcasted_iota(jnp.int32, (unit_max, given), 1)
+    ahead = lax.broadcasted_iota(jnp.int32, (unit_max, given), 1) - row
 
     def step(slot, carry):
         start, count = slot_start(units_ref, order_ref, slot, shard_count)
-        pick = jnp.where((col - start == row) & (row < count), 1.0, 0.0).astype(bf16)
-        out_ref[slot] = plain_dot(pick, rows_ref[...]).astype(bf16)
+        pick = jnp.where((ahead == start) & (row < count), 1.0, 0.0).astype(bf16)
+        pick_ref[pl.ds(pl.multiple_of(slot * unit_max, unit_max), unit_max), :] = pick
         return carry
 
     lax.fori_loop(0, shard_count, step, 0)
+
+
+def deal_kernel(units_ref, order_ref, rows_ref, out_ref, pick_ref):
+    shard_count, unit_max, width = out_ref.shape
+    pick_rows(units_ref, order_ref, pick_ref, shard_count, unit_max)
+    found = plain_dot(pick_ref[...], rows_ref[...]).astype(bf16)
+    out_ref[...] = found.reshape(shard_count, unit_max, width)
 
 
 def undeal_kernel(units_ref, order_ref, back_ref, out_ref, pick_ref):
     shard_count, unit_max, width = back_ref.shape
-    given = out_ref.shape[0]
-    row = lax.broadcasted_iota(jnp.int32, (unit_max, given), 0)
-    col = lax.broadcasted_iota(jnp.int32, (unit_max, given), 1)
-
-    def step(slot, carry):
-        start, count = slot_start(units_ref, order_ref, slot, shard_count)
-        pick = jnp.where((col - start == row) & (row < count), 1.0, 0.0).astype(bf16)
-        pick_ref[pl.ds(pl.multiple_of(slot * unit_max, unit_max), unit_max), :] = pick
-        return carry
-
-    lax.fori_loop(0, shard_count, step, 0)
+    pick_rows(units_ref, order_ref, pick_ref, shard_count, unit_max)
     whole = back_ref[...].reshape(shard_count * unit_max, width)
     out_ref[...] = left_dot(pick_ref[...], whole).astype(bf16)
 
@@ -91,6 +87,7 @@
         out_shape=jax.ShapeDtypeStruct((shard_count, unit_max, rows.shape[1]), bf16),
         in_specs=[smem(), smem(), vmem()],
         out_specs=vmem(),
+        scratch_shapes=[pltpu.VMEM((shard_count * unit_max, rows.shape[0]), bf16)],
         name="deal_rows",
     )(units, order, rows)
 
@@ -129,43 +126,66 @@
     return ref[...].reshape(parts * rows, lanes)
 
 
-def qkv_kernel(x_ref, gain_ref, w_ref, n1_ref, qkv_ref):
+def qkv_kernel(me_ref, x_ref, gain_ref, a_ref, b_ref, fa_ref, fb_ref, n1_ref, qkv_ref, w_ref):
     block = pl.program_id(0)
+    along = a_ref.shape[0]
+    width = n1_ref.shape[1]
+    me = me_ref[0]
+    core = lax.rem(me, 2)
+    side = lax.rem(lax.div(me, 2), 2)
+    height = lax.div(me, 4)
 
     @pl.when(block == 0)
     def _():
         rows = x_ref[...].astype(f32)
         n1_ref[...] = (rows * inverse_rms(rows) * gain_ref[...]).astype(bf16)
 
-    factor = jnp.where(block < n1_ref.shape[1] // LANES, HD ** (-0.5), 1.0)
-    made = plain_dot(n1_ref[...], whole_block(w_ref)).astype(bf16).astype(f32)
-    qkv_ref[...] = (made * factor).astype(bf16)
-
-
-def make_qkv(tokens, gain, packed, rows):
+    for step in range(along):
+        there = lax.rem(height - step + along, along) * 4
+        w_ref[there + 2 * side + core] = a_ref[step]
+        w_ref[there + 2 * side + 1 - core] = fa_ref[step]
+        w_ref[there + 2 * (1 - side) + core] = b_ref[step]
+        w_ref[there + 2 * (1 - side) + 1 - core] = fb_ref[step]
+
+    @pl.when(block < 3 * width // LANES)
+    def _():
+        factor = jnp.where(block < width // LANES, HD ** (-0.5), 1.0)
+        made = plain_dot(n1_ref[...], whole_block(w_ref)).astype(bf16).astype(f32)
+        qkv_ref[...] = (made * factor).astype(bf16)
+
+
+def make_qkv(me, tokens, gain, pieces, rows):
     span, width = tokens.shape
-    parts = packed.shape[0]
+    along = pieces[0].shape[0]
     blocks = 3 * width // LANES
+    everything = 4 * width // LANES
+    piece = pl.BlockSpec((along, rows, LANES), lambda j: (0, j, 0))
     return pl.pallas_call(
         qkv_kernel,
-        grid=(blocks,),
+        grid=(everything,),
         out_shape=(
             jax.ShapeDtypeStruct((span, width), bf16),
             jax.ShapeDtypeStruct((span, 3 * width), bf16),
+            jax.ShapeDtypeStruct((4 * along, everything * rows, LANES), bf16),
         ),
         in_specs=[
+            smem(),
             const_block((span, width)),
             const_block((1, width)),
-            pl.BlockSpec((parts, rows, LANES), lambda j: (0, j, 0)),
+            piece,
+            piece,
+            piece,
+            piece,
         ],
         out_specs=(
             const_block((span, width)),
-            pl.BlockSpec((span, LANES), lambda j: (0, j)),
+            pl.BlockSpec((span, LANES), lambda j: (0, jnp.minimum(j, blocks - 1))),
+            pl.BlockSpec((4 * along, rows, LANES), lambda j: (0, j, 0)),
         ),
         compiler_params=params(),
         cost_estimate=cost(6 * span * width * width, 14 << 20),
         name="make_qkv",
-    )(tokens, gain, packed)
+    )(me, tokens, gain, *pieces)
 
 
 def live_bias(count, span, unit_max):
@@ -698,21 +718,30 @@
     )(count, place, qkv, qkv, qkv, mixed, lse, n1, tokens, g_h, g_hb, gain, packed, packed, packed, packed)
 
 
-def finish_kernel(layout, own, gain_cols, me_ref, mine_ref, other_ref, *outs):
+def finish_kernel(layout, own, gain_cols, halves, me_ref, mine_ref, other_ref, *outs):
+    outs, sum_ref = outs[:-1], outs[-1]
+    if halves:
+        rows = mine_ref.shape[0]
+        first = me_ref[1]
+        sum_ref[pl.ds(pl.multiple_of(first * rows, 8), rows), :] = mine_ref[...].astype(f32)
+        sum_ref[pl.ds(pl.multiple_of((1 - first) * rows, 8), rows), :] = other_ref[...].astype(f32)
+    else:
+        sum_ref[...] = mine_ref[...].astype(f32) + other_ref[...].astype(f32)
     begin = 0
     for (rows, blocks), out_ref in zip(layout, outs[:-1]):
         for c in range(blocks):
-            at = slice(begin, begin + rows)
-            out_ref[:, c * LANES : (c + 1) * LANES] = mine_ref[at].astype(f32) + other_ref[at].astype(f32)
+            out_ref[:, c * LANES : (c + 1) * LANES] = sum_ref[begin : begin + rows]
             begin += rows
-    at = slice(begin, begin + GAIN_ROWS)
+    gains = sum_ref[begin : begin + GAIN_ROWS]
     row = lax.broadcasted_iota(jnp.int32, (GAIN_ROWS, own), 0)
     from_lane = lax.broadcasted_iota(jnp.int32, (LANES, own), 0)
     to_lane = lax.broadcasted_iota(jnp.int32, (LANES, own), 1)
+    high = gains.astype(bf16)
+    low = (gains - high.astype(f32)).astype(bf16)
     total = jnp.zeros((GAIN_ROWS, own), f32)
     for c in range(gain_cols):
         pick = jnp.where(from_lane + c * LANES == to_lane + me_ref[0] * own, 1.0, 0.0).astype(bf16)
-        found = plain_dot(mine_ref[at], pick) + plain_dot(other_ref[at], pick)
+        found = plain_dot(high, pick) + plain_dot(low, pick)
         total += jnp.where(row == c, found, 0.0)
     outs[-1][...] = jnp.sum(total, axis=0, keepdims=True)
 
@@ -746,20 +775,39 @@
     return lax.psum_scatter(packed.reshape(-1, LANES), "shard", scatter_dimension=0, tiled=True)
 
 
-def scatter_permute(keep, send):
+def to_replica(value):
+    return lax.ppermute(value, "replica", [(0, 1), (1, 0)])
+
+
+def half_of(value, which):
+    rows = value.shape[1] // 2
+    return lax.dynamic_slice_in_dim(value, which * rows, rows, axis=1)
+
+
+def scatter_permute(keep, send, later):
     along = keep.shape[0] // 2
+    pair = lax.axis_size("replica") == 2
     came = to_core(send)
-    pass_on = (keep[along:].astype(f32) + came[along:].astype(f32)).astype(bf16)
+    parts = (keep, came)
+    if pair:
+        mine = lax.axis_index("replica")
+        pass_y = sum(half_of(p, 1 - mine).astype(f32) for p in parts).astype(bf16)
+        came_y = to_replica(pass_y)
+        parts = tuple(half_of(p, mine) for p in parts) + (came_y,)
+    pass_on = sum(p[along:].astype(f32) for p in parts).astype(bf16)
     crossed = to_side(pass_on)
-    column = (keep[:along].astype(f32) + came[:along].astype(f32) + crossed.astype(f32)).astype(bf16)
+    column = (sum(p[:along].astype(f32) for p in parts) + crossed.astype(f32)).astype(bf16)
     found = [along_z(column[k], k) for k in range(1, along)]
     total = column[0].astype(f32)
     for piece in found:
         total = total + piece.astype(f32)
-    return total.astype(bf16)
-
-
-def finish(share, layout, own, parts):
+    total, later = lax.optimization_barrier((total.astype(bf16), later))
+    if pair:
+        return total, to_replica(total), later
+    return *replica_rounds(total), later
+
+
+def replica_rounds(share):
     count = lax.axis_size("replica")
     step = 1
     other = jnp.zeros_like(share)
@@ -768,13 +816,19 @@
             share = (share.astype(f32) + other.astype(f32)).astype(bf16)
         other = lax.ppermute(share, "replica", [(i, i ^ step) for i in range(count)])
         step *= 2
-    me = lax.axis_index("shard").reshape(1)
+    return share, other
+
+
+def finish(share, other, layout, own, parts, halves):
+    me = jnp.stack([lax.axis_index("shard"), lax.axis_index("replica")]).astype(jnp.int32)
+    rows = share.shape[0] * (2 if halves else 1)
     outs = pl.pallas_call(
-        functools.partial(finish_kernel, layout, own, parts * own // LANES),
+        functools.partial(finish_kernel, layout, own, parts * own // LANES, halves),
         out_shape=tuple(jax.ShapeDtypeStruct((r, b * LANES), f32) for r, b in layout)
         + (jax.ShapeDtypeStruct((1, own), f32),),
         in_specs=[smem(), vmem(), vmem()],
         out_specs=(vmem(),) * (len(layout) + 1),
+        scratch_shapes=[pltpu.VMEM((rows, LANES), f32)],
         compiler_params=params(),
         cost_estimate=cost(0, 4 << 20),
         name="finish",
@@ -789,8 +843,11 @@
     return split.reshape(parts, cols * rows, LANES)
 
 
-def gather_packed(mats):
-    packed = jnp.concatenate([to_blocks(m, 1)[0] for m in mats], axis=0)
+def pack_own(mats):
+    return jnp.concatenate([to_blocks(m, 1)[0] for m in mats], axis=0)
+
+
+def gather_queue(packed):
     whole = lax.all_gather(packed, "shard", axis=0, tiled=True)
     return whole.reshape(-1, packed.shape[0], LANES)
 
@@ -822,12 +879,20 @@
     arrived = lax.all_to_all(outgoing, "shard", split_axis=0, concat_axis=0, tiled=True)
     own_seq = jnp.sum(jnp.where(slot_ids == my_index, deal[0], 0))
     count = jnp.sum(jnp.where(slot_ids == own_seq, seq_units[0], 0)).reshape(1)
-    attn_pack = gather_packed((w_query, w_key, w_value, w_out))
-    ffn_pack = gather_packed((w_gate, w_up, w_down))
+    attn_own = pack_own((w_query, w_key, w_value, w_out))
+    column = [along_z(attn_own, k) for k in range(1, shard_count // 4)]
+    ffn_own = pack_own((w_gate, w_up, w_down))
+    ffn_own, attn_own, _, *column = lax.optimization_barrier((ffn_own, attn_own, outgoing, *column))
+    ffn_pack = gather_queue(ffn_own)
+    here = jnp.stack([attn_own, *column])
+    beside = to_side(here)
+    pieces = (here, beside, to_core(here), to_core(beside))
     tokens = arrived.reshape(span, width)
     gain_one = gain_attn.reshape(1, width)
     gain_two = gain_ffn.reshape(1, width)
-    n1, qkv = make_qkv(tokens, gain_one, attn_pack, rows)
+    n1, qkv, attn_pack = make_qkv(
+        lax.axis_index("shard").reshape(1), tokens, gain_one, pieces, rows
+    )
     mixed, lse = attend_forward(count, qkv, unit_max)
     hidden, n2 = out_project(tokens, mixed, attn_pack, gain_two, rows)
     layer_out, g_h, g_hb, ffn_grads = ffn_both(
@@ -845,12 +910,21 @@
         g_x.reshape(shard_count, unit_max, width), "shard", split_axis=0, concat_axis=0, tiled=True
     )
     grad_x = undeal_rows(seq_units, deal, returned, given)[None]
-    attn_share = scatter_permute(keep, send)
+    attn_mine, attn_other, ffn_share = scatter_permute(keep, send, ffn_share)
     out_wq, out_wk, out_wv, out_wo, out_gain_one = finish(
-        attn_share, ((rows, cols),) * 4, own, shard_count
+        attn_mine,
+        attn_other,
+        ((rows, cols),) * 4,
+        own,
+        shard_count,
+        lax.axis_size("replica") == 2,
     )
     out_wg, out_wu, out_wd, out_gain_two = finish(
-        ffn_share, ((rows, wide), (rows, wide), (down, cols)), own, shard_count
+        *replica_rounds(ffn_share),
+        ((rows, wide), (rows, wide), (down, cols)),
+        own,
+        shard_count,
+        False,
     )
     return (
         layer_out.reshape(1, 1, span, width),

time: 414 us -> 378 us (0.913)
  waiting for transfers between devices: 194 us -> 137 us
  starting transfers between devices: 18.6 us -> 32.8 us
    all_gather x2 -> x1, waiting for transfers between devices: 52 us -> 0.01 us  [gather_queue(): whole = lax.all_gather(packed, 'shard', axis=0, tiled=True)]
    all_to_all x1, waiting for transfers between devices: 47.3 us -> 0.01 us  [shards(): lax.all_to_all(outgoing, 'shard', split_axis=0, concat_axis=0, tiled=True)]
    ppermute x2 -> x3, waiting for transfers between devices: 2.07 us -> 33.4 us  [the longest x2 33.4 us: to_replica(): return lax.ppermute(value, 'replica', [(0, 1), (1, 0)])]
    ppermute x1 -> x2, waiting for transfers between devices: 59.5 us -> 73.7 us  [to_side(): return lax.ppermute(value, 'shard', [(i, i ^ 2) for i in range(count)])]
    reduce_scatter x1, waiting for transfers between devices: 11.5 us -> 0.02 us  [scatter_queue(): lax.psum_scatter(packed.reshape(-1, LANES), 'shard', scatter_dimension=0,...]
    ppermute x3 -> x6, starting transfers between devices: 3.24 us -> 11.2 us  [along_z(): lax.ppermute(value, 'shard', [(i, (i + 4 * step) % count) for i in range(...]
    ppermute x3 -> x6, waiting for transfers between devices: 20.2 us -> 25 us  [along_z(): lax.ppermute(value, 'shard', [(i, (i + 4 * step) % count) for i in range(...]
    pallas_call x1, Pallas kernels: 10.8 us -> 15 us  [make_qkv(): pl.pallas_call(qkv_kernel, grid=(everything,), out_shape=(jax.ShapeDtypeS...]
  transfers between devices with their start and end apart: 12 -> 18, of which waited for: 8 -> 9; matrix products, arithmetic and copies ran while one was open for 3% -> 4% of each run, Pallas kernels for 28% -> 31%
where the time goes in v4:
time: 378 us; the launch traced here: 376 us
  Pallas kernels  170 us (45%)
  waiting for transfers between devices  137 us (36%)
  starting transfers between devices  32.8 us (9%)
  between operations  14.4 us (4%)
  other arithmetic  12.2 us (3%)
  local copies, waits for them, and re-layouts  10.1 us (3%)
    ppermute x2, waiting for transfers between devices, to_side(): return lax.ppermute(value, 'shard', [(i, i ^ 2) for i in range(count)])  73.7 us
    pallas_call x1, Pallas kernels, attend_back(): pl.pallas_call(functools.partial(attend_back_kernel, unit_max, 512), grid...  57.5 us
    pallas_call x1, Pallas kernels, ffn_both(): pl.pallas_call(functools.partial(ffn_kernel, unit_max), grid=(blocks,), o...  52.8 us
    ppermute x2, waiting for transfers between devices, to_replica(): return lax.ppermute(value, 'replica', [(0, 1), (1, 0)])  33.4 us
    pallas_call x1, Pallas kernels, attend_forward(): pl.pallas_call(functools.partial(attend_kernel, unit_max, 512), grid=(pai...  26.2 us
    ppermute x6, waiting for transfers between devices, along_z(): lax.ppermute(value, 'shard', [(i, (i + 4 * step) % count) for i in range(...  25 us
    pallas_call x1, Pallas kernels, make_qkv(): pl.pallas_call(qkv_kernel, grid=(everything,), out_shape=(jax.ShapeDtypeS...  15 us
    ppermute x6, starting transfers between devices, along_z(): lax.ppermute(value, 'shard', [(i, (i + 4 * step) % count) for i in range(...  11.2 us
  transfers between devices with their start and end apart: 18, of which 9 were waited for; matrix products, arithmetic and copies ran while one was open for 4% of the time, Pallas kernels for 31%

profile of v4, /device:TPU:0, one launch (start us, length us, event | category | flops | bytes accessed | tf_op | source)
XLA Modules:
  0.0 376.1 jit_solution(2876572862384744452)
XLA Ops:
  7.2 0.0 all-gather.2.cloned.1.call-start
  7.2 1.0 reshape.79
  8.2 0.0 copy-start.9
  8.2 1.0 reshape.80
  9.2 0.9 reshape.81
  10.1 0.9 reshape.82
  11.1 3.1 collective-permute-start
  14.2 2.6 collective-permute-start.1
  16.8 1.3 collective-permute-start.2
  18.2 0.2 copy.40
  18.3 0.2 copy.41
  18.7 4.1 %deal_rows.1 = bf16[16,64,768]{2,1,0:T(8,128)(2,1)} custom-call(s32[1,16]{1,0:T(1,128)} %units_ref.3, s32[1,16]{1,0:T(1,128)} %order_ref.3, bf16[512,768]{1,0:T(8,128)(2,1)} %bitcast.68), custom_call_target="tpu_custom_call" | custom-call | tf_op jit(solution)/shard_map/deal_rows/pallas_call | solution.py:85
  22.8 0.9 pad_maximum_fusion.1
  23.6 0.6 collective-permute-done
  24.3 11.8 %collective-permute-done.1 = bf16[576,256]{1,0:T(8,128)(2,1)S(1)} collective-permute-done((bf16[576,256]{1,0:T(8,128)(2,1)S(1)}, bf16[576,256]{1,0:T(8,128)(2,1)S(1)}, u32[]{:S(2)}, u32[]{:S(2)}) %collective-permute-start.1) | collective-permute-done | bytes 294944 | tf_op jit(solution)/shard_map/ppermute | solution.py:771
  36.0 0.0 all-gather.2.cloned.1.call-update
  36.1 0.7 copy-done.6
  36.8 0.1 copy-done.7
  36.9 10.1 %all-to-all-start = ((bf16[16,64,768]{2,1,0:T(8,128)(2,1)}), bf16[16,64,768]{2,1,0:T(8,128)(2,1)S(1)}, u32[]{:S(2)}, u32[]{:S(2)}) async-start(bf16[16,64,768]{2,1,0:T(8,128)(2,1)} %deal_rows.1), calls=%async_computation | async-start | bytes 3145728 | tf_op jit(solution)/shard_map/all_to_all | solution.py:879
  47.0 0.0 copy-start.15
  47.0 0.0 copy-start.14
  47.0 0.0 reduce-scatter.2.cloned.1.call-start
  47.1 1.2 pad_maximum_fusion.a_ref
  48.3 2.0 collective-permute-start.3
  50.3 48.0 %collective-permute-done.3.b_ref = bf16[4,576,256]{2,1,0:T(8,128)(2,1)} collective-permute-done((bf16[4,576,256]{2,1,0:T(8,128)(2,1)S(1)}, bf16[4,576,256]{2,1,0:T(8,128)(2,1)}, u32[]{:S(2)}, u32[]{:S(2)}) %collective-permute-start.3) | collective-permute-done | bytes 1179680 | tf_op jit(solution)/shard_map/ppermute | solution.py:766
  98.3 0.6 reshape.75.gain_ref
  98.9 0.6 reshape.83.gain_ref
  99.5 0.6 fusion.5
  100.1 1.3 fusion.6
  101.4 0.1 collective-permute-done.5.fb_ref
  101.5 1.1 copy-done.1
  102.6 15.0 %make_qkv.1 = (bf16[1024,768]{1,0:T(8,128)(2,1)}, bf16[1024,2304]{1,0:T(8,128)(2,1)}, bf16[16,576,256]{2,1,0:T(8,128)(2,1)}) custom-call(s32[1]{0:T(128)} %bitcast.5.me_ref, bf16[1024,768]{1,0:T(8,128)(2,1)} %bitcast.57, f32[1,768]{1,0:T(1,128)} %reshape.75.gain_ref, bf16[4,576,256]{2,1,0:T(8,128)(2,1)} %copy-done.3, ...), custom_call_target="tpu_custom_call" | custom-call | flops 3623878656 | bytes 14680064 | tf_op jit(solution)/shard_map/make_qkv/pallas_call | solution.py:163
  117.6 26.2 %attend_forward.1 = (bf16[1024,768]{1,0:T(8,128)(2,1)}, f32[6,8,1024]{2,1,0:T(8,128)}) custom-call(s32[1]{0:T(128)} %bitcast.2.count_ref, bf16[1024,2304]{1,0:T(8,128)(2,1)} %get-tuple-element.45.q_ref.k_ref.v_ref, bf16[1024,2304]{1,0:T(8,128)(2,1)} %get-tuple-element.45.q_ref.k_ref.v_ref, bf16[1024,2304]{1,0:T(8,128)(2,1)} %get-tuple-element.45.q_ref.k_ref.v_ref), custom_call_target="tpu_custom_call" | custom-call | flops 3221225472 | bytes 8388608 | tf_op jit(solution)/shard_map/attend_forward/pallas_call | solution.py:242
  143.8 6.0 %out_project.1 = (f32[1024,768]{1,0:T(8,128)}, bf16[1024,768]{1,0:T(8,128)(2,1)}) custom-call(bf16[1024,768]{1,0:T(8,128)(2,1)} %bitcast.58, bf16[1024,768]{1,0:T(8,128)(2,1)} %get-tuple-element.46.o_ref, bf16[16,576,256]{2,1,0:T(8,128)(2,1)} %get-tuple-element.47.w_ref.wq_ref.wk_ref.wv_ref.wo_ref, f32[1,768]{1,0:T(1,128)} %reshape.83.gain_ref), custom_call_target="tpu_custom_call" | custom-call | flops 1207959552 | bytes 9437184 | tf_op jit(solution)/shard_map/out_project/pallas_call | solution.py:277
  149.8 52.8 %ffn_both.1 = (bf16[1024,768]{1,0:T(8,128)(2,1)}, f32[1024,768]{1,0:T(8,128)}, bf16[1024,768]{1,0:T(8,128)(2,1)}, bf16[16,1168,256]{2,1,0:T(8,128)(2,1)}) custom-call(s32[1]{0:T(128)} %bitcast.2.count_ref, f32[1024,768]{1,0:T(8,128)} %get-tuple-element.48.h_ref, bf16[1024,768]{1,0:T(8,128)(2,1)} %get-tuple-element.49.n2_ref, bf16[1024,768]{1,0:T(8,128)(2,1)} %bitcast.86, ...), custom_call_target="tpu_custom_call" | custom-call | flops 28991029248 | bytes 37748736 | tf_op jit(solution)/shard_map/ffn_both/pallas_call | solution.py:454
  202.6 0.0 reduce-scatter.2.cloned.1.call-update
  202.6 0.5 fusion.11.place_ref
  203.2 57.5 %attend_back.1 = (bf16[1024,768]{1,0:T(8,128)(2,1)}, bf16[8,592,256]{2,1,0:T(8,128)(2,1)}, bf16[8,592,256]{2,1,0:T(8,128)(2,1)}) custom-call(s32[1]{0:T(128)} %bitcast.2.count_ref, s32[16]{0:T(128)} %fusion.11.place_ref, bf16[1024,2304]{1,0:T(8,128)(2,1)} %get-tuple-element.45.q_ref.k_ref.v_ref, bf16[1024,2304]{1,0:T(8,128)(2,1)} %get-tuple-element.45.q_ref.k_ref.v_ref, ...), custom_call_target="tpu_custom_call" | custom-call | flops 17716740096 | bytes 25165824 | tf_op jit(solution)/shard_map/attend_back/pallas_call | solution.py:674
  260.7 0.8 collective-permute-start.6
  261.5 4.5 %collective-permute-done.6 = bf16[8,592,256]{2,1,0:T(8,128)(2,1)S(1)} collective-permute-done((bf16[8,592,256]{2,1,0:T(8,128)(2,1)}, bf16[8,592,256]{2,1,0:T(8,128)(2,1)S(1)}, u32[]{:S(2)}, u32[]{:S(2)}) %collective-permute-start.6) | collective-permute-done | bytes 2424864 | tf_op jit(solution)/shard_map/ppermute | solution.py:761
  265.9 3.5 add_convert_fusion
  269.5 1.3 collective-permute-start.7
  270.8 5.1 %all-to-all-start.1 = ((bf16[16,64,768]{2,1,0:T(8,128)(2,1)}), bf16[16,64,768]{2,1,0:T(8,128)(2,1)S(1)}, u32[]{:S(2)}, u32[]{:S(2)}) async-start(bf16[16,64,768]{2,1,0:T(8,128)(2,1)} %bitcast.60), calls=%async_computation.1 | async-start | bytes 3145728 | tf_op jit(solution)/shard_map/all_to_all | solution.py:909
  275.9 22.8 %collective-permute-done.7 = bf16[8,296,256]{2,1,0:T(8,128)(2,1)} collective-permute-done((bf16[8,296,256]{2,1,0:T(8,128)(2,1)}, bf16[8,296,256]{2,1,0:T(8,128)(2,1)}, u32[]{:S(2)}, u32[]{:S(2)}) %collective-permute-start.7) | collective-permute-done | bytes 1212448 | tf_op jit(solution)/shard_map/ppermute | solution.py:779
  298.7 1.7 add_convert_fusion.2
  300.4 0.1 collective-permute-start.8
  300.5 25.7 %collective-permute-done.8 = bf16[4,296,256]{2,1,0:T(8,128)(2,1)S(1)} collective-permute-done((bf16[4,296,256]{2,1,0:T(8,128)(2,1)S(1)}, bf16[4,296,256]{2,1,0:T(8,128)(2,1)S(1)}, u32[]{:S(2)}, u32[]{:S(2)}) %collective-permute-start.8) | collective-permute-done | bytes 606240 | tf_op jit(solution)/shard_map/ppermute | solution.py:766
  326.2 1.8 add_convert_fusion.1
  328.0 2.1 collective-permute-start.10
  330.1 1.5 collective-permute-start.11
  331.5 0.6 collective-permute-start.9
  332.1 12.5 %collective-permute-done.10 = bf16[296,256]{1,0:T(8,128)(2,1)S(1)} collective-permute-done((bf16[296,256]{1,0:T(8,128)(2,1)S(1)}, bf16[296,256]{1,0:T(8,128)(2,1)S(1)}, u32[]{:S(2)}, u32[]{:S(2)}) %collective-permute-start.10) | collective-permute-done | bytes 151584 | tf_op jit(solution)/shard_map/ppermute | solution.py:771
  344.7 0.1 fusion.2.mine_ref
  344.8 0.0 reduce-scatter.2.cloned.1.call-done.mine_ref
  344.8 1.1 collective-permute-start.13
  346.0 0.9 collective-permute-start.12
  346.9 0.7 pad_add_fusion.me_ref
  347.6 1.2 copy-done
  348.7 4.1 %undeal_rows.1 = bf16[512,768]{1,0:T(8,128)(2,1)} custom-call(s32[1,16]{1,0:T(1,128)} %units_ref.3, s32[1,16]{1,0:T(1,128)} %order_ref.3, bf16[16,64,768]{2,1,0:T(8,128)(2,1)} %copy-done), custom_call_target="tpu_custom_call" | custom-call | tf_op jit(solution)/shard_map/undeal_rows/pallas_call | solution.py:97
  352.9 10.5 %collective-permute-done.12.other_ref = bf16[296,256]{1,0:T(8,128)(2,1)S(1)} collective-permute-done((bf16[296,256]{1,0:T(8,128)(2,1)S(1)}, bf16[296,256]{1,0:T(8,128)(2,1)S(1)}, u32[]{:S(2)}, u32[]{:S(2)}) %collective-permute-start.12) | collective-permute-done | bytes 151584 | tf_op jit(solution)/shard_map/ppermute | solution.py:779
  363.4 0.7 copy-done.11
  364.1 1.9 finish.2
  366.0 0.8 copy-done.5
  366.8 2.4 finish.3
  (43 shorter events, 0.3 us)
Async XLA Ops:
  7.2 11.0 %copy-start.8 = (bf16[128,768]{1,0:T(8,128)(2,1)S(1)}, bf16[128,768]{1,0:T(8,128)(2,1)}, u32[]{:S(2)}) copy-start(bf16[128,768]{1,0:T(8,128)(2,1)} %param.24) | copy-start | bytes 589828
  7.2 142.6 %all-gather.2.cloned.1.call-start = ((), (), s32[]{:S(2)}) async-start(), calls=%async_computation.3 | async-start | bytes 10027008 | tf_op jit(solution)/shard_map/all_gather | solution.py:851
  8.2 10.3 %copy-start.9 = (bf16[48,2048]{1,0:T(8,128)(2,1)S(1)}, bf16[48,2048]{1,0:T(8,128)(2,1)}, u32[]{:S(2)}) copy-start(bf16[48,2048]{1,0:T(8,128)(2,1)} %param.22) | copy-start | bytes 589828
  11.1 7.5 %copy-start.10 = (bf16[48,2048]{1,0:T(8,128)(2,1)S(1)}, bf16[48,2048]{1,0:T(8,128)(2,1)}, u32[]{:S(2)}) copy-start(bf16[48,2048]{1,0:T(8,128)(2,1)} %param.23) | copy-start | bytes 589828
  11.1 13.1 %collective-permute-start = (bf16[576,256]{1,0:T(8,128)(2,1)S(1)}, bf16[576,256]{1,0:T(8,128)(2,1)S(1)}, u32[]{:S(2)}, u32[]{:S(2)}) collective-permute-start(bf16[576,256]{1,0:T(8,128)(2,1)S(1)} %pad_maximum_fusion.2), channel_id=1, source_target_pairs={{0,8},{2,10},{4,12},{6,14},{8,16},{10,18},{12,20},{14,22},{16,24},... | collective-permute-start | bytes 884744 | tf_op jit(solution)/shard_map/ppermute | solution.py:771
  14.2 21.8 %collective-permute-start.1 = (bf16[576,256]{1,0:T(8,128)(2,1)S(1)}, bf16[576,256]{1,0:T(8,128)(2,1)S(1)}, u32[]{:S(2)}, u32[]{:S(2)}) collective-permute-start(bf16[576,256]{1,0:T(8,128)(2,1)S(1)} %pad_maximum_fusion.2), channel_id=1, source_target_pairs={{0,16},{2,18},{4,20},{6,22},{8,24},{10,26},{12,28},{14,30},{16,0},... | collective-permute-start | bytes 884744 | tf_op jit(solution)/shard_map/ppermute | solution.py:771
  16.8 19.2 %collective-permute-start.2 = (bf16[576,256]{1,0:T(8,128)(2,1)S(1)}, bf16[576,256]{1,0:T(8,128)(2,1)S(1)}, u32[]{:S(2)}, u32[]{:S(2)}) collective-permute-start(bf16[576,256]{1,0:T(8,128)(2,1)S(1)} %pad_maximum_fusion.2), channel_id=1, source_target_pairs={{0,24},{2,26},{4,28},{6,30},{8,0},{10,2},{12,4},{14,6},{16,8},{18,... | collective-permute-start | bytes 884744 | tf_op jit(solution)/shard_map/ppermute | solution.py:771
  36.0 0.7 copy-start.6
  36.0 0.8 copy-start.7
  36.9 64.6 %all-to-all-start = ((bf16[16,64,768]{2,1,0:T(8,128)(2,1)}), bf16[16,64,768]{2,1,0:T(8,128)(2,1)S(1)}, u32[]{:S(2)}, u32[]{:S(2)}) async-start(bf16[16,64,768]{2,1,0:T(8,128)(2,1)} %deal_rows.1), calls=%async_computation | async-start | bytes 3145728 | tf_op jit(solution)/shard_map/all_to_all | solution.py:879
  47.0 51.3 %copy-start.12 = (f32[768]{0:T(1024)S(1)}, f32[768]{0:T(1024)}, u32[]{:S(2)}) copy-start(f32[768]{0:T(1024)} %param.16) | copy-start | bytes 9220
  47.0 51.9 %copy-start.13 = (f32[768]{0:T(1024)S(1)}, f32[768]{0:T(1024)}, u32[]{:S(2)}) copy-start(f32[768]{0:T(1024)} %param.21) | copy-start | bytes 9220
  47.0 52.5 %copy-start.15 = (s32[1,16]{1,0:T(1,128)S(1)}, s32[1,16]{1,0:T(1,128)}, u32[]{:S(2)}) copy-start(s32[1,16]{1,0:T(1,128)} %order_ref.3) | copy-start | bytes 196
  47.0 53.1 %copy-start.14 = (s32[1,16]{1,0:T(1,128)S(1)}, s32[1,16]{1,0:T(1,128)}, u32[]{:S(2)}) copy-start(s32[1,16]{1,0:T(1,128)} %units_ref.3) | copy-start | bytes 196
  47.0 297.8 %reduce-scatter.2.cloned.1.call-start = ((), (), s32[]{:S(2)}) async-start(), calls=%async_computation.4 | async-start | bytes 10166272 | tf_op jit(solution)/shard_map/reduce_scatter | solution.py:775
  48.3 53.2 %copy-start.3 = (bf16[4,576,256]{2,1,0:T(8,128)(2,1)}, bf16[4,576,256]{2,1,0:T(8,128)(2,1)S(1)}, u32[]{:S(2)}) copy-start(bf16[4,576,256]{2,1,0:T(8,128)(2,1)S(1)} %pad_maximum_fusion.a_ref) | copy-start | bytes 3538948
  48.3 50.0 %collective-permute-start.3 = (bf16[4,576,256]{2,1,0:T(8,128)(2,1)S(1)}, bf16[4,576,256]{2,1,0:T(8,128)(2,1)}, u32[]{:S(2)}, u32[]{:S(2)}) collective-permute-start(bf16[4,576,256]{2,1,0:T(8,128)(2,1)S(1)} %pad_maximum_fusion.a_ref), channel_id=1, source_target_pairs={{0,4},{2,6},{4,0},{6,2},{8,12},{10,14},{12,8},{14,10},{16,20},{18,... | collective-permute-start | bytes 3538952 | tf_op jit(solution)/shard_map/ppermute | solution.py:766
  50.3 51.1 %collective-permute-start.4 = (bf16[4,576,256]{2,1,0:T(8,128)(2,1)S(1)}, bf16[4,576,256]{2,1,0:T(8,128)(2,1)}, u32[]{:S(2)}, u32[]{:S(2)}) collective-permute-start(bf16[4,576,256]{2,1,0:T(8,128)(2,1)S(1)} %pad_maximum_fusion.a_ref), channel_id=1, source_target_pairs={{0,2},{2,0},{4,6},{6,4},{8,10},{10,8},{12,14},{14,12},{16,18},{18,... | collective-permute-start | bytes 3538952 | tf_op jit(solution)/shard_map/ppermute | solution.py:761
  98.3 3.2 collective-permute-start.5
  101.5 1.1 copy-start.1
  260.7 5.3 %collective-permute-start.6 = (bf16[8,592,256]{2,1,0:T(8,128)(2,1)}, bf16[8,592,256]{2,1,0:T(8,128)(2,1)S(1)}, u32[]{:S(2)}, u32[]{:S(2)}) collective-permute-start(bf16[8,592,256]{2,1,0:T(8,128)(2,1)} %get-tuple-element.58), channel_id=1, source_target_pairs={{0,2},{2,0},{4,6},{6,4},{8,10},{10,8},{12,14},{14,12},{16,18},{18,... | collective-permute-start | bytes 7274504 | tf_op jit(solution)/shard_map/ppermute | solution.py:761
  265.9 3.5 copy-start.2
  269.5 29.3 %collective-permute-start.7 = (bf16[8,296,256]{2,1,0:T(8,128)(2,1)}, bf16[8,296,256]{2,1,0:T(8,128)(2,1)}, u32[]{:S(2)}, u32[]{:S(2)}) collective-permute-start(bf16[8,296,256]{2,1,0:T(8,128)(2,1)} %add_convert_fusion), channel_id=1, source_target_pairs={{0,1},{1,0},{2,3},{3,2},{4,5},{5,4},{6,7},{7,6},{8,9},{9,8},{10,11... | collective-permute-start | bytes 3637256 | tf_op jit(solution)/shard_map/ppermute | solution.py:779
  270.8 76.8 %all-to-all-start.1 = ((bf16[16,64,768]{2,1,0:T(8,128)(2,1)}), bf16[16,64,768]{2,1,0:T(8,128)(2,1)S(1)}, u32[]{:S(2)}, u32[]{:S(2)}) async-start(bf16[16,64,768]{2,1,0:T(8,128)(2,1)} %bitcast.60), calls=%async_computation.1 | async-start | bytes 3145728 | tf_op jit(solution)/shard_map/all_to_all | solution.py:909
  300.4 25.8 %collective-permute-start.8 = (bf16[4,296,256]{2,1,0:T(8,128)(2,1)S(1)}, bf16[4,296,256]{2,1,0:T(8,128)(2,1)S(1)}, u32[]{:S(2)}, u32[]{:S(2)}) collective-permute-start(bf16[4,296,256]{2,1,0:T(8,128)(2,1)S(1)} %add_convert_fusion.2), channel_id=1, source_target_pairs={{0,4},{2,6},{4,0},{6,2},{8,12},{10,14},{12,8},{14,10},{16,20},{18,... | collective-permute-start | bytes 1818632 | tf_op jit(solution)/shard_map/ppermute | solution.py:766
  328.0 16.7 %collective-permute-start.10 = (bf16[296,256]{1,0:T(8,128)(2,1)S(1)}, bf16[296,256]{1,0:T(8,128)(2,1)S(1)}, u32[]{:S(2)}, u32[]{:S(2)}) collective-permute-start(bf16[296,256]{1,0:T(8,128)(2,1)S(1)} %get-tuple-element.73), channel_id=1, source_target_pairs={{0,16},{2,18},{4,20},{6,22},{8,24},{10,26},{12,28},{14,30},{16,0},... | collective-permute-start | bytes 454664 | tf_op jit(solution)/shard_map/ppermute | solution.py:771
  330.1 14.6 %collective-permute-start.11 = (bf16[296,256]{1,0:T(8,128)(2,1)S(1)}, bf16[296,256]{1,0:T(8,128)(2,1)S(1)}, u32[]{:S(2)}, u32[]{:S(2)}) collective-permute-start(bf16[296,256]{1,0:T(8,128)(2,1)S(1)} %get-tuple-element.72), channel_id=1, source_target_pairs={{0,24},{2,26},{4,28},{6,30},{8,0},{10,2},{12,4},{14,6},{16,8},{18,... | collective-permute-start | bytes 454664 | tf_op jit(solution)/shard_map/ppermute | solution.py:771
  331.5 13.1 %collective-permute-start.9 = (bf16[296,256]{1,0:T(8,128)(2,1)S(1)}, bf16[296,256]{1,0:T(8,128)(2,1)S(1)}, u32[]{:S(2)}, u32[]{:S(2)}) collective-permute-start(bf16[296,256]{1,0:T(8,128)(2,1)S(1)} %get-tuple-element.71), channel_id=1, source_target_pairs={{0,8},{2,10},{4,12},{6,14},{8,16},{10,18},{12,20},{14,22},{16,24},... | collective-permute-start | bytes 454664 | tf_op jit(solution)/shard_map/ppermute | solution.py:771
  344.8 18.6 %copy-start.4 = (bf16[296,256]{1,0:T(8,128)(2,1)}, bf16[296,256]{1,0:T(8,128)(2,1)S(1)}, u32[]{:S(2)}) copy-start(bf16[296,256]{1,0:T(8,128)(2,1)S(1)} %fusion.2.mine_ref) | copy-start | bytes 454660
  344.8 21.2 %collective-permute-start.13 = (bf16[1168,256]{1,0:T(8,128)(2,1)}, bf16[1168,256]{1,0:T(8,128)(2,1)S(1)}, u32[]{:S(2)}, u32[]{:S(2)}) collective-permute-start(bf16[1168,256]{1,0:T(8,128)(2,1)} %reduce-scatter.2.cloned.1.call-done.mine_ref), channel_id=1, source_target_pairs={{0,1},{1,0},{2,3},{3,2},{4,5},{5,4},{6,7},{7,6},{8,9},{9,8},{10,11... | collective-permute-start | bytes 1794056 | tf_op jit(solution)/shard_map/ppermute | solution.py:817
  346.0 17.4 %collective-permute-start.12 = (bf16[296,256]{1,0:T(8,128)(2,1)S(1)}, bf16[296,256]{1,0:T(8,128)(2,1)S(1)}, u32[]{:S(2)}, u32[]{:S(2)}) collective-permute-start(bf16[296,256]{1,0:T(8,128)(2,1)S(1)} %fusion.2.mine_ref), channel_id=1, source_target_pairs={{0,1},{1,0},{2,3},{3,2},{4,5},{5,4},{6,7},{7,6},{8,9},{9,8},{10,11... | collective-permute-start | bytes 454664 | tf_op jit(solution)/shard_map/ppermute | solution.py:779
  347.5 1.2 copy-start
  363.4 0.7 copy-start.11
  366.0 0.8 copy-start.5
Sparse Core Ops, SparseCore 0:
  36.2 112.1 all-gather.1
  202.7 138.3 reduce-scatter.1

commit v5 on v4

--- a/solution.py
+++ b/solution.py
@@ -147,26 +147,29 @@
         w_ref[there + 2 * (1 - side) + core] = b_ref[step]
         w_ref[there + 2 * (1 - side) + 1 - core] = fb_ref[step]
 
-    @pl.when(block < 3 * width // LANES)
+    @pl.when(block < 3)
     def _():
-        factor = jnp.where(block < width // LANES, HD ** (-0.5), 1.0)
-        made = plain_dot(n1_ref[...], whole_block(w_ref)).astype(bf16).astype(f32)
-        qkv_ref[...] = (made * factor).astype(bf16)
+        factor = jnp.where(block == 0, HD ** (-0.5), 1.0)
+        cols = width // LANES
+        rows = w_ref.shape[1] // cols
+        for c in range(cols):
+            weight = w_ref[:, c * rows : (c + 1) * rows, :].reshape(width, LANES)
+            made = plain_dot(n1_ref[...], weight).astype(bf16).astype(f32)
+            qkv_ref[:, c * LANES : (c + 1) * LANES] = (made * factor).astype(bf16)
 
 
 def make_qkv(me, tokens, gain, pieces, rows):
     span, width = tokens.shape
     along = pieces[0].shape[0]
-    blocks = 3 * width // LANES
-    everything = 4 * width // LANES
-    piece = pl.BlockSpec((along, rows, LANES), lambda j: (0, j, 0))
+    cols = width // LANES
+    piece = pl.BlockSpec((along, cols * rows, LANES), lambda j: (0, j, 0))
     return pl.pallas_call(
         qkv_kernel,
-        grid=(everything,),
+        grid=(4,),
         out_shape=(
             jax.ShapeDtypeStruct((span, width), bf16),
             jax.ShapeDtypeStruct((span, 3 * width), bf16),
-            jax.ShapeDtypeStruct((4 * along, everything * rows, LANES), bf16),
+            jax.ShapeDtypeStruct((4 * along, 4 * cols * rows, LANES), bf16),
         ),
         in_specs=[
             smem(),
@@ -179,8 +182,8 @@
         ],
         out_specs=(
             const_block((span, width)),
-            pl.BlockSpec((span, LANES), lambda j: (0, jnp.minimum(j, blocks - 1))),
-            pl.BlockSpec((4 * along, rows, LANES), lambda j: (0, j, 0)),
+            pl.BlockSpec((span, width), lambda j: (0, jnp.minimum(j, 2))),
+            pl.BlockSpec((4 * along, cols * rows, LANES), lambda j: (0, j, 0)),
         ),
         compiler_params=params(),
         cost_estimate=cost(6 * span * width * width, 14 << 20),
@@ -204,7 +207,7 @@
     return jnp.where(inside, queries, one)
 
 
-def attend_kernel(unit_max, chunk, count_ref, q_ref, k_ref, v_ref, o_ref, lse_ref, kb_ref, vt_ref):
+def attend_kernel(unit_max, chunk, count_ref, q_ref, k_ref, v_ref, o_ref, lse_ref, kb_ref, vt_ref, ot_ref):
     span = q_ref.shape[0]
     pair = 2 * HD
     lane = lax.broadcasted_iota(jnp.int32, (span, pair), 1)
@@ -216,18 +219,28 @@
         vt_ref[head, :HD] = values_t[head * HD : (head + 1) * HD]
         vt_ref[head, HD:] = jnp.ones((vt_ref.shape[1] - HD, span), bf16)
     lane_c = lane[:chunk]
-    for begin in range(0, span, chunk):
-        queries = q_ref[begin : begin + chunk, :]
-        mixed = []
-        for head in range(2):
-            scores = right_dot(kb_ref[head], head_queries(queries, lane_c, head))
-            top = jnp.max(scores, axis=0, keepdims=True)
-            probs = jnp.exp(scores - top).astype(bf16)
-            both = plain_dot(vt_ref[head], probs)
-            total = both[HD : HD + 1]
-            mixed.append(both[:HD] * (1.0 / total))
-            lse_ref[0, head : head + 1, begin : begin + chunk] = top + jnp.log(total)
-        o_ref[begin : begin + chunk, :] = jnp.concatenate(mixed, axis=0).T.astype(bf16)
+    jobs = [(head, begin) for begin in range(0, span, chunk) for head in range(2)]
+
+    def first(job):
+        head, begin = job
+        return right_dot(kb_ref[head], head_queries(q_ref[begin : begin + chunk, :], lane_c, head))
+
+    def second(job, scores):
+        head, begin = job
+        part = slice(begin, begin + chunk)
+        top = jnp.max(scores, axis=0, keepdims=True)
+        probs = jnp.exp(scores - top).astype(bf16)
+        both = plain_dot(vt_ref[head], probs)
+        total = both[HD : HD + 1]
+        ot_ref[head * HD : (head + 1) * HD, part] = both[:HD] * (1.0 / total)
+        lse_ref[0, head : head + 1, part] = top + jnp.log(total)
+
+    held = first(jobs[0])
+    for i, job in enumerate(jobs):
+        later = first(jobs[i + 1]) if i + 1 < len(jobs) else None
+        second(job, held)
+        held = later
+    o_ref[...] = ot_ref[...].T.astype(bf16)
 
 
 def attend_forward(count, qkv, unit_max):
@@ -240,7 +253,7 @@
         return pl.BlockSpec((span, pair), lambda p: (0, first + p))
 
     return pl.pallas_call(
-        functools.partial(attend_kernel, unit_max, 512),
+        functools.partial(attend_kernel, unit_max, 1024),
         grid=(pairs,),
         out_shape=(
             jax.ShapeDtypeStruct((span, width), bf16),
@@ -251,6 +264,7 @@
         scratch_shapes=[
             pltpu.VMEM((2, span, pair), bf16),
             pltpu.VMEM((2, HD + 16, span), bf16),
+            pltpu.VMEM((pair, span), f32),
         ],
         compiler_params=params(),
         cost_estimate=cost(4 * span * span * width, 8 << 20, span * span * H),
@@ -330,6 +344,9 @@
     stage_up,
     stage_down,
     stage_gain,
+    act_s,
+    gg_s,
+    gu_s,
     sems,
 ):
     step = pl.program_id(0)
@@ -367,53 +384,63 @@
     @pl.when(step == 0)
     def _():
         gb_ref[...] = jnp.where(live, d_ref[...].astype(f32), 0.0).astype(bf16)
+        y_ref[...] = jnp.zeros_like(y_ref)
+        gn_ref[...] = jnp.zeros_like(gn_ref)
 
     @pl.when(step >= 2)
     def _():
         for copy in copies(step - 2, slot):
             copy.wait()
 
-    n2 = n2_ref[...]
-    gb = gb_ref[...]
     w_gate = whole_block(wg_ref)
     w_up = whole_block(wu_ref)
-    gate = plain_dot(n2, w_gate)
-    up = plain_dot(n2, w_up)
     downs = [
         wd_ref[:, c * down : (c + 1) * down, :].reshape(few * down, LANES) for c in range(cols)
     ]
-    g_act = right_dot(gb[:, :LANES], downs[0])
-    for c in range(1, cols):
-        g_act += right_dot(gb[:, c * LANES : (c + 1) * LANES], downs[c])
-    c0 = 0.7978845608028654
-    c1 = 0.044715
-    square = gate * gate
-    tang = jnp.tanh(c0 * gate * (1.0 + c1 * square))
-    half = 0.5 * (1.0 + tang)
-    gelu = gate * half
-    slope = half + (0.5 * c0) * gate * (1.0 - tang * tang) * (1.0 + (3.0 * c1) * square)
-    act = (gelu * up).astype(bf16)
-    g_gate = (g_act * up * slope).astype(bf16)
-    g_up = (g_act * gelu).astype(bf16)
+    chunk = span // 2
+
+    def first(part):
+        n2 = n2_ref[part, :]
+        gate = plain_dot(n2, w_gate)
+        up = plain_dot(n2, w_up)
+        g_act = right_dot(gb_ref[part, :LANES], downs[0])
+        for c in range(1, cols):
+            g_act += right_dot(gb_ref[part, c * LANES : (c + 1) * LANES], downs[c])
+        return gate, up, g_act
+
+    def middle(part, gate, up, g_act):
+        c0 = 0.7978845608028654
+        c1 = 0.044715
+        square = gate * gate
+        inner = c0 + (c0 * c1) * square
+        tang = jnp.tanh(gate * inner)
+        half = 0.5 + 0.5 * tang
+        gelu = gate * half
+        slope = half + (gate * (0.5 - 0.5 * tang * tang)) * (c0 + (3.0 * c0 * c1) * square)
+        act_s[part, :] = (gelu * up).astype(bf16)
+        gg_s[part, :] = (g_act * up * slope).astype(bf16)
+        gu_s[part, :] = (g_act * gelu).astype(bf16)
+
+    def second(part):
+        for c in range(cols):
+            place = slice(c * LANES, (c + 1) * LANES)
+            add = plain_dot(act_s[part, :], downs[c])
+            grad = right_dot(gg_s[part, :], w_gate[place]) + right_dot(gu_s[part, :], w_up[place])
+            y_ref[part, place] += add
+            gn_ref[part, place] += grad
+
+    parts_of = [slice(i * chunk, (i + 1) * chunk) for i in range(2)]
+    held = first(parts_of[0])
+    for i, part in enumerate(parts_of):
+        later = first(parts_of[i + 1]) if i + 1 < len(parts_of) else None
+        middle(part, *held)
+        second(part)
+        held = later
     for c in range(cols):
-        place = slice(c * LANES, (c + 1) * LANES)
-        add = plain_dot(act, downs[c])
-        grad = right_dot(g_gate, w_gate[place]) + right_dot(g_up, w_up[place])
-        wide = left_dot(act, gb[:, place]).astype(bf16).reshape(few, down, LANES)
-        stage_down[slot, :, c * down : (c + 1) * down, :] = wide
-
-        @pl.when(step == 0)
-        def _():
-            y_ref[:, place] = add
-            gn_ref[:, place] = grad
-
-        @pl.when(step > 0)
-        def _():
-            y_ref[:, place] += add
-            gn_ref[:, place] += grad
-
-    stage_gate[slot] = left_dot(n2, g_gate).astype(bf16).reshape(parts, rows, LANES)
-    stage_up[slot] = left_dot(n2, g_up).astype(bf16).reshape(parts, rows, LANES)
+        wide = left_dot(act_s[...], gb_ref[:, c * LANES : (c + 1) * LANES]).astype(bf16)
+        stage_down[slot, :, c * down : (c + 1) * down, :] = wide.reshape(few, down, LANES)
+    stage_gate[slot] = left_dot(n2_ref[...], gg_s[...]).astype(bf16).reshape(parts, rows, LANES)
+    stage_up[slot] = left_dot(n2_ref[...], gu_s[...]).astype(bf16).reshape(parts, rows, LANES)
     for copy in copies(step, slot):
         copy.start()
 
@@ -479,6 +506,9 @@
             pltpu.VMEM((2, parts, rows, LANES), bf16),
             pltpu.VMEM((2, few, cols * down, LANES), bf16),
             pltpu.VMEM((parts, GAIN_ROWS, LANES), bf16),
+            pltpu.VMEM((span, LANES), bf16),
+            pltpu.VMEM((span, LANES), bf16),
+            pltpu.VMEM((span, LANES), bf16),
             pltpu.SemaphoreType.DMA((4, 2)),
         ],
         compiler_params=params(),
@@ -552,6 +582,7 @@
 
     @pl.when(step == 0)
     def _():
+        gn_s[...] = jnp.zeros_like(gn_s)
         for c in range(cols):
             wo_s[c] = wo_ref[:, c * rows : (c + 1) * rows, :].reshape(width, LANES)
 
@@ -575,36 +606,45 @@
     dv_s[...] = jnp.zeros_like(dv_s)
     bias = live_bias(count_ref[0], span, unit_max)
 
-    def one_head(head, carry):
-        half = head // 2
-        sub = lax.rem(head, 2)
-        side = pl.ds(pl.multiple_of(half * pair, pair), pair)
-        inside = (lane // HD) == sub
-        inside_c = (lane_c // HD) == sub
-        zero = jnp.zeros((), bf16)
-        keys = head_keys(k_ref[:, side], bias, lane, sub)
-        values = jnp.where(inside, v_ref[:, side], zero)
-        keys_t = kt_s[pl.ds(pl.multiple_of(head * HD, HD), HD), :]
-        d_k = None
-        d_v = None
-        for begin in range(0, span, chunk):
-            part = slice(begin, begin + chunk)
-            queries = q_ref[part, side]
-            grads = do_s[part, side]
-            scores = right_dot(keys, head_queries(queries, lane_c, sub))
+    zero = jnp.zeros((), bf16)
+
+    def some_heads(turn, carry):
+        jobs = []
+        for u in range(2):
+            head = turn * 2 + u
+            half = head // 2
+            sub = u % 2 if 2 > 1 else lax.rem(head, 2)
+            side = pl.ds(pl.multiple_of(half * pair, pair), pair)
+            inside = (lane // HD) == sub
+            keys = head_keys(k_ref[:, side], bias, lane, sub)
+            values = jnp.where(inside, v_ref[:, side], zero)
+            for begin in range(0, span, chunk):
+                jobs.append((head, half, sub, side, keys, values, slice(begin, begin + chunk)))
+
+        def first(job):
+            head, half, sub, side, keys, values, part = job
+            scores = right_dot(keys, head_queries(q_ref[part, side], lane_c, sub))
+            d_probs = right_dot(values, do_s[part, side])
+            return scores, d_probs
+
+        def second(job, scores, d_probs):
+            head, half, sub, side, keys, values, part = job
+            inside_c = (lane_c // HD) == sub
             probs = jnp.exp(scores - lse_ref[half, pl.ds(sub, 1), part])
-            d_probs = right_dot(values, grads)
             d_scores = (probs * (d_probs - delta_s[pl.ds(head, 1), part])).astype(bf16)
-            add_v = plain_dot(probs.astype(bf16), jnp.where(inside_c, grads, zero))
-            add_k = plain_dot(d_scores, jnp.where(inside_c, queries, zero))
-            d_v = add_v if d_v is None else d_v + add_v
-            d_k = add_k if d_k is None else d_k + add_k
-            dqt_s[pl.ds(pl.multiple_of(head * HD, HD), HD), part] = plain_dot(keys_t, d_scores)
-        dk_s[:, side] += d_k
-        dv_s[:, side] += d_v
+            dv_s[:, side] += plain_dot(probs.astype(bf16), jnp.where(inside_c, do_s[part, side], zero))
+            dk_s[:, side] += plain_dot(d_scores, jnp.where(inside_c, q_ref[part, side], zero))
+            rows_t = pl.ds(pl.multiple_of(head * HD, HD), HD)
+            dqt_s[rows_t, part] = plain_dot(kt_s[rows_t, :], d_scores)
+
+        held = first(jobs[0])
+        for i, job in enumerate(jobs):
+            later = first(jobs[i + 1]) if i + 1 < len(jobs) else None
+            second(job, *held)
+            held = later
         return carry
 
-    lax.fori_loop(0, heads, one_head, 0)
+    lax.fori_loop(0, heads // 2, some_heads, 0)
     d_q = (dqt_s[...].T * (HD ** (-0.5))).astype(bf16)
     d_k = dk_s[...].astype(bf16)
     d_v = dv_s[...].astype(bf16)
@@ -615,13 +655,10 @@
         + right_dot(d_v, whole_block(wv_ref))
     )
 
-    @pl.when(step == 0)
-    def _():
-        gn_s[...] = add
+    gn_s[...] += add
 
     @pl.when(step > 0)
     def _():
-        gn_s[...] += add
         for copy in copies(step - 1):
             copy.wait()
 

time: 378 us -> 364 us (0.963)
  Pallas kernels: 170 us -> 150 us
  waiting for transfers between devices: 137 us -> 146 us
    pallas_call x1, Pallas kernels: 52.8 us -> 43.4 us  [ffn_both(): pl.pallas_call(functools.partial(ffn_kernel, unit_max), grid=(blocks,), o...]
    pallas_call x2, Pallas kernels: 41.1 us -> 31.8 us  [the longest x1 20.9 us: attend_forward(): pl.pallas_call(functools.partial(attend_kernel, unit_max, 1024), grid=(pa...]
    all_gather x1, waiting for transfers between devices: 0.01 us -> 7.87 us  [gather_queue(): whole = lax.all_gather(packed, 'shard', axis=0, tiled=True)]
  transfers between devices with their start and end apart: 18 -> 18, of which waited for: 9 -> 10; matrix products, arithmetic and copies ran while one was open for 4% -> 4% of each run, Pallas kernels for 31% -> 29%
where the time goes in v5:
time: 364 us; the launch traced here: 363 us
  Pallas kernels  150 us (41%)
  waiting for transfers between devices  146 us (40%)
  starting transfers between devices  29.8 us (8%)
  between operations  14.3 us (4%)
  other arithmetic  12.2 us (3%)
  local copies, waits for them, and re-layouts  10.1 us (3%)
    ppermute x2, waiting for transfers between devices, to_side(): return lax.ppermute(value, 'shard', [(i, i ^ 2) for i in range(count)])  73.4 us
    pallas_call x1, Pallas kernels, attend_back(): pl.pallas_call(functools.partial(attend_back_kernel, unit_max, 512), grid...  56.5 us
    pallas_call x1, Pallas kernels, ffn_both(): pl.pallas_call(functools.partial(ffn_kernel, unit_max), grid=(blocks,), o...  43.4 us
    ppermute x2, waiting for transfers between devices, to_replica(): return lax.ppermute(value, 'replica', [(0, 1), (1, 0)])  35.1 us
    ppermute x6, waiting for transfers between devices, along_z(): lax.ppermute(value, 'shard', [(i, (i + 4 * step) % count) for i in range(...  25.1 us
    pallas_call x1, Pallas kernels, attend_forward(): pl.pallas_call(functools.partial(attend_kernel, unit_max, 1024), grid=(pa...  20.9 us
    pallas_call x1, Pallas kernels, make_qkv(): pl.pallas_call(qkv_kernel, grid=(4,), out_shape=(jax.ShapeDtypeStruct((sp...  10.9 us
    all_to_all x1, starting transfers between devices, shards(): lax.all_to_all(outgoing, 'shard', split_axis=0, concat_axis=0, tiled=True)  10.1 us
  transfers between devices with their start and end apart: 18, of which 10 were waited for; matrix products, arithmetic and copies ran while one was open for 4% of the time, Pallas kernels for 29%

profile of v5, /device:TPU:0, one launch (start us, length us, event | category | flops | bytes accessed | tf_op | source)
XLA Modules:
  0.0 363.0 jit_solution(12373231083867048680)
XLA Ops:
  7.2 0.0 all-gather.2.cloned.1.call-start
  7.2 1.0 reshape.79
  8.2 1.0 reshape.80
  9.2 0.9 reshape.81
  10.1 0.9 reshape.82
  11.1 3.1 collective-permute-start
  14.2 2.6 collective-permute-start.1
  16.8 1.3 collective-permute-start.2
  18.2 0.2 copy.40
  18.3 0.2 copy.41
  18.7 4.1 %deal_rows.1 = bf16[16,64,768]{2,1,0:T(8,128)(2,1)} custom-call(s32[1,16]{1,0:T(1,128)} %units_ref.3, s32[1,16]{1,0:T(1,128)} %order_ref.3, bf16[512,768]{1,0:T(8,128)(2,1)} %bitcast.68), custom_call_target="tpu_custom_call" | custom-call | tf_op jit(solution)/shard_map/deal_rows/pallas_call | solution.py:85
  22.8 0.9 pad_maximum_fusion.1
  23.6 0.6 collective-permute-done
  24.3 11.8 %collective-permute-done.1 = bf16[576,256]{1,0:T(8,128)(2,1)S(1)} collective-permute-done((bf16[576,256]{1,0:T(8,128)(2,1)S(1)}, bf16[576,256]{1,0:T(8,128)(2,1)S(1)}, u32[]{:S(2)}, u32[]{:S(2)}) %collective-permute-start.1) | collective-permute-done | bytes 294944 | tf_op jit(solution)/shard_map/ppermute | solution.py:808
  36.0 0.0 all-gather.2.cloned.1.call-update
  36.1 0.7 copy-done.6
  36.8 0.1 copy-done.7
  36.9 10.1 %all-to-all-start = ((bf16[16,64,768]{2,1,0:T(8,128)(2,1)}), bf16[16,64,768]{2,1,0:T(8,128)(2,1)S(1)}, u32[]{:S(2)}, u32[]{:S(2)}) async-start(bf16[16,64,768]{2,1,0:T(8,128)(2,1)} %deal_rows.1), calls=%async_computation | async-start | bytes 3145728 | tf_op jit(solution)/shard_map/all_to_all | solution.py:916
  47.0 0.0 copy-start.12
  47.0 0.0 copy-start.13
  47.0 0.0 reduce-scatter.2.cloned.1.call-start
  47.1 1.2 pad_maximum_fusion.a_ref
  48.3 2.0 collective-permute-start.3
  50.3 48.0 %collective-permute-done.3.b_ref = bf16[4,576,256]{2,1,0:T(8,128)(2,1)} collective-permute-done((bf16[4,576,256]{2,1,0:T(8,128)(2,1)S(1)}, bf16[4,576,256]{2,1,0:T(8,128)(2,1)}, u32[]{:S(2)}, u32[]{:S(2)}) %collective-permute-start.3) | collective-permute-done | bytes 1179680 | tf_op jit(solution)/shard_map/ppermute | solution.py:803
  98.3 0.6 reshape.75.gain_ref
  98.9 0.6 reshape.83.gain_ref
  99.5 0.6 fusion.5
  100.1 1.3 fusion.6
  101.4 0.1 collective-permute-done.5.fb_ref
  101.5 1.1 copy-done.1
  102.6 10.9 %make_qkv.1 = (bf16[1024,768]{1,0:T(8,128)(2,1)}, bf16[1024,2304]{1,0:T(8,128)(2,1)}, bf16[16,576,256]{2,1,0:T(8,128)(2,1)}) custom-call(s32[1]{0:T(128)} %bitcast.5.me_ref, bf16[1024,768]{1,0:T(8,128)(2,1)} %bitcast.57, f32[1,768]{1,0:T(1,128)} %reshape.75.gain_ref, bf16[4,576,256]{2,1,0:T(8,128)(2,1)} %copy-done.3, ...), custom_call_target="tpu_custom_call" | custom-call | flops 3623878656 | bytes 14680064 | tf_op jit(solution)/shard_map/make_qkv/pallas_call | solution.py:166
  113.5 20.9 %attend_forward.1 = (bf16[1024,768]{1,0:T(8,128)(2,1)}, f32[6,8,1024]{2,1,0:T(8,128)}) custom-call(s32[1]{0:T(128)} %bitcast.2.count_ref, bf16[1024,2304]{1,0:T(8,128)(2,1)} %get-tuple-element.45.q_ref.k_ref.v_ref, bf16[1024,2304]{1,0:T(8,128)(2,1)} %get-tuple-element.45.q_ref.k_ref.v_ref, bf16[1024,2304]{1,0:T(8,128)(2,1)} %get-tuple-element.45.q_ref.k_ref.v_ref), custom_call_target="tpu_custom_call" | custom-call | flops 3221225472 | bytes 8388608 | tf_op jit(solution)/shard_map/attend_forward/pallas_call | solution.py:255
  134.5 6.0 %out_project.1 = (f32[1024,768]{1,0:T(8,128)}, bf16[1024,768]{1,0:T(8,128)(2,1)}) custom-call(bf16[1024,768]{1,0:T(8,128)(2,1)} %bitcast.58, bf16[1024,768]{1,0:T(8,128)(2,1)} %get-tuple-element.46.o_ref, bf16[16,576,256]{2,1,0:T(8,128)(2,1)} %get-tuple-element.47.w_ref.wq_ref.wk_ref.wv_ref.wo_ref, f32[1,768]{1,0:T(1,128)} %reshape.83.gain_ref), custom_call_target="tpu_custom_call" | custom-call | flops 1207959552 | bytes 9437184 | tf_op jit(solution)/shard_map/out_project/pallas_call | solution.py:291
  140.5 7.9 %all-gather.2.cloned.1.call-done = bf16[18432,256]{1,0:T(8,128)(2,1)} async-done(((bf16[1152,256]{1,0:T(8,128)(2,1)}), bf16[18432,256]{1,0:T(8,128)(2,1)}) %all-gather.2.cloned.1.call-update) | async-done | bytes 9437200 | tf_op jit(solution)/shard_map/all_gather | solution.py:888
  148.4 43.4 %ffn_both.1 = (bf16[1024,768]{1,0:T(8,128)(2,1)}, f32[1024,768]{1,0:T(8,128)}, bf16[1024,768]{1,0:T(8,128)(2,1)}, bf16[16,1168,256]{2,1,0:T(8,128)(2,1)}) custom-call(s32[1]{0:T(128)} %bitcast.2.count_ref, f32[1024,768]{1,0:T(8,128)} %get-tuple-element.48.h_ref, bf16[1024,768]{1,0:T(8,128)(2,1)} %get-tuple-element.49.n2_ref, bf16[1024,768]{1,0:T(8,128)(2,1)} %bitcast.86, ...), custom_call_target="tpu_custom_call" | custom-call | flops 28991029248 | bytes 37748736 | tf_op jit(solution)/shard_map/ffn_both/pallas_call | solution.py:481
  191.7 0.0 reduce-scatter.2.cloned.1.call-update
  191.8 0.5 fusion.11.place_ref
  192.3 56.5 %attend_back.1 = (bf16[1024,768]{1,0:T(8,128)(2,1)}, bf16[8,592,256]{2,1,0:T(8,128)(2,1)}, bf16[8,592,256]{2,1,0:T(8,128)(2,1)}) custom-call(s32[1]{0:T(128)} %bitcast.2.count_ref, s32[16]{0:T(128)} %fusion.11.place_ref, bf16[1024,2304]{1,0:T(8,128)(2,1)} %get-tuple-element.45.q_ref.k_ref.v_ref, bf16[1024,2304]{1,0:T(8,128)(2,1)} %get-tuple-element.45.q_ref.k_ref.v_ref, ...), custom_call_target="tpu_custom_call" | custom-call | flops 17716740096 | bytes 25165824 | tf_op jit(solution)/shard_map/attend_back/pallas_call | solution.py:711
  248.9 0.3 collective-permute-start.6
  249.2 4.6 %collective-permute-done.6 = bf16[8,592,256]{2,1,0:T(8,128)(2,1)S(1)} collective-permute-done((bf16[8,592,256]{2,1,0:T(8,128)(2,1)}, bf16[8,592,256]{2,1,0:T(8,128)(2,1)S(1)}, u32[]{:S(2)}, u32[]{:S(2)}) %collective-permute-start.6) | collective-permute-done | bytes 2424864 | tf_op jit(solution)/shard_map/ppermute | solution.py:798
  253.8 3.5 add_convert_fusion
  257.3 1.3 collective-permute-start.7
  258.6 3.7 %all-to-all-start.1 = ((bf16[16,64,768]{2,1,0:T(8,128)(2,1)}), bf16[16,64,768]{2,1,0:T(8,128)(2,1)S(1)}, u32[]{:S(2)}, u32[]{:S(2)}) async-start(bf16[16,64,768]{2,1,0:T(8,128)(2,1)} %bitcast.60), calls=%async_computation.1 | async-start | bytes 3145728 | tf_op jit(solution)/shard_map/all_to_all | solution.py:946
  262.3 24.2 %collective-permute-done.7 = bf16[8,296,256]{2,1,0:T(8,128)(2,1)} collective-permute-done((bf16[8,296,256]{2,1,0:T(8,128)(2,1)}, bf16[8,296,256]{2,1,0:T(8,128)(2,1)}, u32[]{:S(2)}, u32[]{:S(2)}) %collective-permute-start.7) | collective-permute-done | bytes 1212448 | tf_op jit(solution)/shard_map/ppermute | solution.py:816
  286.5 1.7 add_convert_fusion.2
  288.1 0.2 collective-permute-start.8
  288.3 25.3 %collective-permute-done.8 = bf16[4,296,256]{2,1,0:T(8,128)(2,1)S(1)} collective-permute-done((bf16[4,296,256]{2,1,0:T(8,128)(2,1)S(1)}, bf16[4,296,256]{2,1,0:T(8,128)(2,1)S(1)}, u32[]{:S(2)}, u32[]{:S(2)}) %collective-permute-start.8) | collective-permute-done | bytes 606240 | tf_op jit(solution)/shard_map/ppermute | solution.py:803
  313.6 1.8 add_convert_fusion.1
  315.4 1.0 collective-permute-start.10
  316.4 1.6 collective-permute-start.11
  318.0 0.5 collective-permute-start.9
  318.4 12.7 %collective-permute-done.10 = bf16[296,256]{1,0:T(8,128)(2,1)S(1)} collective-permute-done((bf16[296,256]{1,0:T(8,128)(2,1)S(1)}, bf16[296,256]{1,0:T(8,128)(2,1)S(1)}, u32[]{:S(2)}, u32[]{:S(2)}) %collective-permute-start.10) | collective-permute-done | bytes 151584 | tf_op jit(solution)/shard_map/ppermute | solution.py:808
  331.1 0.1 fusion.2.mine_ref
  331.2 0.0 reduce-scatter.2.cloned.1.call-done.mine_ref
  331.3 1.7 collective-permute-start.13
  332.9 0.4 collective-permute-start.12
  333.4 0.7 pad_add_fusion.me_ref
  334.0 1.2 copy-done
  335.2 4.1 %undeal_rows.1 = bf16[512,768]{1,0:T(8,128)(2,1)} custom-call(s32[1,16]{1,0:T(1,128)} %units_ref.3, s32[1,16]{1,0:T(1,128)} %order_ref.3, bf16[16,64,768]{2,1,0:T(8,128)(2,1)} %copy-done), custom_call_target="tpu_custom_call" | custom-call | tf_op jit(solution)/shard_map/undeal_rows/pallas_call | solution.py:97
  339.3 11.0 %collective-permute-done.12.other_ref = bf16[296,256]{1,0:T(8,128)(2,1)S(1)} collective-permute-done((bf16[296,256]{1,0:T(8,128)(2,1)S(1)}, bf16[296,256]{1,0:T(8,128)(2,1)S(1)}, u32[]{:S(2)}, u32[]{:S(2)}) %collective-permute-start.12) | collective-permute-done | bytes 151584 | tf_op jit(solution)/shard_map/ppermute | solution.py:816
  350.3 0.7 copy-done.11
  351.0 1.9 finish.2
  352.9 0.8 copy-done.5
  353.7 2.4 finish.3
  (43 shorter events, 0.3 us)
Async XLA Ops:
  7.2 11.0 %copy-start.8 = (bf16[128,768]{1,0:T(8,128)(2,1)S(1)}, bf16[128,768]{1,0:T(8,128)(2,1)}, u32[]{:S(2)}) copy-start(bf16[128,768]{1,0:T(8,128)(2,1)} %param.24) | copy-start | bytes 589828
  7.2 141.2 %all-gather.2.cloned.1.call-start = ((), (), s32[]{:S(2)}) async-start(), calls=%async_computation.3 | async-start | bytes 10027008 | tf_op jit(solution)/shard_map/all_gather | solution.py:888
  8.2 10.3 %copy-start.9 = (bf16[48,2048]{1,0:T(8,128)(2,1)S(1)}, bf16[48,2048]{1,0:T(8,128)(2,1)}, u32[]{:S(2)}) copy-start(bf16[48,2048]{1,0:T(8,128)(2,1)} %param.22) | copy-start | bytes 589828
  11.1 7.5 %copy-start.10 = (bf16[48,2048]{1,0:T(8,128)(2,1)S(1)}, bf16[48,2048]{1,0:T(8,128)(2,1)}, u32[]{:S(2)}) copy-start(bf16[48,2048]{1,0:T(8,128)(2,1)} %param.23) | copy-start | bytes 589828
  11.1 13.1 %collective-permute-start = (bf16[576,256]{1,0:T(8,128)(2,1)S(1)}, bf16[576,256]{1,0:T(8,128)(2,1)S(1)}, u32[]{:S(2)}, u32[]{:S(2)}) collective-permute-start(bf16[576,256]{1,0:T(8,128)(2,1)S(1)} %pad_maximum_fusion.2), channel_id=1, source_target_pairs={{0,8},{2,10},{4,12},{6,14},{8,16},{10,18},{12,20},{14,22},{16,24},... | collective-permute-start | bytes 884744 | tf_op jit(solution)/shard_map/ppermute | solution.py:808
  14.2 21.8 %collective-permute-start.1 = (bf16[576,256]{1,0:T(8,128)(2,1)S(1)}, bf16[576,256]{1,0:T(8,128)(2,1)S(1)}, u32[]{:S(2)}, u32[]{:S(2)}) collective-permute-start(bf16[576,256]{1,0:T(8,128)(2,1)S(1)} %pad_maximum_fusion.2), channel_id=1, source_target_pairs={{0,16},{2,18},{4,20},{6,22},{8,24},{10,26},{12,28},{14,30},{16,0},... | collective-permute-start | bytes 884744 | tf_op jit(solution)/shard_map/ppermute | solution.py:808
  16.8 19.2 %collective-permute-start.2 = (bf16[576,256]{1,0:T(8,128)(2,1)S(1)}, bf16[576,256]{1,0:T(8,128)(2,1)S(1)}, u32[]{:S(2)}, u32[]{:S(2)}) collective-permute-start(bf16[576,256]{1,0:T(8,128)(2,1)S(1)} %pad_maximum_fusion.2), channel_id=1, source_target_pairs={{0,24},{2,26},{4,28},{6,30},{8,0},{10,2},{12,4},{14,6},{16,8},{18,... | collective-permute-start | bytes 884744 | tf_op jit(solution)/shard_map/ppermute | solution.py:808
  36.0 0.7 copy-start.6
  36.0 0.8 copy-start.7
  36.9 64.6 %all-to-all-start = ((bf16[16,64,768]{2,1,0:T(8,128)(2,1)}), bf16[16,64,768]{2,1,0:T(8,128)(2,1)S(1)}, u32[]{:S(2)}, u32[]{:S(2)}) async-start(bf16[16,64,768]{2,1,0:T(8,128)(2,1)} %deal_rows.1), calls=%async_computation | async-start | bytes 3145728 | tf_op jit(solution)/shard_map/all_to_all | solution.py:916
  47.0 51.3 %copy-start.12 = (f32[768]{0:T(1024)S(1)}, f32[768]{0:T(1024)}, u32[]{:S(2)}) copy-start(f32[768]{0:T(1024)} %param.16) | copy-start | bytes 9220
  47.0 51.9 %copy-start.13 = (f32[768]{0:T(1024)S(1)}, f32[768]{0:T(1024)}, u32[]{:S(2)}) copy-start(f32[768]{0:T(1024)} %param.21) | copy-start | bytes 9220
  47.0 52.5 %copy-start.15 = (s32[1,16]{1,0:T(1,128)S(1)}, s32[1,16]{1,0:T(1,128)}, u32[]{:S(2)}) copy-start(s32[1,16]{1,0:T(1,128)} %order_ref.3) | copy-start | bytes 196
  47.0 53.1 %copy-start.14 = (s32[1,16]{1,0:T(1,128)S(1)}, s32[1,16]{1,0:T(1,128)}, u32[]{:S(2)}) copy-start(s32[1,16]{1,0:T(1,128)} %units_ref.3) | copy-start | bytes 196
  47.0 284.2 %reduce-scatter.2.cloned.1.call-start = ((), (), s32[]{:S(2)}) async-start(), calls=%async_computation.4 | async-start | bytes 10166272 | tf_op jit(solution)/shard_map/reduce_scatter | solution.py:812
  48.3 53.2 %copy-start.3 = (bf16[4,576,256]{2,1,0:T(8,128)(2,1)}, bf16[4,576,256]{2,1,0:T(8,128)(2,1)S(1)}, u32[]{:S(2)}) copy-start(bf16[4,576,256]{2,1,0:T(8,128)(2,1)S(1)} %pad_maximum_fusion.a_ref) | copy-start | bytes 3538948
  48.3 50.0 %collective-permute-start.3 = (bf16[4,576,256]{2,1,0:T(8,128)(2,1)S(1)}, bf16[4,576,256]{2,1,0:T(8,128)(2,1)}, u32[]{:S(2)}, u32[]{:S(2)}) collective-permute-start(bf16[4,576,256]{2,1,0:T(8,128)(2,1)S(1)} %pad_maximum_fusion.a_ref), channel_id=1, source_target_pairs={{0,4},{2,6},{4,0},{6,2},{8,12},{10,14},{12,8},{14,10},{16,20},{18,... | collective-permute-start | bytes 3538952 | tf_op jit(solution)/shard_map/ppermute | solution.py:803
  50.3 51.1 %collective-permute-start.4 = (bf16[4,576,256]{2,1,0:T(8,128)(2,1)S(1)}, bf16[4,576,256]{2,1,0:T(8,128)(2,1)}, u32[]{:S(2)}, u32[]{:S(2)}) collective-permute-start(bf16[4,576,256]{2,1,0:T(8,128)(2,1)S(1)} %pad_maximum_fusion.a_ref), channel_id=1, source_target_pairs={{0,2},{2,0},{4,6},{6,4},{8,10},{10,8},{12,14},{14,12},{16,18},{18,... | collective-permute-start | bytes 3538952 | tf_op jit(solution)/shard_map/ppermute | solution.py:798
  98.3 3.2 collective-permute-start.5
  101.5 1.1 copy-start.1
  248.9 4.9 %collective-permute-start.6 = (bf16[8,592,256]{2,1,0:T(8,128)(2,1)}, bf16[8,592,256]{2,1,0:T(8,128)(2,1)S(1)}, u32[]{:S(2)}, u32[]{:S(2)}) collective-permute-start(bf16[8,592,256]{2,1,0:T(8,128)(2,1)} %get-tuple-element.58), channel_id=1, source_target_pairs={{0,2},{2,0},{4,6},{6,4},{8,10},{10,8},{12,14},{14,12},{16,18},{18,... | collective-permute-start | bytes 7274504 | tf_op jit(solution)/shard_map/ppermute | solution.py:798
  253.8 3.5 copy-start.2
  257.3 29.1 %collective-permute-start.7 = (bf16[8,296,256]{2,1,0:T(8,128)(2,1)}, bf16[8,296,256]{2,1,0:T(8,128)(2,1)}, u32[]{:S(2)}, u32[]{:S(2)}) collective-permute-start(bf16[8,296,256]{2,1,0:T(8,128)(2,1)} %add_convert_fusion), channel_id=1, source_target_pairs={{0,1},{1,0},{2,3},{3,2},{4,5},{5,4},{6,7},{7,6},{8,9},{9,8},{10,11... | collective-permute-start | bytes 3637256 | tf_op jit(solution)/shard_map/ppermute | solution.py:816
  258.6 75.4 %all-to-all-start.1 = ((bf16[16,64,768]{2,1,0:T(8,128)(2,1)}), bf16[16,64,768]{2,1,0:T(8,128)(2,1)S(1)}, u32[]{:S(2)}, u32[]{:S(2)}) async-start(bf16[16,64,768]{2,1,0:T(8,128)(2,1)} %bitcast.60), calls=%async_computation.1 | async-start | bytes 3145728 | tf_op jit(solution)/shard_map/all_to_all | solution.py:946
  288.1 25.5 %collective-permute-start.8 = (bf16[4,296,256]{2,1,0:T(8,128)(2,1)S(1)}, bf16[4,296,256]{2,1,0:T(8,128)(2,1)S(1)}, u32[]{:S(2)}, u32[]{:S(2)}) collective-permute-start(bf16[4,296,256]{2,1,0:T(8,128)(2,1)S(1)} %add_convert_fusion.2), channel_id=1, source_target_pairs={{0,4},{2,6},{4,0},{6,2},{8,12},{10,14},{12,8},{14,10},{16,20},{18,... | collective-permute-start | bytes 1818632 | tf_op jit(solution)/shard_map/ppermute | solution.py:803
  315.4 15.7 %collective-permute-start.10 = (bf16[296,256]{1,0:T(8,128)(2,1)S(1)}, bf16[296,256]{1,0:T(8,128)(2,1)S(1)}, u32[]{:S(2)}, u32[]{:S(2)}) collective-permute-start(bf16[296,256]{1,0:T(8,128)(2,1)S(1)} %get-tuple-element.73), channel_id=1, source_target_pairs={{0,16},{2,18},{4,20},{6,22},{8,24},{10,26},{12,28},{14,30},{16,0},... | collective-permute-start | bytes 454664 | tf_op jit(solution)/shard_map/ppermute | solution.py:808
  316.4 14.7 %collective-permute-start.11 = (bf16[296,256]{1,0:T(8,128)(2,1)S(1)}, bf16[296,256]{1,0:T(8,128)(2,1)S(1)}, u32[]{:S(2)}, u32[]{:S(2)}) collective-permute-start(bf16[296,256]{1,0:T(8,128)(2,1)S(1)} %get-tuple-element.72), channel_id=1, source_target_pairs={{0,24},{2,26},{4,28},{6,30},{8,0},{10,2},{12,4},{14,6},{16,8},{18,... | collective-permute-start | bytes 454664 | tf_op jit(solution)/shard_map/ppermute | solution.py:808
  318.0 13.2 %collective-permute-start.9 = (bf16[296,256]{1,0:T(8,128)(2,1)S(1)}, bf16[296,256]{1,0:T(8,128)(2,1)S(1)}, u32[]{:S(2)}, u32[]{:S(2)}) collective-permute-start(bf16[296,256]{1,0:T(8,128)(2,1)S(1)} %get-tuple-element.71), channel_id=1, source_target_pairs={{0,8},{2,10},{4,12},{6,14},{8,16},{10,18},{12,20},{14,22},{16,24},... | collective-permute-start | bytes 454664 | tf_op jit(solution)/shard_map/ppermute | solution.py:808
  331.2 19.1 %copy-start.4 = (bf16[296,256]{1,0:T(8,128)(2,1)}, bf16[296,256]{1,0:T(8,128)(2,1)S(1)}, u32[]{:S(2)}) copy-start(bf16[296,256]{1,0:T(8,128)(2,1)S(1)} %fusion.2.mine_ref) | copy-start | bytes 454660
  331.3 21.6 %collective-permute-start.13 = (bf16[1168,256]{1,0:T(8,128)(2,1)}, bf16[1168,256]{1,0:T(8,128)(2,1)S(1)}, u32[]{:S(2)}, u32[]{:S(2)}) collective-permute-start(bf16[1168,256]{1,0:T(8,128)(2,1)} %reduce-scatter.2.cloned.1.call-done.mine_ref), channel_id=1, source_target_pairs={{0,1},{1,0},{2,3},{3,2},{4,5},{5,4},{6,7},{7,6},{8,9},{9,8},{10,11... | collective-permute-start | bytes 1794056 | tf_op jit(solution)/shard_map/ppermute | solution.py:854
  332.9 17.4 %collective-permute-start.12 = (bf16[296,256]{1,0:T(8,128)(2,1)S(1)}, bf16[296,256]{1,0:T(8,128)(2,1)S(1)}, u32[]{:S(2)}, u32[]{:S(2)}) collective-permute-start(bf16[296,256]{1,0:T(8,128)(2,1)S(1)} %fusion.2.mine_ref), channel_id=1, source_target_pairs={{0,1},{1,0},{2,3},{3,2},{4,5},{5,4},{6,7},{7,6},{8,9},{9,8},{10,11... | collective-permute-start | bytes 454664 | tf_op jit(solution)/shard_map/ppermute | solution.py:816
  334.0 1.2 copy-start
  350.3 0.7 copy-start.11
  352.9 0.8 copy-start.5
Sparse Core Ops, SparseCore 0:
  36.2 112.1 all-gather.1
  191.9 135.8 reduce-scatter.1

commit v6 on v5

--- a/solution.py
+++ b/solution.py
@@ -109,8 +109,8 @@
     return pl.BlockSpec(shape, lambda *_: zeros)
 
 
-def params():
-    return pltpu.CompilerParams(vmem_limit_bytes=60 << 20)
+def params(mib):
+    return pltpu.CompilerParams(vmem_limit_bytes=mib << 20)
 
 
 def cost(flops, moved, trans=0):
@@ -185,7 +185,7 @@
             pl.BlockSpec((span, width), lambda j: (0, jnp.minimum(j, 2))),
             pl.BlockSpec((4 * along, cols * rows, LANES), lambda j: (0, j, 0)),
         ),
-        compiler_params=params(),
+        compiler_params=params(24),
         cost_estimate=cost(6 * span * width * width, 14 << 20),
         name="make_qkv",
     )(me, tokens, gain, *pieces)
@@ -266,7 +266,7 @@
             pltpu.VMEM((2, HD + 16, span), bf16),
             pltpu.VMEM((pair, span), f32),
         ],
-        compiler_params=params(),
+        compiler_params=params(32),
         cost_estimate=cost(4 * span * span * width, 8 << 20, span * span * H),
         name="attend_forward",
     )(count, qkv, qkv, qkv)
@@ -302,7 +302,7 @@
             const_block((1, width)),
         ],
         out_specs=(const_block((span, width)), const_block((span, width))),
-        compiler_params=params(),
+        compiler_params=params(24),
         cost_estimate=cost(2 * span * width * width, 9 << 20),
         name="out_project",
     )(tokens, mixed, packed, gain)
@@ -334,7 +334,6 @@
     wu_ref,
     wd_ref,
     out_ref,
-    gh_ref,
     ghb_ref,
     pack_ref,
     gb_ref,
@@ -462,7 +461,6 @@
         weighted = grad * gain_ref[...]
         mean = jnp.mean(scaled * weighted, axis=-1, keepdims=True)
         g_h = gb_ref[...].astype(f32) + inv * (weighted - scaled * mean)
-        gh_ref[...] = g_h
         ghb_ref[...] = g_h.astype(bf16)
         for copy in copies(step - 1, 1 - slot) + copies(step, slot):
             copy.wait()
@@ -483,7 +481,6 @@
         grid=(blocks,),
         out_shape=(
             jax.ShapeDtypeStruct((span, width), bf16),
-            jax.ShapeDtypeStruct((span, width), f32),
             jax.ShapeDtypeStruct((span, width), bf16),
             jax.ShapeDtypeStruct((parts, moved + GAIN_ROWS, LANES), bf16),
         ),
@@ -497,7 +494,7 @@
             pl.BlockSpec((parts, rows, LANES), lambda j: (0, blocks + j, 0)),
             pl.BlockSpec((few, cols * down, LANES), lambda j: (j, 2 * blocks * rows // (cols * down), 0)),
         ],
-        out_specs=(full, full, full, pl.BlockSpec(memory_space=pl.ANY)),
+        out_specs=(full, full, pl.BlockSpec(memory_space=pl.ANY)),
         scratch_shapes=[
             pltpu.VMEM((span, width), bf16),
             pltpu.VMEM((span, width), f32),
@@ -511,7 +508,7 @@
             pltpu.VMEM((span, LANES), bf16),
             pltpu.SemaphoreType.DMA((4, 2)),
         ],
-        compiler_params=params(),
+        compiler_params=params(60),
         cost_estimate=cost(18 * span * width * ff, 36 << 20, span * ff),
         name="ffn_both",
     )(count, hidden, normed, d_rows, gain, packed, packed, packed)
@@ -529,7 +526,6 @@
     lse_ref,
     n1_ref,
     x_ref,
-    gh_ref,
     ghb_ref,
     gain_ref,
     wq_ref,
@@ -691,12 +687,12 @@
             copy.start()
         weighted = grad * gain_ref[...]
         mean = jnp.mean(scaled * weighted, axis=-1, keepdims=True)
-        gx_ref[...] = (gh_ref[...] + inv * (weighted - scaled * mean)).astype(bf16)
+        gx_ref[...] = (ghb_ref[...].astype(f32) + inv * (weighted - scaled * mean)).astype(bf16)
         for copy in copies(step) + last:
             copy.wait()
 
 
-def attend_back(count, place, qkv, mixed, lse, n1, tokens, g_h, g_hb, gain, packed, unit_max, rows):
+def attend_back(count, place, qkv, mixed, lse, n1, tokens, g_hb, gain, packed, unit_max, rows):
     span, width = tokens.shape
     parts = packed.shape[0]
     cols = width // LANES
@@ -724,7 +720,6 @@
             block(2 * cols),
             full,
             pl.BlockSpec((2, 8, span), lambda p: (p, 0, 0)),
-            full,
             full,
             full,
             full,
@@ -749,10 +744,10 @@
             pltpu.SemaphoreType.DMA((4, 2)),
             pltpu.SemaphoreType.DMA((2,)),
         ],
-        compiler_params=params(),
+        compiler_params=params(48),
         cost_estimate=cost(10 * span * span * width + 16 * span * width * width, 24 << 20, span * span * H),
         name="attend_back",
-    )(count, place, qkv, qkv, qkv, mixed, lse, n1, tokens, g_h, g_hb, gain, packed, packed, packed, packed)
+    )(count, place, qkv, qkv, qkv, mixed, lse, n1, tokens, g_hb, gain, packed, packed, packed, packed)
 
 
 def finish_kernel(layout, own, gain_cols, halves, me_ref, mine_ref, other_ref, *outs):
@@ -834,11 +829,12 @@
     pass_on = sum(p[along:].astype(f32) for p in parts).astype(bf16)
     crossed = to_side(pass_on)
     column = (sum(p[:along].astype(f32) for p in parts) + crossed.astype(f32)).astype(bf16)
+    column, later = lax.optimization_barrier((column, later))
     found = [along_z(column[k], k) for k in range(1, along)]
     total = column[0].astype(f32)
     for piece in found:
         total = total + piece.astype(f32)
-    total, later = lax.optimization_barrier((total.astype(bf16), later))
+    total = total.astype(bf16)
     if pair:
         return total, to_replica(total), later
     return *replica_rounds(total), later
@@ -866,22 +862,47 @@
         in_specs=[smem(), vmem(), vmem()],
         out_specs=(vmem(),) * (len(layout) + 1),
         scratch_shapes=[pltpu.VMEM((rows, LANES), f32)],
-        compiler_params=params(),
+        compiler_params=params(40),
         cost_estimate=cost(0, 4 << 20),
         name="finish",
     )(me, share, other)
     return outs[:-1] + (outs[-1][0],)
 
 
-def to_blocks(mat, parts):
-    rows = mat.shape[0] // parts
-    cols = mat.shape[1] // LANES
-    split = mat.reshape(parts, rows, cols, LANES).transpose(0, 2, 1, 3)
-    return split.reshape(parts, cols * rows, LANES)
+def pack_kernel(*refs):
+    out_ref, sems = refs[-2:]
+    begin = 0
+    copies = []
+    for mat_ref in refs[:-2]:
+        rows, cols = mat_ref.shape
+        for c in range(cols // LANES):
+            copies.append(
+                pltpu.make_async_copy(
+                    mat_ref.at[:, pl.ds(c * LANES, LANES)],
+                    out_ref.at[pl.ds(begin, rows), :],
+                    sems.at[len(copies)],
+                )
+            )
+            begin += rows
+    for copy in copies:
+        copy.start()
+    for copy in copies:
+        copy.wait()
 
 
 def pack_own(mats):
-    return jnp.concatenate([to_blocks(m, 1)[0] for m in mats], axis=0)
+    total = sum(m.shape[0] * m.shape[1] for m in mats) // LANES
+    blocks = sum(m.shape[1] for m in mats) // LANES
+    return pl.pallas_call(
+        pack_kernel,
+        out_shape=jax.ShapeDtypeStruct((total, LANES), bf16),
+        in_specs=[pl.BlockSpec(memory_space=pl.ANY)] * len(mats),
+        out_specs=vmem(),
+        scratch_shapes=[pltpu.SemaphoreType.DMA((blocks,))],
+        compiler_params=params(62),
+        cost_estimate=cost(0, 4 * total * LANES),
+        name="pack_own",
+    )(*mats)
 
 
 def gather_queue(packed):
@@ -932,7 +953,7 @@
     )
     mixed, lse = attend_forward(count, qkv, unit_max)
     hidden, n2 = out_project(tokens, mixed, attn_pack, gain_two, rows)
-    layer_out, g_h, g_hb, ffn_grads = ffn_both(
+    layer_out, g_hb, ffn_grads = ffn_both(
         count, hidden, n2, d_out[0, 0], gain_two, ffn_pack, unit_max, rows, down
     )
     own = width // shard_count
@@ -941,13 +962,21 @@
     ffn_share = scatter_queue(ffn_grads)
     place = relative_places(shard_count)
     g_x, keep, send = attend_back(
-        count, place, qkv, mixed, lse, n1, tokens, g_h, g_hb, gain_one, attn_pack, unit_max, rows
+        count, place, qkv, mixed, lse, n1, tokens, g_hb, gain_one, attn_pack, unit_max, rows
     )
     returned = lax.all_to_all(
         g_x.reshape(shard_count, unit_max, width), "shard", split_axis=0, concat_axis=0, tiled=True
     )
     grad_x = undeal_rows(seq_units, deal, returned, given)[None]
     attn_mine, attn_other, ffn_share = scatter_permute(keep, send, ffn_share)
+    out_wg, out_wu, out_wd, out_gain_two = finish(
+        *replica_rounds(ffn_share),
+        ((rows, wide), (rows, wide), (down, cols)),
+        own,
+        shard_count,
+        False,
+    )
+    attn_other, out_gain_two = lax.optimization_barrier((attn_other, out_gain_two))
     out_wq, out_wk, out_wv, out_wo, out_gain_one = finish(
         attn_mine,
         attn_other,
@@ -955,13 +984,6 @@
         own,
         shard_count,
         lax.axis_size("replica") == 2,
-    )
-    out_wg, out_wu, out_wd, out_gain_two = finish(
-        *replica_rounds(ffn_share),
-        ((rows, wide), (rows, wide), (down, cols)),
-        own,
-        shard_count,
-        False,
     )
     return (
         layer_out.reshape(1, 1, span, width),

time: 364 us -> 351 us (0.964)
  Pallas kernels: 150 us -> 141 us
  local copies, waits for them, and re-layouts: 10.1 us -> 6.24 us
    ppermute x2, waiting for transfers between devices: 35.1 us -> 23.7 us  [to_replica(): return lax.ppermute(value, 'replica', [(0, 1), (1, 0)])]
    reduce_scatter x1, waiting for transfers between devices: 0.02 us -> 8.65 us  [scatter_queue(): lax.psum_scatter(packed.reshape(-1, LANES), 'shard', scatter_dimension=0,...]
    all_gather x1, waiting for transfers between devices: 7.87 us -> 14.3 us  [gather_queue(): whole = lax.all_gather(packed, 'shard', axis=0, tiled=True)]
    pallas_call x1, Pallas kernels: 6.04 us -> 1.75 us  [out_project(): pl.pallas_call(out_kernel, grid=(1,), out_shape=(jax.ShapeDtypeStruct((sp...]
    reshape x6 -> x0, local copies, waits for them, and re-layouts: 3.83 us -> none  [to_blocks(): split = mat.reshape(parts, rows, cols, LANES).transpose(0, 2, 1, 3)]
    pallas_call x0 -> x2, Pallas kernels: none -> 3.81 us  [pack_own(): pl.pallas_call(pack_kernel, out_shape=jax.ShapeDtypeStruct((total, LANES)...]
  transfers between devices with their start and end apart: 18 -> 18, of which waited for: 10 -> 10; matrix products, arithmetic and copies ran while one was open for 4% -> 3% of each run, Pallas kernels for 29% -> 27%
where the time goes in v6:
time: 351 us; the launch traced here: 350 us
  waiting for transfers between devices  147 us (42%)
  Pallas kernels  141 us (40%)
  starting transfers between devices  30 us (9%)
  between operations  14.4 us (4%)
  other arithmetic  10.4 us (3%)
  local copies, waits for them, and re-layouts  6.24 us (2%)
    ppermute x2, waiting for transfers between devices, to_side(): return lax.ppermute(value, 'shard', [(i, i ^ 2) for i in range(count)])  73.2 us
    pallas_call x1, Pallas kernels, attend_back(): pl.pallas_call(functools.partial(attend_back_kernel, unit_max, 512), grid...  54.4 us
    pallas_call x1, Pallas kernels, ffn_both(): pl.pallas_call(functools.partial(ffn_kernel, unit_max), grid=(blocks,), o...  42.4 us
    ppermute x2, waiting for transfers between devices, to_replica(): return lax.ppermute(value, 'replica', [(0, 1), (1, 0)])  23.7 us
    ppermute x6, waiting for transfers between devices, along_z(): lax.ppermute(value, 'shard', [(i, (i + 4 * step) % count) for i in range(...  21.5 us
    pallas_call x1, Pallas kernels, attend_forward(): pl.pallas_call(functools.partial(attend_kernel, unit_max, 1024), grid=(pa...  20.1 us
    all_gather x1, waiting for transfers between devices, gather_queue(): whole = lax.all_gather(packed, 'shard', axis=0, tiled=True)  14.3 us
    all_to_all x1, starting transfers between devices, shards(): lax.all_to_all(outgoing, 'shard', split_axis=0, concat_axis=0, tiled=True)  10.1 us
  transfers between devices with their start and end apart: 18, of which 10 were waited for; matrix products, arithmetic and copies ran while one was open for 3% of the time, Pallas kernels for 27%

profile of v6, /device:TPU:0, one launch (start us, length us, event | category | flops | bytes accessed | tf_op | source)
XLA Modules:
  0.0 349.7 jit_solution(7073516182274706132)
XLA Ops:
  7.2 0.0 all-gather.2.cloned.1.call-start
  7.2 1.7 pack_own.3
  9.0 3.1 collective-permute-start
  12.1 2.6 collective-permute-start.1
  14.6 1.3 collective-permute-start.2
  16.0 4.1 %deal_rows.1 = bf16[16,64,768]{2,1,0:T(8,128)(2,1)} custom-call(s32[1,16]{1,0:T(1,128)} %units_ref.3, s32[1,16]{1,0:T(1,128)} %order_ref.3, bf16[512,768]{1,0:T(8,128)(2,1)} %bitcast.35), custom_call_target="tpu_custom_call" | custom-call | tf_op jit(solution)/shard_map/deal_rows/pallas_call | solution.py:85
  20.1 2.1 pack_own.2
  22.2 0.1 collective-permute-done
  22.3 11.8 %collective-permute-done.1 = bf16[576,256]{1,0:T(8,128)(2,1)S(1)} collective-permute-done((bf16[576,256]{1,0:T(8,128)(2,1)}, bf16[576,256]{1,0:T(8,128)(2,1)S(1)}, u32[]{:S(2)}, u32[]{:S(2)}) %collective-permute-start.1) | collective-permute-done | bytes 294944 | tf_op jit(solution)/shard_map/ppermute | solution.py:803
  34.1 0.0 collective-permute-done.2
  34.1 0.0 all-gather.2.cloned.1.call-update
  34.1 0.0 copy-start.11
  34.1 0.7 copy-done.13
  34.8 0.1 copy-done.14
  34.9 10.1 %all-to-all-start = ((bf16[16,64,768]{2,1,0:T(8,128)(2,1)}), bf16[16,64,768]{2,1,0:T(8,128)(2,1)S(1)}, u32[]{:S(2)}, u32[]{:S(2)}) async-start(bf16[16,64,768]{2,1,0:T(8,128)(2,1)} %deal_rows.1), calls=%async_computation | async-start | bytes 3145728 | tf_op jit(solution)/shard_map/all_to_all | solution.py:937
  45.0 0.0 copy-start.15
  45.0 0.0 copy-start.16
  45.0 0.0 copy-start.18
  45.1 0.0 copy-start.17
  45.1 0.0 reduce-scatter.2.cloned.1.call-start
  45.1 1.3 pad_maximum_fusion.a_ref
  46.4 2.0 collective-permute-start.3
  48.4 0.0 collective-permute-start.4
  48.4 47.9 %collective-permute-done.3.b_ref = bf16[4,576,256]{2,1,0:T(8,128)(2,1)} collective-permute-done((bf16[4,576,256]{2,1,0:T(8,128)(2,1)S(1)}, bf16[4,576,256]{2,1,0:T(8,128)(2,1)}, u32[]{:S(2)}, u32[]{:S(2)}) %collective-permute-start.3) | collective-permute-done | bytes 1179680 | tf_op jit(solution)/shard_map/ppermute | solution.py:798
  96.3 0.0 collective-permute-start.5
  96.4 0.0 copy-start.3
  96.4 0.6 fusion.5
  97.0 1.3 fusion.6
  98.3 0.0 collective-permute-done.4.fa_ref
  98.3 1.2 collective-permute-done.5.fb_ref
  99.5 7.7 %make_qkv.1 = (bf16[1024,768]{1,0:T(8,128)(2,1)S(1)}, bf16[1024,2304]{1,0:T(8,128)(2,1)S(1)}, bf16[16,576,256]{2,1,0:T(8,128)(2,1)S(1)}) custom-call(s32[1]{0:T(128)} %bitcast.5.me_ref, bf16[1024,768]{1,0:T(8,128)(2,1)S(1)} %bitcast.30, f32[1,768]{1,0:T(1,128)S(1)} %reshape.54.gain_ref, bf16[4,576,256]{2,1,0:T(8,128)(2,1)S(1)} %pad_maximum_fusion.a_ref, ...), custom_call_target="tpu_custom_call" | custom-call | flops 3623878656 | bytes 14680064 | tf_op jit(solution)/shard_map/make_qkv/pallas_call | solution.py:166
  107.3 20.1 %attend_forward.1 = (bf16[1024,768]{1,0:T(8,128)(2,1)S(1)}, f32[6,8,1024]{2,1,0:T(8,128)S(1)}) custom-call(s32[1]{0:T(128)} %bitcast.2.count_ref, bf16[1024,2304]{1,0:T(8,128)(2,1)S(1)} %get-tuple-element.46.q_ref.k_ref.v_ref, bf16[1024,2304]{1,0:T(8,128)(2,1)S(1)} %get-tuple-element.46.q_ref.k_ref.v_ref, ...), custom_call_target="tpu_custom_call" | custom-call | flops 3221225472 | bytes 8388608 | tf_op jit(solution)/shard_map/attend_forward/pallas_call | solution.py:255
  127.4 1.8 out_project.1
  129.2 1.7 copy-done.4
  130.9 1.2 copy-done.5
  132.1 14.3 %all-gather.2.cloned.1.call-done = bf16[18432,256]{1,0:T(8,128)(2,1)} async-done(((bf16[1152,256]{1,0:T(8,128)(2,1)}), bf16[18432,256]{1,0:T(8,128)(2,1)}) %all-gather.2.cloned.1.call-update) | async-done | bytes 9437200 | tf_op jit(solution)/shard_map/all_gather | solution.py:909
  146.4 42.4 %ffn_both.1 = (bf16[1024,768]{1,0:T(8,128)(2,1)}, bf16[1024,768]{1,0:T(8,128)(2,1)}, bf16[16,1168,256]{2,1,0:T(8,128)(2,1)}) custom-call(s32[1]{0:T(128)} %bitcast.2.count_ref, f32[1024,768]{1,0:T(8,128)} %copy-done.4, bf16[1024,768]{1,0:T(8,128)(2,1)} %copy-done.5, bf16[1024,768]{1,0:T(8,128)(2,1)} %bitcast.43, f32[1,768]{1,0:T(1,128)} %copy-done.3, ...), custom_call_target="tpu_custom_call" | custom-call | flops 28991029248 | bytes 37748736 | tf_op jit(solution)/shard_map/ffn_both/pallas_call | solution.py:479
  188.8 0.0 reduce-scatter.2.cloned.1.call-update
  188.9 1.3 copy-done.8
  190.2 54.4 %attend_back.1 = (bf16[1024,768]{1,0:T(8,128)(2,1)}, bf16[8,592,256]{2,1,0:T(8,128)(2,1)}, bf16[8,592,256]{2,1,0:T(8,128)(2,1)}) custom-call(s32[1]{0:T(128)} %bitcast.2.count_ref, s32[16]{0:T(128)S(1)} %fusion.11.place_ref, bf16[1024,2304]{1,0:T(8,128)(2,1)} %copy-done.6, bf16[1024,2304]{1,0:T(8,128)(2,1)} %copy-done.6, bf16[1024,2304]{1,0:T(8,128)(2,1)} %copy-done.6, ...), custom_call_target="tpu_custom_call" | custom-call | flops 17716740096 | bytes 25165824 | tf_op jit(solution)/shard_map/attend_back/pallas_call | solution.py:707
  244.6 0.3 collective-permute-start.6
  244.9 4.6 %collective-permute-done.6 = bf16[8,592,256]{2,1,0:T(8,128)(2,1)S(1)} collective-permute-done((bf16[8,592,256]{2,1,0:T(8,128)(2,1)}, bf16[8,592,256]{2,1,0:T(8,128)(2,1)S(1)}, u32[]{:S(2)}, u32[]{:S(2)}) %collective-permute-start.6) | collective-permute-done | bytes 2424864 | tf_op jit(solution)/shard_map/ppermute | solution.py:793
  249.5 3.5 %add_convert_fusion = bf16[8,296,256]{2,1,0:T(8,128)(2,1)} fusion(bf16[8,592,256]{2,1,0:T(8,128)(2,1)S(1)} %collective-permute-done.6, s32[]{:T(128)S(6)} %select_n.38, bf16[8,592,256]{2,1,0:T(8,128)(2,1)} %get-tuple-element.57), kind=kLoop, calls=%fused_computation | loop fusion | flops 2424832 | bytes 3637252 | tf_op jit(solution)/shard_map/convert_element_type | solution.py:826
  253.0 1.4 collective-permute-start.7
  254.4 4.0 %all-to-all-start.1 = ((bf16[16,64,768]{2,1,0:T(8,128)(2,1)}), bf16[16,64,768]{2,1,0:T(8,128)(2,1)S(1)}, u32[]{:S(2)}, u32[]{:S(2)}) async-start(bf16[16,64,768]{2,1,0:T(8,128)(2,1)} %bitcast.13), calls=%async_computation.1 | async-start | bytes 3145728 | tf_op jit(solution)/shard_map/all_to_all | solution.py:967
  258.4 23.7 %collective-permute-done.7 = bf16[8,296,256]{2,1,0:T(8,128)(2,1)} collective-permute-done((bf16[8,296,256]{2,1,0:T(8,128)(2,1)}, bf16[8,296,256]{2,1,0:T(8,128)(2,1)}, u32[]{:S(2)}, u32[]{:S(2)}) %collective-permute-start.7) | collective-permute-done | bytes 1212448 | tf_op jit(solution)/shard_map/ppermute | solution.py:811
  282.1 1.7 add_convert_fusion.2
  283.9 0.3 collective-permute-start.8
  284.2 25.2 %collective-permute-done.8 = bf16[4,296,256]{2,1,0:T(8,128)(2,1)S(1)} collective-permute-done((bf16[4,296,256]{2,1,0:T(8,128)(2,1)S(1)}, bf16[4,296,256]{2,1,0:T(8,128)(2,1)S(1)}, u32[]{:S(2)}, u32[]{:S(2)}) %collective-permute-start.8) | collective-permute-done | bytes 606240 | tf_op jit(solution)/shard_map/ppermute | solution.py:798
  309.4 1.8 add_convert_fusion.1
  311.2 8.6 %reduce-scatter.2.cloned.1.call-done.mine_ref = bf16[1168,256]{1,0:T(8,128)(2,1)} async-done(((bf16[18688,256]{1,0:T(8,128)(2,1)}), bf16[1168,256]{1,0:T(8,128)(2,1)}) %reduce-scatter.2.cloned.1.call-update) | async-done | bytes 598032 | tf_op jit(solution)/shard_map/reduce_scatter | solution.py:807
  319.9 0.9 collective-permute-start.13
  320.8 1.0 collective-permute-start.10
  321.8 1.9 collective-permute-start.11
  323.7 0.1 collective-permute-start.9
  323.8 9.6 %collective-permute-done.10 = bf16[296,256]{1,0:T(8,128)(2,1)S(1)} collective-permute-done((bf16[296,256]{1,0:T(8,128)(2,1)S(1)}, bf16[296,256]{1,0:T(8,128)(2,1)S(1)}, u32[]{:S(2)}, u32[]{:S(2)}) %collective-permute-start.10) | collective-permute-done | bytes 151584 | tf_op jit(solution)/shard_map/ppermute | solution.py:803
  333.4 0.1 fusion.2.mine_ref
  333.5 0.8 collective-permute-start.12
  334.3 0.1 pad_add_fusion.me_ref
  334.4 1.2 copy-done.9
  335.6 4.1 %undeal_rows.1 = bf16[512,768]{1,0:T(8,128)(2,1)} custom-call(s32[1,16]{1,0:T(1,128)} %units_ref.3, s32[1,16]{1,0:T(1,128)} %order_ref.3, bf16[16,64,768]{2,1,0:T(8,128)(2,1)} %copy-done.9), custom_call_target="tpu_custom_call" | custom-call | tf_op jit(solution)/shard_map/undeal_rows/pallas_call | solution.py:97
  339.7 0.0 collective-permute-done.13.other_ref
  339.7 1.7 finish.2
  341.5 1.4 finish.3
  (35 shorter events, 0.1 us)
Async XLA Ops:
  7.2 139.2 %all-gather.2.cloned.1.call-start = ((), (), s32[]{:S(2)}) async-start(), calls=%async_computation.3 | async-start | bytes 10027008 | tf_op jit(solution)/shard_map/all_gather | solution.py:909
  9.0 13.3 %collective-permute-start = (bf16[576,256]{1,0:T(8,128)(2,1)}, bf16[576,256]{1,0:T(8,128)(2,1)S(1)}, u32[]{:S(2)}, u32[]{:S(2)}) collective-permute-start(bf16[576,256]{1,0:T(8,128)(2,1)} %pack_own.3), channel_id=1, source_target_pairs={{0,8},{2,10},{4,12},{6,14},{8,16},{10,18},{12,20},{14,22},{16,24},... | collective-permute-start | bytes 884744 | tf_op jit(solution)/shard_map/ppermute | solution.py:803
  12.1 22.0 %collective-permute-start.1 = (bf16[576,256]{1,0:T(8,128)(2,1)}, bf16[576,256]{1,0:T(8,128)(2,1)S(1)}, u32[]{:S(2)}, u32[]{:S(2)}) collective-permute-start(bf16[576,256]{1,0:T(8,128)(2,1)} %pack_own.3), channel_id=1, source_target_pairs={{0,16},{2,18},{4,20},{6,22},{8,24},{10,26},{12,28},{14,30},{16,0},... | collective-permute-start | bytes 884744 | tf_op jit(solution)/shard_map/ppermute | solution.py:803
  14.6 19.4 %collective-permute-start.2 = (bf16[576,256]{1,0:T(8,128)(2,1)}, bf16[576,256]{1,0:T(8,128)(2,1)S(1)}, u32[]{:S(2)}, u32[]{:S(2)}) collective-permute-start(bf16[576,256]{1,0:T(8,128)(2,1)} %pack_own.3), channel_id=1, source_target_pairs={{0,24},{2,26},{4,28},{6,30},{8,0},{10,2},{12,4},{14,6},{16,8},{18,... | collective-permute-start | bytes 884744 | tf_op jit(solution)/shard_map/ppermute | solution.py:803
  22.3 11.8 %copy-start.12 = (bf16[576,256]{1,0:T(8,128)(2,1)}, bf16[576,256]{1,0:T(8,128)(2,1)S(1)}, u32[]{:S(2)}) copy-start(bf16[576,256]{1,0:T(8,128)(2,1)S(1)} %collective-permute-done) | copy-start | bytes 884740
  34.1 0.7 copy-start.13
  34.1 0.8 copy-start.14
  34.1 11.0 %copy-start.11 = (bf16[576,256]{1,0:T(8,128)(2,1)S(1)}, bf16[576,256]{1,0:T(8,128)(2,1)}, u32[]{:S(2)}) copy-start(bf16[576,256]{1,0:T(8,128)(2,1)} %pack_own.3) | copy-start | bytes 884740
  34.9 64.6 %all-to-all-start = ((bf16[16,64,768]{2,1,0:T(8,128)(2,1)}), bf16[16,64,768]{2,1,0:T(8,128)(2,1)S(1)}, u32[]{:S(2)}, u32[]{:S(2)}) async-start(bf16[16,64,768]{2,1,0:T(8,128)(2,1)} %deal_rows.1), calls=%async_computation | async-start | bytes 3145728 | tf_op jit(solution)/shard_map/all_to_all | solution.py:937
  45.0 51.3 %copy-start.15 = (f32[768]{0:T(1024)S(1)}, f32[768]{0:T(1024)}, u32[]{:S(2)}) copy-start(f32[768]{0:T(1024)} %param.16) | copy-start | bytes 9220
  45.0 51.3 %copy-start.16 = (f32[768]{0:T(1024)S(1)}, f32[768]{0:T(1024)}, u32[]{:S(2)}) copy-start(f32[768]{0:T(1024)} %param.21) | copy-start | bytes 9220
  45.0 51.3 %copy-start.18 = (s32[1,16]{1,0:T(1,128)S(1)}, s32[1,16]{1,0:T(1,128)}, u32[]{:S(2)}) copy-start(s32[1,16]{1,0:T(1,128)} %order_ref.3) | copy-start | bytes 196
  45.1 52.0 %copy-start.17 = (s32[1,16]{1,0:T(1,128)S(1)}, s32[1,16]{1,0:T(1,128)}, u32[]{:S(2)}) copy-start(s32[1,16]{1,0:T(1,128)} %units_ref.3) | copy-start | bytes 196
  45.1 274.8 %reduce-scatter.2.cloned.1.call-start = ((), (), s32[]{:S(2)}) async-start(), calls=%async_computation.4 | async-start | bytes 10166272 | tf_op jit(solution)/shard_map/reduce_scatter | solution.py:807
  46.4 49.9 %collective-permute-start.3 = (bf16[4,576,256]{2,1,0:T(8,128)(2,1)S(1)}, bf16[4,576,256]{2,1,0:T(8,128)(2,1)}, u32[]{:S(2)}, u32[]{:S(2)}) collective-permute-start(bf16[4,576,256]{2,1,0:T(8,128)(2,1)S(1)} %pad_maximum_fusion.a_ref), channel_id=1, source_target_pairs={{0,4},{2,6},{4,0},{6,2},{8,12},{10,14},{12,8},{14,10},{16,20},{18,... | collective-permute-start | bytes 3538952 | tf_op jit(solution)/shard_map/ppermute | solution.py:798
  48.4 49.9 %collective-permute-start.4 = (bf16[4,576,256]{2,1,0:T(8,128)(2,1)S(1)}, bf16[4,576,256]{2,1,0:T(8,128)(2,1)}, u32[]{:S(2)}, u32[]{:S(2)}) collective-permute-start(bf16[4,576,256]{2,1,0:T(8,128)(2,1)S(1)} %pad_maximum_fusion.a_ref), channel_id=1, source_target_pairs={{0,2},{2,0},{4,6},{6,4},{8,10},{10,8},{12,14},{14,12},{16,18},{18,... | collective-permute-start | bytes 3538952 | tf_op jit(solution)/shard_map/ppermute | solution.py:793
  96.3 3.2 collective-permute-start.5
  96.4 31.0 %copy-start.3 = (f32[1,768]{1,0:T(1,128)}, f32[1,768]{1,0:T(1,128)S(1)}, u32[]{:S(2)}) copy-start(f32[1,768]{1,0:T(1,128)S(1)} %reshape.55.gain_ref) | copy-start | bytes 9220
  99.5 27.9 %copy-start = (bf16[16,64,768]{2,1,0:T(8,128)(2,1)}, bf16[16,64,768]{2,1,0:T(8,128)(2,1)S(1)}, u32[]{:S(2)}) copy-start(bf16[16,64,768]{2,1,0:T(8,128)(2,1)S(1)} %all-to-all-done) | copy-start | bytes 4718596
  107.2 20.1 %copy-start.6 = (bf16[1024,2304]{1,0:T(8,128)(2,1)}, bf16[1024,2304]{1,0:T(8,128)(2,1)S(1)}, u32[]{:S(2)}) copy-start(bf16[1024,2304]{1,0:T(8,128)(2,1)S(1)} %get-tuple-element.46.q_ref.k_ref.v_ref) | copy-start | bytes 14155780
  107.3 20.1 %copy-start.7 = (bf16[1024,768]{1,0:T(8,128)(2,1)}, bf16[1024,768]{1,0:T(8,128)(2,1)S(1)}, u32[]{:S(2)}) copy-start(bf16[1024,768]{1,0:T(8,128)(2,1)S(1)} %get-tuple-element.54.n1_ref) | copy-start | bytes 4718596
  107.3 20.2 %copy-start.1 = (bf16[16,576,256]{2,1,0:T(8,128)(2,1)}, bf16[16,576,256]{2,1,0:T(8,128)(2,1)S(1)}, u32[]{:S(2)}) copy-start(bf16[16,576,256]{2,1,0:T(8,128)(2,1)S(1)} %get-tuple-element.48.w_ref.wq_ref.wk_ref.wv_ref.wo_ref) | copy-start | bytes 14155780
  129.2 1.7 copy-start.4
  130.9 1.2 copy-start.5
  188.8 1.4 copy-start.8
  244.6 4.9 %collective-permute-start.6 = (bf16[8,592,256]{2,1,0:T(8,128)(2,1)}, bf16[8,592,256]{2,1,0:T(8,128)(2,1)S(1)}, u32[]{:S(2)}, u32[]{:S(2)}) collective-permute-start(bf16[8,592,256]{2,1,0:T(8,128)(2,1)} %get-tuple-element.58), channel_id=1, source_target_pairs={{0,2},{2,0},{4,6},{6,4},{8,10},{10,8},{12,14},{14,12},{16,18},{18,... | collective-permute-start | bytes 7274504 | tf_op jit(solution)/shard_map/ppermute | solution.py:793
  249.5 3.5 %copy-start.10 = (bf16[8,592,256]{2,1,0:T(8,128)(2,1)}, bf16[8,592,256]{2,1,0:T(8,128)(2,1)S(1)}, u32[]{:S(2)}) copy-start(bf16[8,592,256]{2,1,0:T(8,128)(2,1)S(1)} %collective-permute-done.6) | copy-start | bytes 7274500
  253.0 29.1 %collective-permute-start.7 = (bf16[8,296,256]{2,1,0:T(8,128)(2,1)}, bf16[8,296,256]{2,1,0:T(8,128)(2,1)}, u32[]{:S(2)}, u32[]{:S(2)}) collective-permute-start(bf16[8,296,256]{2,1,0:T(8,128)(2,1)} %add_convert_fusion), channel_id=1, source_target_pairs={{0,1},{1,0},{2,3},{3,2},{4,5},{5,4},{6,7},{7,6},{8,9},{9,8},{10,11... | collective-permute-start | bytes 3637256 | tf_op jit(solution)/shard_map/ppermute | solution.py:811
  254.4 80.0 %all-to-all-start.1 = ((bf16[16,64,768]{2,1,0:T(8,128)(2,1)}), bf16[16,64,768]{2,1,0:T(8,128)(2,1)S(1)}, u32[]{:S(2)}, u32[]{:S(2)}) async-start(bf16[16,64,768]{2,1,0:T(8,128)(2,1)} %bitcast.13), calls=%async_computation.1 | async-start | bytes 3145728 | tf_op jit(solution)/shard_map/all_to_all | solution.py:967
  283.9 25.6 %collective-permute-start.8 = (bf16[4,296,256]{2,1,0:T(8,128)(2,1)S(1)}, bf16[4,296,256]{2,1,0:T(8,128)(2,1)S(1)}, u32[]{:S(2)}, u32[]{:S(2)}) collective-permute-start(bf16[4,296,256]{2,1,0:T(8,128)(2,1)S(1)} %add_convert_fusion.2), channel_id=1, source_target_pairs={{0,4},{2,6},{4,0},{6,2},{8,12},{10,14},{12,8},{14,10},{16,20},{18,... | collective-permute-start | bytes 1818632 | tf_op jit(solution)/shard_map/ppermute | solution.py:798
  319.9 19.9 %collective-permute-start.13 = (bf16[1168,256]{1,0:T(8,128)(2,1)}, bf16[1168,256]{1,0:T(8,128)(2,1)S(1)}, u32[]{:S(2)}, u32[]{:S(2)}) collective-permute-start(bf16[1168,256]{1,0:T(8,128)(2,1)} %reduce-scatter.2.cloned.1.call-done.mine_ref), channel_id=1, source_target_pairs={{0,1},{1,0},{2,3},{3,2},{4,5},{5,4},{6,7},{7,6},{8,9},{9,8},{10,11... | collective-permute-start | bytes 1794056 | tf_op jit(solution)/shard_map/ppermute | solution.py:850
  320.8 12.6 %collective-permute-start.10 = (bf16[296,256]{1,0:T(8,128)(2,1)S(1)}, bf16[296,256]{1,0:T(8,128)(2,1)S(1)}, u32[]{:S(2)}, u32[]{:S(2)}) collective-permute-start(bf16[296,256]{1,0:T(8,128)(2,1)S(1)} %get-tuple-element.75), channel_id=1, source_target_pairs={{0,16},{2,18},{4,20},{6,22},{8,24},{10,26},{12,28},{14,30},{16,0},... | collective-permute-start | bytes 454664 | tf_op jit(solution)/shard_map/ppermute | solution.py:803
  321.8 11.6 %collective-permute-start.11 = (bf16[296,256]{1,0:T(8,128)(2,1)S(1)}, bf16[296,256]{1,0:T(8,128)(2,1)S(1)}, u32[]{:S(2)}, u32[]{:S(2)}) collective-permute-start(bf16[296,256]{1,0:T(8,128)(2,1)S(1)} %get-tuple-element.74), channel_id=1, source_target_pairs={{0,24},{2,26},{4,28},{6,30},{8,0},{10,2},{12,4},{14,6},{16,8},{18,... | collective-permute-start | bytes 454664 | tf_op jit(solution)/shard_map/ppermute | solution.py:803
  323.7 9.7 %collective-permute-start.9 = (bf16[296,256]{1,0:T(8,128)(2,1)S(1)}, bf16[296,256]{1,0:T(8,128)(2,1)S(1)}, u32[]{:S(2)}, u32[]{:S(2)}) collective-permute-start(bf16[296,256]{1,0:T(8,128)(2,1)S(1)} %get-tuple-element.73), channel_id=1, source_target_pairs={{0,8},{2,10},{4,12},{6,14},{8,16},{10,18},{12,20},{14,22},{16,24},... | collective-permute-start | bytes 454664 | tf_op jit(solution)/shard_map/ppermute | solution.py:803
  333.5 6.3 %copy-start.2 = (bf16[1168,256]{1,0:T(8,128)(2,1)S(1)}, bf16[1168,256]{1,0:T(8,128)(2,1)}, u32[]{:S(2)}) copy-start(bf16[1168,256]{1,0:T(8,128)(2,1)} %reduce-scatter.2.cloned.1.call-done.mine_ref) | copy-start | bytes 1794052
  333.5 8.0 %collective-permute-start.12 = (bf16[296,256]{1,0:T(8,128)(2,1)S(1)}, bf16[296,256]{1,0:T(8,128)(2,1)S(1)}, u32[]{:S(2)}, u32[]{:S(2)}) collective-permute-start(bf16[296,256]{1,0:T(8,128)(2,1)S(1)} %fusion.2.mine_ref), channel_id=1, source_target_pairs={{0,1},{1,0},{2,3},{3,2},{4,5},{5,4},{6,7},{7,6},{8,9},{9,8},{10,11... | collective-permute-start | bytes 454664 | tf_op jit(solution)/shard_map/ppermute | solution.py:811
  334.4 1.2 copy-start.9
Sparse Core Ops, SparseCore 0:
  34.2 112.1 all-gather.1
  188.9 130.8 reduce-scatter.1
